TPU v7x, 32 devices: a whole 2x2x4 slice. The times are simulated.
32 devices in a mesh: dp: 16 (over z, y, x), tensor: 2 (over core).
Axes of the slice: x: 2, y: 2, z: 4, core: 2. Of those that a mesh axis runs over, the one named last changes fastest.
Arguments:
- block_input: bfloat16 [8192, 1536], P(('dp', 'tensor')), may hold values from -6 to 6
- teacher: bfloat16 [8192, 1536], P(('dp', 'tensor')), may hold values from -6 to 6
- lengths: int32 [16], replicated, may hold values from 256 to 512, as said below
- routes: int32 [8192, 6], P('dp'), may hold values from 0 to 15, all different within a row; in each aligned block of 256 rows (0 to 255, 256 to 511, ...) at most 128 rows name the same one
- gain_attn: float32 [1536], replicated, may hold values from 0.5 to 1.5
- w_query: bfloat16 [1536, 1536], P('dp', 'tensor'), may hold values from -0.15625 to 0.15625
- key_value_weight: bfloat16 [2, 1536, 512], P(None, 'dp', 'tensor'), may hold values from -0.15625 to 0.15625
- w_out: bfloat16 [1536, 1536], P('dp', 'tensor'), may hold values from -1.75 to 1.75
- gain_moe: float32 [1536], replicated, may hold values from 0.5 to 1.5
- w_router: bfloat16 [1536, 16], P('dp'), may hold values from -0.078125 to 0.078125
- w_shared_in: bfloat16 [2, 1536, 1024], P(None, 'dp', 'tensor'), may hold values from -0.15625 to 0.15625
- w_shared_out: bfloat16 [1536, 1024], P('dp', 'tensor'), may hold values from -0.25 to 0.25
- w_expert_in: bfloat16 [16, 2, 1536, 512], P('dp', None, None, 'tensor'), may hold values from -0.15625 to 0.15625
- w_expert_out: bfloat16 [16, 1536, 512], P('dp', None, 'tensor'), may hold values from -0.5 to 0.5
Outputs:
- block_output: bfloat16 [8192, 1536], P(('dp', 'tensor'))
- loss: float32 [], replicated
- input_grad: float32 [8192, 1536], P(('dp', 'tensor'))
- grad_gain_attn: float32 [1536], replicated
- grad_w_query: float32 [1536, 1536], P('dp', 'tensor')
- grad_w_kv: float32 [2, 1536, 512], P(None, 'dp', 'tensor')
- grad_w_out: float32 [1536, 1536], P('dp', 'tensor')
- grad_gain_moe: float32 [1536], replicated
- grad_w_router: float32 [1536, 16], P('dp')
- grad_w_shared_in: float32 [2, 1536, 1024], P(None, 'dp', 'tensor')
- grad_w_shared_out: float32 [1536, 1024], P('dp', 'tensor')
- grad_w_expert_in: float32 [16, 2, 1536, 512], P('dp', None, None, 'tensor')
- grad_w_expert_out: float32 [16, 1536, 512], P('dp', None, 'tensor')
Inputs may be any that keep to these rules, and one draw needn't show every extreme that they name: `lengths`: each sequence has at least half of its 512 slots valid; the longest has exactly 512. `routes`: the 6 experts of a row differ. Within each aligned block of 256 rows (one slice of a sequence) no expert is named by more than 128 rows, and some block has an expert named by exactly 128 rows.
All inputs are finite; a program needn't handle non-finite values.
Results may differ from a plain program's by a relative error of at most 0.018.
Values may be sent and summed in bfloat16 or wider, within the bound.
No kernel may reach another device: no remote copies, remote signals or barrier semaphores. Data moves between devices by JAX's collectives and lax.ppermute only.
A program may use at most 192 MiB of HBM per device.

v0:
```python
import jax
import jax.numpy as jnp
from jax import lax
from jax.sharding import PartitionSpec as P

MODEL_WIDTH = 1536
HEAD_SIZE = 128
TOPK = 6


norm_eps = 1e-05
block_limit = 512
masked_score = -1e30


def product(left_side, right_side):
    return jnp.dot(left_side, right_side, preferred_element_type=jnp.float32)


def product_transposed(left_side, right_side):
    return lax.dot_general(
        left_side, right_side, (((1,), (1,)), ((), ())), preferred_element_type=jnp.float32
    )


def product_left(left_side, right_side):
    return lax.dot_general(
        left_side, right_side, (((0,), (0,)), ((), ())), preferred_element_type=jnp.float32
    )


def normalize_rows(values, gain):
    row_scale = lax.rsqrt(jnp.mean(values * values, axis=-1, keepdims=True) + norm_eps)
    return ((values * row_scale * gain).astype(jnp.bfloat16), row_scale)


def normalize_back(values, row_scale, gain, grad_normed):
    scaled = grad_normed * gain
    inner_mean = jnp.mean(scaled * values, axis=-1, keepdims=True)
    grad_values = row_scale * (scaled - values * row_scale * row_scale * inner_mean)
    grad_gain = jnp.sum(grad_normed * values * row_scale, axis=0)
    return (grad_values, grad_gain)


def swish_back(pre_gate, pre_up, grad_act, stack_axis):
    logistic = jax.nn.sigmoid(pre_gate)
    grad_gate = grad_act * pre_up * logistic * (1.0 + pre_gate * (1.0 - logistic))
    grad_up = grad_act * pre_gate * logistic
    return jnp.stack([grad_gate, grad_up], axis=stack_axis).astype(jnp.bfloat16)


def gather_tokens(values):
    return lax.all_gather(values, "tensor", axis=0, tiled=True)


def scatter_tokens(values):
    return lax.psum_scatter(
        values.astype(jnp.bfloat16), "tensor", scatter_dimension=0, tiled=True
    ).astype(jnp.float32)


def to_owner(rows_out):
    return lax.all_to_all(rows_out, "dp", split_axis=0, concat_axis=0, tiled=True)


def from_owner(rows_back):
    return lax.all_to_all(
        rows_back.astype(jnp.bfloat16), "dp", split_axis=0, concat_axis=0, tiled=True
    ).astype(rows_back.dtype)


def owner_layout(arrived, dp_count, local_experts):
    capacity, feature_dim = (arrived.shape[1], arrived.shape[2])
    shaped = arrived.reshape(dp_count, local_experts, capacity, feature_dim)
    return shaped.transpose(1, 0, 2, 3).reshape(local_experts, dp_count * capacity, feature_dim)


def source_layout(produced, dp_count):
    local_experts, rows_all, feature_dim = produced.shape
    capacity = rows_all // dp_count
    shaped = produced.reshape(local_experts, dp_count, capacity, feature_dim)
    return shaped.transpose(1, 0, 2, 3).reshape(dp_count * local_experts, capacity, feature_dim)


def slot_table(route_rows, experts, capacity):
    slices = route_rows.shape[0]
    flat_routes = route_rows.reshape(slices, -1)
    one_hot = (
        flat_routes[:, :, None] == jnp.arange(experts, dtype=jnp.int32)[None, None, :]
    ).astype(jnp.int32)
    within = jnp.sum(jnp.cumsum(one_hot, axis=1) * one_hot, axis=-1) - 1
    slice_ids = jnp.arange(slices, dtype=jnp.int32)[:, None]
    return (flat_routes * (slices * capacity) + slice_ids * capacity + within).reshape(-1)


def slot_owner(slot_rows, buffer_size, token_count, gate_weights):
    token_ids = jnp.repeat(jnp.arange(token_count, dtype=jnp.int32), TOPK)
    slot_token = jnp.zeros((buffer_size,), jnp.int32).at[slot_rows].set(token_ids)
    filled = jnp.zeros((buffer_size,), jnp.bfloat16).at[slot_rows].set(1.0)
    slot_gate = jnp.zeros((buffer_size,), jnp.float32).at[slot_rows].set(gate_weights.reshape(-1))
    return (slot_token, filled, slot_gate)


def expert_forward(inputs, weight_in, weight_out):
    pre_acts = jnp.einsum("erd,ecdf->ecrf", inputs, weight_in, preferred_element_type=jnp.float32)
    activated = (jax.nn.silu(pre_acts[:, 0]) * pre_acts[:, 1]).astype(jnp.bfloat16)
    outputs = jnp.einsum("erf,edf->erd", activated, weight_out, preferred_element_type=jnp.float32)
    return (pre_acts, activated, outputs)


def expert_backward(inputs, weight_in, weight_out, grad_slot):
    pre_acts, activated, outputs = expert_forward(inputs, weight_in, weight_out)
    grad_act = jnp.einsum("erd,edf->erf", grad_slot, weight_out, preferred_element_type=jnp.float32)
    grad_wout = jnp.einsum("erd,erf->edf", grad_slot, activated, preferred_element_type=jnp.float32)
    grad_pre = swish_back(pre_acts[:, 0], pre_acts[:, 1], grad_act, 1)
    grad_win = jnp.einsum("erd,ecrf->ecdf", inputs, grad_pre, preferred_element_type=jnp.float32)
    grad_inputs = jnp.einsum(
        "ecrf,ecdf->erd", grad_pre, weight_in, preferred_element_type=jnp.float32
    )
    return (grad_inputs, grad_win, grad_wout, outputs)


def score_block(query_block, key_row_table, first_row, length):
    scores = jnp.einsum(
        "qvgd,kvd->vgqk", query_block, key_row_table, preferred_element_type=jnp.float32
    ) * HEAD_SIZE ** (-0.5)
    row_pos = first_row + jnp.arange(query_block.shape[0])
    col_pos = jnp.arange(key_row_table.shape[0])
    allowed = (col_pos[None, :] <= row_pos[:, None]) & (col_pos[None, :] < length)
    return jnp.where(allowed, scores, masked_score)


def on_device(
    block_input,
    teacher,
    lengths,
    routes,
    gain_attn,
    w_query,
    key_value_weight,
    w_out,
    gain_moe,
    w_router,
    w_shared_in,
    w_shared_out,
    w_expert_in,
    w_expert_out,
):
    own_rows = block_input.shape[0]
    slices = lax.axis_size("tensor")
    dp_count = lax.axis_size("dp")
    tp_index = lax.axis_index("tensor")
    sequence_length = own_rows * slices
    local_experts = w_expert_in.shape[0]
    experts = local_experts * dp_count
    capacity = max(2, own_rows * TOPK * 4 // (3 * experts))
    length = lengths[lax.axis_index("dp")]
    own_valid = (tp_index * own_rows + jnp.arange(own_rows) < length).astype(jnp.float32)[:, None]
    query_full, kv_full, out_full, router_full, shared_in_full, shared_out_full = (
        lax.all_gather(w_query, "dp", axis=0, tiled=True),
        lax.all_gather(key_value_weight, "dp", axis=1, tiled=True),
        lax.all_gather(w_out, "dp", axis=0, tiled=True),
        lax.all_gather(w_router, "dp", axis=0, tiled=True),
        lax.all_gather(w_shared_in, "dp", axis=1, tiled=True),
        lax.all_gather(w_shared_out, "dp", axis=0, tiled=True),
    )
    residual = block_input.astype(jnp.float32)
    normed_own, scale_attn = normalize_rows(residual, gain_attn)
    normed_all = gather_tokens(normed_own)
    head_count = query_full.shape[1] // HEAD_SIZE
    kv_count = kv_full.shape[2] // HEAD_SIZE
    head_group = head_count // kv_count
    queries = (
        product(normed_all, query_full)
        .astype(jnp.bfloat16)
        .reshape(sequence_length, kv_count, head_group, HEAD_SIZE)
    )
    key_vals = jnp.einsum(
        "td,cdf->ctf", normed_all, kv_full, preferred_element_type=jnp.float32
    ).astype(jnp.bfloat16)
    key_row_table = key_vals[0].reshape(sequence_length, kv_count, HEAD_SIZE)
    value_row_table = key_vals[1].reshape(sequence_length, kv_count, HEAD_SIZE)
    block = min(block_limit, sequence_length)

    def attend_block(block_index):
        first_row = block_index * block
        query_block = lax.dynamic_slice_in_dim(queries, first_row, block, 0)
        scores = score_block(query_block, key_row_table, first_row, length)
        row_max = jnp.max(scores, axis=-1, keepdims=True)
        exponent_terms = jnp.exp(scores - row_max)
        row_sum = jnp.sum(exponent_terms, axis=-1, keepdims=True)
        attn_probs = (exponent_terms / row_sum).astype(jnp.bfloat16)
        mixed_block = jnp.einsum(
            "vgqk,kvd->qvgd", attn_probs, value_row_table, preferred_element_type=jnp.float32
        ).astype(jnp.bfloat16)
        return (mixed_block, row_max + jnp.log(row_sum))

    mixed_blocks, log_totals = lax.map(attend_block, jnp.arange(sequence_length // block))
    mixed_heads = mixed_blocks.reshape(sequence_length, head_count * HEAD_SIZE)
    attn_own = scatter_tokens(product_transposed(mixed_heads, out_full))
    hidden = residual + attn_own
    moe_own, scale_moe = normalize_rows(hidden, gain_moe)
    moe_all = gather_tokens(moe_own)
    logits = product(moe_all, router_full)
    route_hot = (routes[:, :, None] == jnp.arange(experts, dtype=jnp.int32)[None, None, :]).astype(
        jnp.float32
    )
    chosen = jnp.sum(route_hot * logits[:, None, :], axis=-1)
    gate_weights = jax.nn.softmax(chosen, axis=-1)
    shared_pre = jnp.einsum(
        "td,cdf->ctf", moe_all, shared_in_full, preferred_element_type=jnp.float32
    )
    shared_act = (jax.nn.silu(shared_pre[0]) * shared_pre[1]).astype(jnp.bfloat16)
    shared_part = product_transposed(shared_act, shared_out_full)
    expert_in_whole, expert_out_whole = (
        lax.all_gather(w_expert_in, "tensor", axis=3, tiled=True),
        lax.all_gather(w_expert_out, "tensor", axis=2, tiled=True),
    )
    own_routes = lax.dynamic_slice_in_dim(routes, tp_index * own_rows, own_rows, 0)
    own_gates = lax.dynamic_slice_in_dim(gate_weights, tp_index * own_rows, own_rows, 0)
    slot_rows = slot_table(own_routes.reshape(1, own_rows, TOPK), experts, capacity)
    slot_token, filled, slot_gate = slot_owner(slot_rows, experts * capacity, own_rows, own_gates)
    inputs = (moe_own[slot_token] * filled[:, None]).reshape(experts, capacity, MODEL_WIDTH)
    work_rows = owner_layout(to_owner(inputs), dp_count, local_experts)
    produced = expert_forward(work_rows, expert_in_whole, expert_out_whole)[2]
    returned = from_owner(source_layout(produced, dp_count)).reshape(-1, MODEL_WIDTH)
    routed_own = (
        jnp.zeros((own_rows, MODEL_WIDTH), jnp.float32)
        .at[slot_token]
        .add(returned * slot_gate[:, None])
    )
    moe_own_out = scatter_tokens(shared_part) + routed_own
    out_rows = (hidden + moe_own_out) * own_valid
    residual_error = (out_rows - teacher.astype(jnp.float32)) * own_valid
    loss_part = 0.5 * jnp.sum(residual_error * residual_error)
    grad_out_low = residual_error.astype(jnp.bfloat16)
    grad_all = gather_tokens(grad_out_low)
    grad_shared_act = product(grad_all, shared_out_full)
    grad_shared_out = product_left(grad_all, shared_act)
    grad_shared_pre = swish_back(shared_pre[0], shared_pre[1], grad_shared_act, 0)
    grad_shared_in = jnp.einsum(
        "td,ctf->cdf", moe_all, grad_shared_pre, preferred_element_type=jnp.float32
    )
    grad_normed_part = jnp.einsum(
        "ctf,cdf->td", grad_shared_pre, shared_in_full, preferred_element_type=jnp.float32
    )
    grad_rows = grad_out_low[slot_token].astype(jnp.float32)
    grad_slot = (
        (grad_rows * slot_gate[:, None])
        .astype(jnp.bfloat16)
        .reshape(experts, capacity, MODEL_WIDTH)
    )
    slot_grad_gate = jnp.sum(grad_rows * returned, axis=-1)
    grad_work = owner_layout(to_owner(grad_slot), dp_count, local_experts)
    grad_inputs, grad_win, grad_wout, _ = expert_backward(
        work_rows, expert_in_whole, expert_out_whole, grad_work
    )
    grad_back = from_owner(source_layout(grad_inputs, dp_count)).reshape(-1, MODEL_WIDTH)
    expert_extra = jnp.zeros((own_rows, MODEL_WIDTH), jnp.float32).at[slot_token].add(grad_back)
    grad_expert_in, grad_expert_out = (
        lax.psum_scatter(
            grad_win.astype(jnp.bfloat16), "tensor", scatter_dimension=3, tiled=True
        ).astype(jnp.float32),
        lax.psum_scatter(
            grad_wout.astype(jnp.bfloat16), "tensor", scatter_dimension=2, tiled=True
        ).astype(jnp.float32),
    )
    own_grad_gate = slot_grad_gate[slot_rows].reshape(own_rows, TOPK)
    grad_gate_part = lax.dynamic_update_slice_in_dim(
        jnp.zeros((sequence_length, TOPK), jnp.float32), own_grad_gate, tp_index * own_rows, 0
    )
    grad_gates = lax.psum(grad_gate_part, "tensor")
    grad_chosen = gate_weights * (
        grad_gates - jnp.sum(gate_weights * grad_gates, axis=-1, keepdims=True)
    )
    grad_logits = jnp.sum(route_hot * grad_chosen[:, :, None], axis=1).astype(jnp.bfloat16)
    grad_router = product_left(moe_all, grad_logits)
    own_logit_grads = lax.dynamic_slice_in_dim(grad_logits, tp_index * own_rows, own_rows, 0)
    router_back = product_transposed(own_logit_grads, router_full)
    grad_normed_own = scatter_tokens(grad_normed_part) + expert_extra + router_back
    grad_from_moe, grad_gain_moe_part = normalize_back(hidden, scale_moe, gain_moe, grad_normed_own)
    grad_hidden = residual_error + grad_from_moe
    grad_attn = gather_tokens(grad_hidden.astype(jnp.bfloat16))
    grad_out_weight = product_left(grad_attn, mixed_heads)
    grad_mixed = (
        product(grad_attn, out_full)
        .astype(jnp.bfloat16)
        .reshape(sequence_length, kv_count, head_group, HEAD_SIZE)
    )

    def backward_block(running, block_index):
        grad_keys, grad_values = running
        first_row = block_index * block
        query_block = lax.dynamic_slice_in_dim(queries, first_row, block, 0)
        grad_block = lax.dynamic_slice_in_dim(grad_mixed, first_row, block, 0)
        scores = score_block(query_block, key_row_table, first_row, length)
        probs_full = jnp.exp(scores - log_totals[block_index])
        probs_low = probs_full.astype(jnp.bfloat16)
        grad_values = grad_values + jnp.einsum(
            "vgqk,qvgd->kvd", probs_low, grad_block, preferred_element_type=jnp.float32
        )
        grad_probs = jnp.einsum(
            "qvgd,kvd->vgqk", grad_block, value_row_table, preferred_element_type=jnp.float32
        )
        delta_sum = jnp.sum(probs_full * grad_probs, axis=-1, keepdims=True)
        grad_scores = (probs_full * (grad_probs - delta_sum)).astype(jnp.bfloat16)
        grad_query = (
            jnp.einsum(
                "vgqk,kvd->qvgd", grad_scores, key_row_table, preferred_element_type=jnp.float32
            )
            * HEAD_SIZE ** (-0.5)
        ).astype(jnp.bfloat16)
        grad_keys = grad_keys + jnp.einsum(
            "vgqk,qvgd->kvd", grad_scores, query_block, preferred_element_type=jnp.float32
        ) * HEAD_SIZE ** (-0.5)
        return ((grad_keys, grad_values), grad_query)

    start_grads = (
        jnp.zeros((sequence_length, kv_count, HEAD_SIZE), jnp.float32),
        jnp.zeros((sequence_length, kv_count, HEAD_SIZE), jnp.float32),
    )
    key_value_grads, query_grads = lax.scan(
        backward_block, start_grads, jnp.arange(sequence_length // block)
    )
    grad_queries = query_grads.reshape(sequence_length, head_count * HEAD_SIZE)
    grad_key_low = (
        key_value_grads[0].astype(jnp.bfloat16).reshape(sequence_length, kv_count * HEAD_SIZE)
    )
    grad_value_low = (
        key_value_grads[1].astype(jnp.bfloat16).reshape(sequence_length, kv_count * HEAD_SIZE)
    )
    grad_query_weight = product_left(normed_all, grad_queries)
    grad_kv_weight = jnp.stack(
        [product_left(normed_all, grad_key_low), product_left(normed_all, grad_value_low)], axis=0
    )
    grad_normed_attn = (
        product_transposed(grad_queries, query_full)
        + product_transposed(grad_key_low, kv_full[0])
        + product_transposed(grad_value_low, kv_full[1])
    )
    grad_normed_attn_own = scatter_tokens(grad_normed_attn)
    grad_from_attn, grad_gain_attn_part = normalize_back(
        residual, scale_attn, gain_attn, grad_normed_attn_own
    )
    input_grad = grad_hidden + grad_from_attn
    grad_w_query, grad_w_kv, grad_w_out, grad_w_router, grad_w_shared_in, grad_w_shared_out = (
        lax.psum_scatter(grad_query_weight, "dp", scatter_dimension=0, tiled=True),
        lax.psum_scatter(grad_kv_weight, "dp", scatter_dimension=1, tiled=True),
        lax.psum_scatter(grad_out_weight, "dp", scatter_dimension=0, tiled=True),
        lax.psum_scatter(grad_router, "dp", scatter_dimension=0, tiled=True),
        lax.psum_scatter(grad_shared_in, "dp", scatter_dimension=1, tiled=True),
        lax.psum_scatter(grad_shared_out, "dp", scatter_dimension=0, tiled=True),
    )
    loss_total, grad_gain_attn, grad_gain_moe = lax.psum(
        (loss_part, grad_gain_attn_part, grad_gain_moe_part), ("dp", "tensor")
    )
    valid_count = jnp.sum(lengths).astype(jnp.float32)
    loss = loss_total / (valid_count * MODEL_WIDTH)
    return (
        out_rows.astype(jnp.bfloat16),
        loss,
        input_grad,
        grad_gain_attn,
        grad_w_query,
        grad_w_kv,
        grad_w_out,
        grad_gain_moe,
        grad_w_router,
        grad_w_shared_in,
        grad_w_shared_out,
        grad_expert_in,
        grad_expert_out,
    )


def solution(mesh):
    return jax.shard_map(
        on_device,
        mesh=mesh,
        in_specs=(
            P(("dp", "tensor"), None),
            P(("dp", "tensor"), None),
            P(),
            P("dp", None),
            P(),
            P("dp", "tensor"),
            P(None, "dp", "tensor"),
            P("dp", "tensor"),
            P(),
            P("dp", None),
            P(None, "dp", "tensor"),
            P("dp", "tensor"),
            P("dp", None, None, "tensor"),
            P("dp", None, "tensor"),
        ),
        out_specs=(
            P(("dp", "tensor"), None),
            P(),
            P(("dp", "tensor"), None),
            P(),
            P("dp", "tensor"),
            P(None, "dp", "tensor"),
            P("dp", "tensor"),
            P(),
            P("dp", None),
            P(None, "dp", "tensor"),
            P("dp", "tensor"),
            P("dp", None, None, "tensor"),
            P("dp", None, "tensor"),
        ),
        check_vma=False,
    )
```

profile of v0, /device:TPU:0, one launch (start us, length us, event | category | flops | bytes accessed | tf_op | source)
XLA Modules:
  0.0 1985.2 jit_solution(13446222807111014756)
XLA Ops:
  14.4 9.2 all-gather.13.cloned.1.call-done
  23.6 61.7 %all-gather.15.cloned.1.call-done = bf16[2,1536,256]{2,1,0:T(8,128)(2,1)} async-done(((bf16[2,96,256]{2,1,0:T(8,128)(2,1)}), bf16[2,1536,256]{2,1,0:T(8,128)(2,1)}) %all-gather.15.cloned.1.call-update) | async-done | bytes 1572880 | tf_op jit(solution)/shard_map/all_gather | solution.py:161
  88.3 60.9 %all-gather.17.cloned.1.call-done = bf16[1536,768]{1,0:T(8,128)(2,1)} async-done(((bf16[96,768]{1,0:T(8,128)(2,1)}), bf16[1536,768]{1,0:T(8,128)(2,1)}) %all-gather.17.cloned.1.call-update) | async-done | bytes 2359312 | tf_op jit(solution)/shard_map/all_gather | solution.py:160
  159.9 53.1 %all-gather.19.cloned.1.call-done = bf16[1536,768]{1,0:T(8,128)(2,1)} async-done(((bf16[96,768]{1,0:T(8,128)(2,1)}), bf16[1536,768]{1,0:T(8,128)(2,1)}) %all-gather.19.cloned.1.call-update) | async-done | bytes 2359312 | tf_op jit(solution)/shard_map/all_gather | solution.py:162
  213.0 4.3 convolution_convert_fusion.4
  217.7 4.5 reduce-window.6
  223.3 6.4 scatter_custom_fusion
  229.7 11.1 scatter_custom_fusion.1
  243.8 10.2 gather_fusion
  253.9 5.9 broadcast_multiply_fusion
  259.8 4.7 all-to-all-start
  266.6 12.9 all-gather.27.cloned.1.call-done
  279.5 115.4 %all-to-all-done = bf16[16,128,1536]{2,1,0:T(8,128)(2,1)} async-done(((bf16[16,128,1536]{2,1,0:T(8,128)(2,1)}), bf16[16,128,1536]{2,1,0:T(8,128)(2,1)}, u32[]{:S(2)}, u32[]{:S(2)}) %all-to-all-start) | async-done | bytes 6291488 | tf_op jit(solution)/shard_map/all_to_all | solution.py:63
  395.0 10.1 convolution_bitcast_fusion.1
  409.8 7.5 convolution_convert_fusion
  417.3 45.6 %all-to-all-start.1 = ((bf16[16,128,1536]{2,1,0:T(8,128)(2,1)}), bf16[16,128,1536]{2,1,0:T(8,128)(2,1)}, u32[]{:S(2)}, u32[]{:S(2)}) async-start(bf16[16,128,1536]{2,1,0:T(8,128)(2,1)} %convolution_convert_fusion), calls=%async_computation.3 | async-start | bytes 12582912 | tf_op jit(solution)/shard_map/all_to_all | solution.py:67
  464.7 12.3 all-gather.21.cloned.1.call-done
  477.0 4.1 convolution_bitcast_fusion.5
  482.9 118.9 %all-gather.25.cloned.1.call-done = bf16[1536,512]{1,0:T(8,128)(2,1)} async-done(((bf16[96,512]{1,0:T(8,128)(2,1)}), bf16[1536,512]{1,0:T(8,128)(2,1)}) %all-gather.25.cloned.1.call-update) | async-done | bytes 1572880 | tf_op jit(solution)/shard_map/all_gather | solution.py:165
  605.3 40.4 %all-gather = bf16[16,96,16]{1,2,0:T(8,128)(2,1)S(1)} all-gather(bf16[1,96,16]{1,2,0:T(8,128)(2,1)S(1)} %bitcast.293), channel_id=1, replica_groups=mesh['dp'=16,'tensor'=2] {'dp'}, dimensions={0}, use_global_device_ids=true | all-gather | bytes 52224 | tf_op jit(solution)/shard_map/all_gather | solution.py:163
  647.5 6.2 scatter_custom_fusion.2
  655.1 8.2 bitcast_multiply_fusion
  663.3 22.2 %scatter_fusion = f32[256,1536]{1,0:T(8,128)S(1)} fusion(f32[256,1536]{1,0:T(8,128)S(1)} %convert_add_fusion.1, s32[2048]{0:T(1024)S(1)} %get-tuple-element.136, f32[2048,1536]{1,0:T(8,128)} %bitcast_multiply_fusion), kind=kCustom, calls=%fused_computation.6 | custom fusion | flops 3145728 | bytes 37756928 | tf_op jit(solution)/shard_map/scatter-add | solution.py:230
  687.0 10.2 gather_fusion.1
  701.0 135.0 %all_to_all.20 = bf16[16,128,1536]{2,1,0:T(8,128)(2,1)S(1)} all-to-all(bf16[16,128,1536]{2,1,0:T(8,128)(2,1)S(1)} %fusion.1), channel_id=1, replica_groups=mesh['dp'=16,'tensor'=2] {'dp'}, dimensions={0} | all-to-all | bytes 12582912 | tf_op jit(solution)/shard_map/all_to_all | solution.py:63
  836.0 9.5 fusion.30
  848.9 8.7 bitcast_convert_fusion
  857.6 4.7 all-to-all-start.3
  862.9 13.1 all-gather.31.cloned.1.call-done
  884.2 6.3 fusion
  890.5 8.4 gather_fusion.2
  905.3 70.0 %all-to-all-done.3 = bf16[16,128,1536]{2,1,0:T(8,128)(2,1)} async-done(((bf16[16,128,1536]{2,1,0:T(8,128)(2,1)}), bf16[16,128,1536]{2,1,0:T(8,128)(2,1)}, u32[]{:S(2)}, u32[]{:S(2)}) %all-to-all-start.3) | async-done | bytes 6291488 | tf_op jit(solution)/shard_map/all_to_all | solution.py:67
  975.3 24.3 %scatter_custom_fusion.4 = f32[256,1536]{1,0:T(8,128)} fusion(f32[256,1536]{1,0:T(8,128)} %convolution_add_fusion.2, s32[2048]{0:T(1024)S(1)} %get-tuple-element.136, bf16[2048,1536]{1,0:T(8,128)(2,1)} %bitcast.89), kind=kCustom, calls=%fused_computation.12 | custom fusion | flops 6291456 | bytes 7864320 | tf_op jit(solution)/shard_map/scatter-add | solution.py:259
  1008.4 5.5 convolution_bitcast_fusion
  1013.9 10.3 copy.106
  1025.7 7.4 fusion.27
  1033.2 11.8 fusion.18
  1049.6 4.3 fusion.4
  1086.5 78.7 %reduce-scatter.34.cloned.1.call-done = f32[96,16]{1,0:T(8,128)} async-done(((f32[1536,16]{1,0:T(8,128)}), f32[96,16]{1,0:T(8,128)}) %reduce-scatter.34.cloned.1.call-update) | async-done | bytes 6160
  1166.6 214.9 %all-reduce.4.cloned.1.call-done = f32[2,1536,512]{2,0,1:T(2,128)} async-done(((f32[2,1536,512]{2,0,1:T(2,128)}), f32[2,1536,512]{2,0,1:T(2,128)}) %all-reduce.4.cloned.1.call-update) | async-done | bytes 6291472
  1383.4 9.0 reduce-scatter.32.cloned.1.call-done
  1394.8 12.4 reduce-scatter.30.cloned.1.call-done
  1411.0 8.8 reduce-scatter.20.cloned.1.call-done
  1421.4 41.6 %all-reduce.1 = (f32[]{:T(128)}, f32[1536]{0:T(1024)}, f32[1536]{0:T(1024)}) all-reduce(f32[]{:T(128)S(6)} %mul_shard_map.3, f32[1536]{0:T(1024)S(1)} %get-tuple-element.118, f32[1536]{0:T(1024)S(1)} %get-tuple-element.116), channel_id=1, replica_groups=mesh['dp'=16,'tensor'=2] {'dp','tensor'}, use_global_device_ids=true, to_apply=%region_17.18 | all-reduce | flops 3073 | bytes 24584 | tf_op jit(solution)/shard_map/psum | solution.py:354
  1466.5 90.8 %reduce-scatter.28.cloned.1.call-done = f32[96,512]{1,0:T(8,128)} async-done(((f32[1536,512]{1,0:T(8,128)}), f32[96,512]{1,0:T(8,128)}) %reduce-scatter.28.cloned.1.call-update) | async-done | bytes 196624 | tf_op jit(solution)/shard_map/reduce_scatter | solution.py:352
  1557.3 135.3 %reduce-scatter.24.cloned.1.call-done = f32[2,96,256]{2,1,0:T(8,128)} async-done(((f32[2,1536,256]{2,1,0:T(8,128)}), f32[2,96,256]{2,1,0:T(8,128)}) %reduce-scatter.24.cloned.1.call-update) | async-done | bytes 196624 | tf_op jit(solution)/shard_map/reduce_scatter | solution.py:348
  1692.6 142.0 %reduce-scatter.22.cloned.1.call-done = f32[96,768]{1,0:T(8,128)} async-done(((f32[1536,768]{1,0:T(8,128)}), f32[96,768]{1,0:T(8,128)}) %reduce-scatter.22.cloned.1.call-update) | async-done | bytes 294928 | tf_op jit(solution)/shard_map/reduce_scatter | solution.py:347
  1834.6 142.7 %reduce-scatter.26.cloned.1.call-done = f32[96,768]{1,0:T(8,128)} async-done(((f32[1536,768]{1,0:T(8,128)}), f32[96,768]{1,0:T(8,128)}) %reduce-scatter.26.cloned.1.call-update) | async-done | bytes 294928 | tf_op jit(solution)/shard_map/reduce_scatter | solution.py:349
  (268 shorter events, 124.8 us)
Async XLA Ops:
  7.2 16.4 all-gather.13.cloned.1.call-start
  8.6 15.0 copy-start.43
  10.9 74.4 %all-gather.15.cloned.1.call-start = ((), (), s32[]{:S(2)}) async-start(), calls=%async_computation.16 | async-start | bytes 1671168 | tf_op jit(solution)/shard_map/all_gather | solution.py:161
  11.7 137.5 %all-gather.17.cloned.1.call-start = ((), (), s32[]{:S(2)}) async-start(), calls=%async_computation.17 | async-start | bytes 2506752 | tf_op jit(solution)/shard_map/all_gather | solution.py:160
  12.4 200.6 %all-gather.19.cloned.1.call-start = ((), (), s32[]{:S(2)}) async-start(), calls=%async_computation.18 | async-start | bytes 2506752 | tf_op jit(solution)/shard_map/all_gather | solution.py:162
  13.0 227.8 %reduce-scatter.14.cloned.1.call-start = ((), (), s32[]{:S(2)}) async-start(), calls=%async_computation.19 | async-start | bytes 2359296 | tf_op jit(solution)/shard_map/reduce_scatter | solution.py:57
  23.6 125.6 %copy-start.6 = (bf16[512,1536]{1,0:T(8,128)(2,1)S(1)}, bf16[512,1536]{1,0:T(8,128)(2,1)}, u32[]{:S(2)}) copy-start(bf16[512,1536]{1,0:T(8,128)(2,1)} %all-gather.13.cloned.1.call-done) | copy-start | bytes 4718596
  88.3 66.3 %copy-start.19 = (bf16[1,512,256]{1,2,0:T(8,128)(2,1)}, bf16[1,512,256]{1,2,0:T(8,128)(2,1)S(1)}, u32[]{:S(2)}) copy-start(bf16[1,512,256]{1,2,0:T(8,128)(2,1)S(1)} %get-tuple-element.133) | copy-start | bytes 786436
  88.3 68.5 %copy-start.29 = (bf16[1,512,256]{1,2,0:T(8,128)(2,1)}, bf16[1,512,256]{1,2,0:T(8,128)(2,1)S(1)}, u32[]{:S(2)}) copy-start(bf16[1,512,256]{1,2,0:T(8,128)(2,1)S(1)} %get-tuple-element.134) | copy-start | bytes 786436
  159.9 53.1 %copy-start.31 = (bf16[2,128,3,512]{3,1,2,0:T(8,128)(2,1)}, bf16[2,128,3,512]{3,1,2,0:T(8,128)(2,1)S(1)}, u32[]{:S(2)}) copy-start(bf16[2,128,3,512]{3,1,2,0:T(8,128)(2,1)S(1)} %fusion.49) | copy-start | bytes 2359300
  217.3 23.6 %copy-start.3 = (bf16[256,1536]{1,0:T(8,128)(2,1)S(1)}, bf16[256,1536]{1,0:T(8,128)(2,1)}, u32[]{:S(2)}) copy-start(bf16[256,1536]{1,0:T(8,128)(2,1)} %param.14) | copy-start | bytes 2359300
  217.3 25.0 %copy-start.36 = (f32[1536]{0:T(1024)S(1)}, f32[1536]{0:T(1024)}, u32[]{:S(2)}) copy-start(f32[1536]{0:T(1024)} %param.22) | copy-start | bytes 18436
  242.3 11.6 copy-start.41
  243.8 10.2 copy-start
  259.8 135.1 %all-to-all-start = ((bf16[16,128,1536]{2,1,0:T(8,128)(2,1)}), bf16[16,128,1536]{2,1,0:T(8,128)(2,1)}, u32[]{:S(2)}, u32[]{:S(2)}) async-start(bf16[16,128,1536]{2,1,0:T(8,128)(2,1)} %broadcast_multiply_fusion), calls=%async_computation.2 | async-start | bytes 12582912 | tf_op jit(solution)/shard_map/all_to_all | solution.py:63
  264.5 15.0 all-gather.27.cloned.1.call-start
  265.1 144.7 %all-gather.29.cloned.1.call-start = ((), (), s32[]{:S(2)}) async-start(), calls=%async_computation.25 | async-start | bytes 2359296 | tf_op jit(solution)/shard_map/all_gather | solution.py:217
  265.8 198.9 %all-gather.23.cloned.1.call-start = ((), (), s32[]{:S(2)}) async-start(), calls=%async_computation.21 | async-start | bytes 3342336 | tf_op jit(solution)/shard_map/all_gather | solution.py:164
  417.3 237.8 %all-to-all-start.1 = ((bf16[16,128,1536]{2,1,0:T(8,128)(2,1)}), bf16[16,128,1536]{2,1,0:T(8,128)(2,1)}, u32[]{:S(2)}, u32[]{:S(2)}) async-start(bf16[16,128,1536]{2,1,0:T(8,128)(2,1)} %convolution_convert_fusion), calls=%async_computation.3 | async-start | bytes 12582912 | tf_op jit(solution)/shard_map/all_to_all | solution.py:67
  462.9 14.1 all-gather.21.cloned.1.call-start
  463.7 138.1 %all-gather.25.cloned.1.call-start = ((), (), s32[]{:S(2)}) async-start(), calls=%async_computation.22 | async-start | bytes 1671168 | tf_op jit(solution)/shard_map/all_gather | solution.py:165
  464.3 189.4 %reduce-scatter.16.cloned.1.call-start = ((), (), s32[]{:S(2)}) async-start(), calls=%async_computation.23 | async-start | bytes 2359296 | tf_op jit(solution)/shard_map/reduce_scatter | solution.py:57
  482.8 118.9 %copy-start.27 = (bf16[512,512]{1,0:T(8,128)(2,1)}, bf16[512,512]{1,0:T(8,128)(2,1)S(1)}, u32[]{:S(2)}) copy-start(bf16[512,512]{1,0:T(8,128)(2,1)S(1)} %multiply_convert_fusion.6) | copy-start | bytes 1572868
  482.9 122.5 %copy-start.45 = (bf16[96,16]{0,1:T(8,128)(2,1)S(1)}, bf16[96,16]{0,1:T(8,128)(2,1)}, u32[]{:S(2)}) copy-start(bf16[96,16]{0,1:T(8,128)(2,1)} %param.23) | copy-start | bytes 9220
  482.9 163.6 %copy-start.13 = (bf16[512,1536]{1,0:T(8,128)(2,1)S(1)}, bf16[512,1536]{1,0:T(8,128)(2,1)}, u32[]{:S(2)}) copy-start(bf16[512,1536]{1,0:T(8,128)(2,1)} %all-gather.21.cloned.1.call-done) | copy-start | bytes 4718596
  605.3 48.4 %copy-start.4 = (bf16[256,1536]{1,0:T(8,128)(2,1)S(1)}, bf16[256,1536]{1,0:T(8,128)(2,1)}, u32[]{:S(2)}) copy-start(bf16[256,1536]{1,0:T(8,128)(2,1)} %reduce-scatter.14.cloned.1.call-done) | copy-start | bytes 2359300
  687.0 10.2 copy-start.1
  701.0 135.0 %copy-start.49 = (bf16[1,1536,512]{2,1,0:T(8,128)(2,1)S(1)}, bf16[1,1536,512]{2,1,0:T(8,128)(2,1)}, u32[]{:S(2)}) copy-start(bf16[1,1536,512]{2,1,0:T(8,128)(2,1)} %all-gather.29.cloned.1.call-done) | copy-start | bytes 4718596
  836.0 9.5 copy-start.12
  857.6 117.7 %all-to-all-start.3 = ((bf16[16,128,1536]{2,1,0:T(8,128)(2,1)}), bf16[16,128,1536]{2,1,0:T(8,128)(2,1)}, u32[]{:S(2)}, u32[]{:S(2)}) async-start(bf16[16,128,1536]{2,1,0:T(8,128)(2,1)} %bitcast_convert_fusion), calls=%async_computation.6 | async-start | bytes 12582912 | tf_op jit(solution)/shard_map/all_to_all | solution.py:67
  862.3 13.7 all-gather.31.cloned.1.call-start
  862.9 39.7 %reduce-scatter.18.cloned.1.call-start = ((), (), s32[]{:S(2)}) async-start(), calls=%async_computation.27 | async-start | bytes 2359296 | tf_op jit(solution)/shard_map/reduce_scatter | solution.py:57
  883.7 162.0 %all-gather.33.cloned.1.call-start = ((), (), s32[]{:S(2)}) async-start(), calls=%async_computation.28 | async-start | bytes 2359296 | tf_op jit(solution)/shard_map/all_gather | solution.py:53
  975.3 24.3 %copy-start.5 = (bf16[256,1536]{1,0:T(8,128)(2,1)S(1)}, bf16[256,1536]{1,0:T(8,128)(2,1)}, u32[]{:S(2)}) copy-start(bf16[256,1536]{1,0:T(8,128)(2,1)} %reduce-scatter.14.cloned.1.call-done) | copy-start | bytes 2359300
  975.3 24.3 %copy-start.37 = (f32[1536]{0:T(1024)S(1)}, f32[1536]{0:T(1024)}, u32[]{:S(2)}) copy-start(f32[1536]{0:T(1024)} %param.22) | copy-start | bytes 18436
  975.3 24.3 %copy-start.42 = (f32[256]{0:T(256)S(1)}, f32[256]{0:T(256)}, u32[]{:S(2)}) copy-start(f32[256]{0:T(256)} %copy-done.41) | copy-start | bytes 3076
  1005.1 160.1 %reduce-scatter.34.cloned.1.call-start = ((), (), s32[]{:S(2)}) async-start(), calls=%async_computation.36 | async-start | bytes 835584
  1008.3 373.2 %all-reduce.4.cloned.1.call-start = ((), (), s32[]{:S(2)}) async-start(), calls=%async_computation.37 | async-start | bytes 12582912
  1024.2 368.3 %reduce-scatter.32.cloned.1.call-start = ((), (), s32[]{:S(2)}) async-start(), calls=%async_computation.35 | async-start | bytes 2359296 | tf_op jit(solution)/shard_map/reduce_scatter | solution.py:264
  1033.1 374.1 %reduce-scatter.30.cloned.1.call-start = ((), (), s32[]{:S(2)}) async-start(), calls=%async_computation.34 | async-start | bytes 4718592 | tf_op jit(solution)/shard_map/reduce_scatter | solution.py:261
  1045.0 374.9 %reduce-scatter.20.cloned.1.call-start = ((), (), s32[]{:S(2)}) async-start(), calls=%async_computation.29 | async-start | bytes 2359296 | tf_op jit(solution)/shard_map/reduce_scatter | solution.py:57
  1064.8 492.6 %reduce-scatter.28.cloned.1.call-start = ((), (), s32[]{:S(2)}) async-start(), calls=%async_computation.33 | async-start | bytes 3342336 | tf_op jit(solution)/shard_map/reduce_scatter | solution.py:352
  1068.6 624.0 %reduce-scatter.24.cloned.1.call-start = ((), (), s32[]{:S(2)}) async-start(), calls=%async_computation.31 | async-start | bytes 3342336 | tf_op jit(solution)/shard_map/reduce_scatter | solution.py:348
  1074.2 760.4 %reduce-scatter.22.cloned.1.call-start = ((), (), s32[]{:S(2)}) async-start(), calls=%async_computation.30 | async-start | bytes 5013504 | tf_op jit(solution)/shard_map/reduce_scatter | solution.py:347
  1078.1 899.2 %reduce-scatter.26.cloned.1.call-start = ((), (), s32[]{:S(2)}) async-start(), calls=%async_computation.32 | async-start | bytes 5013504 | tf_op jit(solution)/shard_map/reduce_scatter | solution.py:349
  1394.8 25.0 %copy-start.38 = (f32[1536]{0:T(1024)S(1)}, f32[1536]{0:T(1024)}, u32[]{:S(2)}) copy-start(f32[1536]{0:T(1024)} %param.18) | copy-start | bytes 18436
  1394.8 25.0 %copy-start.44 = (f32[256]{0:T(256)S(1)}, f32[256]{0:T(256)}, u32[]{:S(2)}) copy-start(f32[256]{0:T(256)} %copy-done.43) | copy-start | bytes 3076
  1394.8 68.9 %copy-start.15 = (f32[256,1536]{1,0:T(8,128)S(1)}, f32[256,1536]{1,0:T(8,128)}, u32[]{:S(2)}) copy-start(f32[256,1536]{1,0:T(8,128)} %get-tuple-element.124) | copy-start | bytes 4718596
  (36 other events, 89.3 us)
Sparse Core Ops, SparseCore 0:
  11.0 12.4 all-gather.12
  26.2 59.0 all-gather.14
  88.1 61.0 all-gather.16
  151.9 61.0 all-gather.18
  217.4 7.8 reduce-scatter.13
  266.6 12.8 all-gather.26
  281.1 10.8 all-gather.28
  295.0 130.3 all-gather.22
  466.0 11.0 all-gather.20
  480.0 121.6 all-gather.24
  605.5 9.0 reduce-scatter.15
  865.0 10.9 all-gather.30
  883.8 10.2 reduce-scatter.17
  1005.2 30.9 all-gather.32
  1041.5 123.6 reduce-scatter.33
  1172.1 209.4 all-reduce.3
  1384.3 8.0 reduce-scatter.31
  1395.1 12.1 reduce-scatter.29
  1409.6 10.1 reduce-scatter.19
  1425.2 132.0 reduce-scatter.27
  1562.9 129.6 reduce-scatter.23
  1698.3 136.1 reduce-scatter.21
  1841.1 136.1 reduce-scatter.25
where the time goes:
time: 1990 us
  waiting for transfers between devices  1370 us (69%)
  blocking collectives  220 us (11%)
  matrix products  123 us (6%)
  other arithmetic  106 us (5%)
  local copies, waits for them, and re-layouts  91.6 us (5%)
  starting transfers between devices  57.1 us (3%)
    unnamed x25, waiting for transfers between devices  299 us
    reduce_scatter x1, waiting for transfers between devices, on_device(): lax.psum_scatter(grad_out_weight, 'dp', scatter_dimension=0, tiled=True)  143 us
    reduce_scatter x1, waiting for transfers between devices, on_device(): lax.psum_scatter(grad_query_weight, 'dp', scatter_dimension=0, tiled=True)  142 us
    reduce_scatter x1, waiting for transfers between devices, on_device(): lax.psum_scatter(grad_kv_weight, 'dp', scatter_dimension=1, tiled=True)  135 us
    all_to_all x1, blocking collectives, to_owner(): lax.all_to_all(rows_out, 'dp', split_axis=0, concat_axis=0, tiled=True)  135 us
    all_gather x1, waiting for transfers between devices, on_device(): lax.all_gather(w_shared_out, 'dp', axis=0, tiled=True)  119 us
    all_to_all x1, waiting for transfers between devices, to_owner(): lax.all_to_all(rows_out, 'dp', split_axis=0, concat_axis=0, tiled=True)  115 us
    reduce_scatter x1, waiting for transfers between devices, on_device(): lax.psum_scatter(grad_shared_out, 'dp', scatter_dimension=0, tiled=True)  90.8 us
  transfers between devices with their start and end apart: 26, of which 19 were waited for; matrix products, arithmetic and copies ran while one was open for 9% of the time, Pallas kernels for 0%

commit v1 on v0

v1 whole, which is shorter than its diff:
```python
import jax
import jax.numpy as jnp
from jax import lax
from jax.sharding import PartitionSpec as P

HEAD_SIZE = 128
TOPK = 6

norm_eps = 1e-05
masked_score = -1e30
bf16 = jnp.bfloat16
f32 = jnp.float32


def product(left_side, right_side):
    return jnp.dot(left_side, right_side, preferred_element_type=f32)


def product_transposed(left_side, right_side):
    return lax.dot_general(
        left_side, right_side, (((1,), (1,)), ((), ())), preferred_element_type=f32
    )


def product_left(left_side, right_side):
    return lax.dot_general(
        left_side, right_side, (((0,), (0,)), ((), ())), preferred_element_type=f32
    )


def contract(spec, *operands):
    return jnp.einsum(spec, *operands, preferred_element_type=f32)


def normalize_rows(values, gain):
    row_scale = lax.rsqrt(jnp.mean(values * values, axis=-1, keepdims=True) + norm_eps)
    return ((values * row_scale * gain).astype(bf16), row_scale)


def normalize_back(values, row_scale, gain, grad_normed):
    scaled = grad_normed * gain
    inner_mean = jnp.mean(scaled * values, axis=-1, keepdims=True)
    grad_values = row_scale * (scaled - values * row_scale * row_scale * inner_mean)
    grad_gain = jnp.sum(grad_normed * values * row_scale, axis=0)
    return (grad_values, grad_gain)


def swish_back(pre_gate, pre_up, grad_act):
    logistic = jax.nn.sigmoid(pre_gate)
    grad_gate = grad_act * pre_up * logistic * (1.0 + pre_gate * (1.0 - logistic))
    grad_up = grad_act * pre_gate * logistic
    return grad_gate.astype(bf16), grad_up.astype(bf16)


def subset_masks(bits):
    masks = [0]
    for bit in bits:
        masks = masks + [mask | (1 << bit) for mask in masks]
    return masks


class Layout:
    def __init__(self):
        self.dp = lax.axis_size("dp")
        self.tp = lax.axis_size("tensor")
        self.place = lax.axis_index("dp")
        self.core = lax.axis_index("tensor")
        bits = self.dp.bit_length() - 1
        self.w_bits = [bit for bit in (1, 3) if bit < bits]
        self.g_bits = [bit for bit in range(bits) if bit not in self.w_bits]
        self.w_masks = subset_masks(self.w_bits)
        self.g_masks = subset_masks(self.g_bits)
        self.steps = [(bit, bit) for bit in range(bits - 1, 1, -1)] + [(1, 0), (0, 1)]

    def shift(self, values, mask):
        return lax.ppermute(values, "dp", [(i, i ^ mask) for i in range(self.dp)])

    def shift_core(self, values, mask):
        return lax.ppermute(values, "tensor", [(i, i ^ mask) for i in range(self.tp)])

    def shift_step(self, values, step):
        even, odd = step
        pairs = []
        for i in range(self.dp):
            for c in range(self.tp):
                target = i ^ (1 << (odd if c % 2 else even))
                pairs.append((i * self.tp + c, target * self.tp + c))
        return lax.ppermute(values, ("dp", "tensor"), pairs)

    def step_bit(self, step):
        even, odd = step
        return even if even == odd else jnp.where(self.core % 2 == 1, odd, even)

    def gather_dp(self, shard):
        held = shard[None]
        for step in self.steps:
            held = jnp.concatenate([held, self.shift_step(held, step)], axis=0)
        apart = self.place ^ jnp.arange(self.dp)
        at = sum(((apart >> self.step_bit(step)) & 1) << k for k, step in enumerate(self.steps))
        return held[at].reshape((-1,) + shard.shape[1:])

    def scatter_dp(self, whole):
        blocks = whole.astype(bf16).reshape((self.dp, -1) + whole.shape[1:])
        rel = jnp.arange(self.dp)
        apart = sum(((rel >> k) & 1) << self.step_bit(step) for k, step in enumerate(self.steps))
        at = self.place ^ apart
        half = self.dp // 2
        keep, send = blocks[at[:half]].astype(f32), blocks[at[half:]]
        for k in range(len(self.steps) - 1, -1, -1):
            total = keep + self.shift_step(send, self.steps[k]).astype(f32)
            half = half // 2
            if k > 0:
                keep, send = total[:half], total[half:].astype(bf16)
        return total[0]

    def gather_g(self, values):
        return [values] + [self.shift(values, mask) for mask in self.g_masks[1:]]

    def gather_w(self, values):
        held = [values]
        for bit in reversed(self.w_bits):
            held = held + [self.shift(v, 1 << bit) for v in held]
        order = subset_masks(list(reversed(self.w_bits)))
        return [held[order.index(mask)] for mask in self.w_masks]

    def scatter_w(self, blocks):
        order = subset_masks(list(reversed(self.w_bits)))
        held = [blocks[self.w_masks.index(mask)] for mask in order]
        for bit in self.w_bits:
            half = len(held) // 2
            held = [
                keep.astype(f32) + self.shift(send.astype(bf16), 1 << bit).astype(f32)
                for keep, send in zip(held[:half], held[half:])
            ]
        return held[0]

    def gather_core(self, values):
        return [values] + [self.shift_core(values, k) for k in range(1, self.tp)]

    def scatter_core(self, blocks):
        total = blocks[0].astype(f32)
        for k in range(1, self.tp):
            total = total + self.shift_core(blocks[k].astype(bf16), k).astype(f32)
        return total

    def sum_all(self, values):
        for bit in range(self.dp.bit_length() - 1):
            values = values + self.shift(values, 1 << bit)
        for bit in range(self.tp.bit_length() - 1):
            values = values + self.shift_core(values, 1 << bit)
        return values

    def chunk(self, mask):
        place = self.place ^ mask
        return sum(((place >> bit) & 1) << k for k, bit in enumerate(self.g_bits))

    def rows_order(self):
        apart = self.place ^ jnp.arange(self.dp)
        g = sum(((apart >> bit) & 1) << k for k, bit in enumerate(self.g_bits))
        w = sum(((apart >> bit) & 1) << k for k, bit in enumerate(self.w_bits))
        return g * len(self.w_masks) + w

    def rows_apart(self):
        masks = jnp.array([g | w for g in self.g_masks for w in self.w_masks], jnp.int32)
        return self.place ^ masks


def gather_shared(lay, shared_in, shared_out):
    part = shared_out.shape[1] // len(lay.g_masks)
    rows = shared_out.shape[0]
    stacked = jnp.concatenate([shared_in, shared_out[None]], axis=0)

    def piece(mask):
        return lax.dynamic_slice_in_dim(stacked, lay.chunk(mask) * part, part, 2)

    arrived = jnp.stack([piece(0)] + [lay.shift(piece(m), m) for m in lay.g_masks[1:]])
    everyone = jnp.stack(lay.gather_w(arrived), axis=1)
    natural = everyone.reshape((lay.dp, 3, rows, part))[lay.rows_order()]
    own = natural.transpose(1, 0, 2, 3).reshape(3, lay.dp * rows, part)
    return jnp.concatenate(lay.gather_core(own), axis=2)


def scatter_shared(lay, grads):
    part = grads.shape[2] // lay.tp
    rows = grads.shape[1] // lay.dp
    own = lay.scatter_core([grads[:, :, k * part : (k + 1) * part] for k in range(lay.tp)])
    natural = own.astype(bf16).reshape(3, lay.dp, rows, part).transpose(1, 0, 2, 3)
    blocks = natural[lay.rows_apart()].reshape(len(lay.g_masks), len(lay.w_masks), 3, rows, part)
    summed = lay.scatter_w([blocks[:, k] for k in range(len(lay.w_masks))])
    out = jnp.zeros((3, rows, part * len(lay.g_masks)), f32)
    for k, mask in enumerate(lay.g_masks):
        got = summed[k] if k == 0 else lay.shift(summed[k].astype(bf16), mask).astype(f32)
        out = lax.dynamic_update_slice_in_dim(out, got, lay.chunk(mask) * part, 2)
    return out


def on_device(
    block_input,
    teacher,
    lengths,
    routes,
    gain_attn,
    w_query,
    key_value_weight,
    w_out,
    gain_moe,
    w_router,
    w_shared_in,
    w_shared_out,
    w_expert_in,
    w_expert_out,
):
    lay = Layout()
    own_rows, width = block_input.shape
    tp, dp = lay.tp, lay.dp
    sequence_length = own_rows * tp
    experts = w_expert_in.shape[0] * dp
    capacity = max(2, own_rows * TOPK * 4 // (3 * experts))
    n_g, n_w = len(lay.g_masks), len(lay.w_masks)
    length = lengths[lay.place]
    slices = jnp.array(range(tp), jnp.int32) ^ lay.core
    positions = (slices[:, None] * own_rows + jnp.arange(own_rows)[None, :]).reshape(-1)
    own_valid = (positions[:own_rows] < length).astype(f32)[:, None]
    head_count = w_query.shape[1] // HEAD_SIZE
    kv_count = key_value_weight.shape[2] // HEAD_SIZE
    head_group = head_count // kv_count
    q_dim, kv_dim = head_count * HEAD_SIZE, kv_count * HEAD_SIZE

    qkv_full = lay.gather_dp(
        jnp.concatenate([w_query, key_value_weight[0], key_value_weight[1]], axis=1)
    )
    out_full = lay.gather_dp(w_out)
    router_full = lax.all_gather(w_router, "dp", axis=0, tiled=True)
    shared_full = gather_shared(lay, w_shared_in, w_shared_out)
    shared_in_full, shared_out_full = shared_full[:2], shared_full[2]
    expert_own = jnp.concatenate([w_expert_in[0], w_expert_out], axis=0)
    expert_parts = lay.gather_core(jnp.stack(lay.gather_w(expert_own)))
    expert_whole = jnp.concatenate(expert_parts, axis=3)
    expert_in_whole, expert_out_whole = expert_whole[:, :2], expert_whole[:, 2]

    inputs_all = jnp.concatenate(lay.gather_core(block_input), axis=0).astype(f32)
    normed_all, scale_all = normalize_rows(inputs_all, gain_attn)
    residual, scale_attn = inputs_all[:own_rows], scale_all[:own_rows]
    projected = product(normed_all, qkv_full).astype(bf16)
    queries = projected[:, :q_dim].reshape(sequence_length, kv_count, head_group, HEAD_SIZE)
    key_row_table = projected[:, q_dim : q_dim + kv_dim].reshape(
        sequence_length, kv_count, HEAD_SIZE
    )
    value_row_table = projected[:, q_dim + kv_dim :].reshape(sequence_length, kv_count, HEAD_SIZE)
    allowed = (positions[None, :] <= positions[:, None]) & (positions[None, :] < length)
    scores = contract("qvgd,kvd->vgqk", queries, key_row_table) * HEAD_SIZE ** (-0.5)
    scores = jnp.where(allowed, scores, masked_score)
    row_max = jnp.max(scores, axis=-1, keepdims=True)
    exponent_terms = jnp.exp(scores - row_max)
    row_sum = jnp.sum(exponent_terms, axis=-1, keepdims=True)
    probs_full = exponent_terms / row_sum
    probs_low = probs_full.astype(bf16)
    mixed_heads = (
        contract("vgqk,kvd->qvgd", probs_low, value_row_table)
        .astype(bf16)
        .reshape(sequence_length, q_dim)
    )

    def by_core(rows):
        return [rows[k * own_rows : (k + 1) * own_rows] for k in range(tp)]

    hidden = residual + lay.scatter_core(by_core(product_transposed(mixed_heads, out_full)))
    moe_own, scale_moe = normalize_rows(hidden, gain_moe)

    own_routes = lax.dynamic_slice_in_dim(routes, lay.core * own_rows, own_rows, 0)
    group_routes = jnp.stack(lay.gather_g(own_routes))
    expert_ids = jnp.arange(experts, dtype=jnp.int32)
    member = jnp.any(group_routes[:, :, :, None] == expert_ids, axis=2)
    held_ids = lay.place ^ jnp.array(lay.w_masks, jnp.int32)
    held_member = jnp.any(group_routes[:, :, :, None] == held_ids, axis=2).astype(bf16)
    before = jnp.tril(jnp.ones((own_rows, own_rows), bf16), -1)
    position = contract("ut,gtj->guj", before, held_member)
    position = jnp.where(held_member > 0, position, -1.0)
    dispatch = (
        position.transpose(0, 2, 1)[:, :, None, :] == jnp.arange(capacity, dtype=f32)[:, None]
    ).astype(bf16)

    moe_all = jnp.stack(lay.gather_g(moe_own))
    logits = contract("gtd,de->gte", moe_all, router_full)
    shown = jnp.where(member, logits, masked_score)
    gate_terms = jnp.exp(shown - jnp.max(shown, axis=-1, keepdims=True))
    gates = gate_terms / jnp.sum(gate_terms, axis=-1, keepdims=True)
    held_gates = jnp.sum(gates[:, :, None, :] * (expert_ids == held_ids[:, None]), axis=-1)
    slot_gate = jnp.sum(dispatch.astype(f32) * held_gates.transpose(0, 2, 1)[:, :, None, :], axis=-1)
    slot_gate = slot_gate.transpose(1, 0, 2).reshape(n_w, n_g * capacity, 1)
    group_rows = moe_all.reshape(n_g * own_rows, width)
    shared_pre = contract("td,cdf->ctf", group_rows, shared_in_full)
    shared_act = (jax.nn.silu(shared_pre[0]) * shared_pre[1]).astype(bf16)
    work_rows = (
        contract("gjct,gtd->jgcd", dispatch, moe_all)
        .astype(bf16)
        .reshape(n_w, n_g * capacity, width)
    )
    pre_acts = contract("jrd,jcdf->jcrf", work_rows, expert_in_whole)
    activated = jax.nn.silu(pre_acts[:, 0]) * pre_acts[:, 1]
    act_low = activated.astype(bf16)
    produced = (contract("jrf,jdf->jrd", act_low, expert_out_whole) * slot_gate).astype(bf16)
    combined = contract(
        "gjct,jgcd->gtd", dispatch, produced.reshape(n_w, n_g, capacity, width)
    ) + product_transposed(shared_act, shared_out_full).reshape(n_g, own_rows, width)

    def scatter_g(parts):
        total = parts[0].astype(f32)
        for k in range(1, n_g):
            total = total + lay.shift(parts[k].astype(bf16), lay.g_masks[k]).astype(f32)
        return total

    out_rows = (hidden + scatter_g([combined[k] for k in range(n_g)])) * own_valid
    residual_error = (out_rows - teacher.astype(f32)) * own_valid
    loss_part = 0.5 * jnp.sum(residual_error * residual_error)

    grad_all = jnp.stack(lay.gather_g(residual_error.astype(bf16)))
    grad_rows = (
        contract("gjct,gtd->jgcd", dispatch, grad_all)
        .astype(bf16)
        .reshape(n_w, n_g * capacity, width)
    )
    back_act = contract("jrd,jdf->jrf", grad_rows, expert_out_whole)
    slot_grad_gate = jnp.sum(back_act * act_low.astype(f32), axis=-1)
    grad_wout = contract("jrd,jrf->jdf", grad_rows, (activated * slot_gate).astype(bf16))
    grad_gate_pre, grad_up_pre = swish_back(pre_acts[:, 0], pre_acts[:, 1], back_act * slot_gate)
    grad_pre = jnp.stack([grad_gate_pre, grad_up_pre], axis=1)
    grad_win = contract("jrd,jcrf->jcdf", work_rows, grad_pre)
    grad_inputs = contract("jcrf,jcdf->jrd", grad_pre, expert_in_whole).astype(bf16)
    group_grad = grad_all.reshape(n_g * own_rows, width)
    grad_shared_act = product(group_grad, shared_out_full)
    grad_shared_out = product_left(group_grad, shared_act)
    grad_shared_pre = jnp.stack(swish_back(shared_pre[0], shared_pre[1], grad_shared_act))
    grad_shared_in = contract("td,ctf->cdf", group_rows, grad_shared_pre)
    grad_combined = contract(
        "gjct,jgcd->gtd", dispatch, grad_inputs.reshape(n_w, n_g, capacity, width)
    ) + contract("ctf,cdf->td", grad_shared_pre, shared_in_full).reshape(n_g, own_rows, width)
    held_grad_gates = jnp.sum(
        dispatch.astype(f32) * slot_grad_gate.reshape(n_w, n_g, capacity).transpose(1, 0, 2)[..., None],
        axis=2,
    )
    spread = (expert_ids[None, :] == held_ids[:, None]).astype(f32)
    grad_gates_part = jnp.sum(held_grad_gates[..., None] * spread[None, :, None, :], axis=1)
    high = grad_gates_part.astype(bf16)
    low = (grad_gates_part - high.astype(f32)).astype(bf16)
    pad = -(2 * experts) % 128
    payload = jnp.concatenate(
        [grad_combined.astype(bf16), high, low, jnp.zeros((n_g, own_rows, pad), bf16)], axis=-1
    )
    returned = scatter_g([payload[k] for k in range(n_g)])
    grad_gates = returned[:, width : width + experts] + returned[:, width + experts : width + 2 * experts]
    own_gates = gates[0]
    grad_logits = (
        own_gates * (grad_gates - jnp.sum(own_gates * grad_gates, axis=-1, keepdims=True))
    ).astype(bf16)
    grad_router_part = product_left(moe_own, grad_logits)
    grad_normed_own = returned[:, :width] + product_transposed(grad_logits, router_full)

    grad_expert = jnp.concatenate([grad_win, grad_wout[:, None]], axis=1)
    part = grad_expert.shape[3] // tp
    grad_expert = lay.scatter_core(
        [grad_expert[..., k * part : (k + 1) * part] for k in range(tp)]
    )
    grad_expert = lay.scatter_w([grad_expert[k] for k in range(n_w)])
    grad_w_expert_in, grad_w_expert_out = grad_expert[None, :2], grad_expert[2:3]
    grad_shared = scatter_shared(lay, jnp.concatenate([grad_shared_in, grad_shared_out[None]]))

    grad_from_moe, grad_gain_moe_part = normalize_back(hidden, scale_moe, gain_moe, grad_normed_own)
    grad_hidden = residual_error + grad_from_moe
    grad_attn = jnp.concatenate(lay.gather_core(grad_hidden.astype(bf16)), axis=0)
    grad_w_out = lay.scatter_dp(product_left(grad_attn, mixed_heads))
    grad_mixed = (
        product(grad_attn, out_full)
        .astype(bf16)
        .reshape(sequence_length, kv_count, head_group, HEAD_SIZE)
    )
    grad_values = contract("vgqk,qvgd->kvd", probs_low, grad_mixed)
    grad_probs = contract("qvgd,kvd->vgqk", grad_mixed, value_row_table)
    delta_sum = jnp.sum(probs_full * grad_probs, axis=-1, keepdims=True)
    grad_scores = (probs_full * (grad_probs - delta_sum)).astype(bf16)
    grad_queries = contract("vgqk,kvd->qvgd", grad_scores, key_row_table) * HEAD_SIZE ** (-0.5)
    grad_keys = contract("vgqk,qvgd->kvd", grad_scores, queries) * HEAD_SIZE ** (-0.5)
    grad_projected = jnp.concatenate(
        [
            grad_queries.astype(bf16).reshape(sequence_length, q_dim),
            grad_keys.astype(bf16).reshape(sequence_length, kv_dim),
            grad_values.astype(bf16).reshape(sequence_length, kv_dim),
        ],
        axis=1,
    )
    grad_qkv = lay.scatter_dp(product_left(normed_all, grad_projected))
    grad_normed_attn = lay.scatter_core(by_core(product_transposed(grad_projected, qkv_full)))
    grad_from_attn, grad_gain_attn_part = normalize_back(
        residual, scale_attn, gain_attn, grad_normed_attn
    )
    input_grad = grad_hidden + grad_from_attn
    grad_w_kv = jnp.stack(
        [grad_qkv[:, q_dim : q_dim + kv_dim], grad_qkv[:, q_dim + kv_dim :]], axis=0
    )
    grad_w_router = lax.psum_scatter(
        lay.scatter_core([grad_router_part, grad_router_part]) if tp == 2 else lax.psum(grad_router_part, "tensor"),
        "dp",
        scatter_dimension=0,
        tiled=True,
    )
    small = jnp.stack(
        [grad_gain_attn_part, grad_gain_moe_part, jnp.full((width,), loss_part, f32)], axis=0
    )
    small = lay.sum_all(small)
    loss = small[2, 0] / (jnp.sum(lengths).astype(f32) * width)
    return (
        out_rows.astype(bf16),
        loss,
        input_grad,
        small[0],
        grad_qkv[:, :q_dim],
        grad_w_kv,
        grad_w_out,
        small[1],
        grad_w_router,
        grad_shared[:2],
        grad_shared[2],
        grad_w_expert_in,
        grad_w_expert_out,
    )


def solution(mesh):
    rows, weights = P(("dp", "tensor"), None), P("dp", "tensor")
    stacked = P(None, "dp", "tensor")
    expert_in, expert_out = P("dp", None, None, "tensor"), P("dp", None, "tensor")
    return jax.shard_map(
        on_device,
        mesh=mesh,
        in_specs=(
            rows,
            rows,
            P(),
            P("dp", None),
            P(),
            weights,
            stacked,
            weights,
            P(),
            P("dp", None),
            stacked,
            weights,
            expert_in,
            expert_out,
        ),
        out_specs=(
            rows,
            P(),
            rows,
            P(),
            weights,
            stacked,
            weights,
            P(),
            P("dp", None),
            stacked,
            weights,
            expert_in,
            expert_out,
        ),
        check_vma=False,
    )
```

time: 1990 us -> 1030 us (0.52)
  waiting for transfers between devices: 1370 us -> 530 us
  blocking collectives: 220 us -> 41.8 us
  matrix products: 123 us -> 146 us
    reduce_scatter x10 -> x0, waiting for transfers between devices: 541 us -> none  [the longest x1 143 us: on_device(): lax.psum_scatter(grad_out_weight, 'dp', scatter_dimension=0, tiled=True)]
    ppermute x0 -> x63, waiting for transfers between devices: none -> 412 us  [the longest x37 273 us: shift(): return lax.ppermute(values, 'dp', [(i, i ^ mask) for i in range(self.dp)])]
    all_gather x11 -> x0, waiting for transfers between devices: 342 us -> none  [the longest x1 119 us: on_device(): lax.all_gather(w_shared_out, 'dp', axis=0, tiled=True)]
    all_to_all x3 -> x0, waiting for transfers between devices: 185 us -> none  [the longest x1 115 us: to_owner(): lax.all_to_all(rows_out, 'dp', split_axis=0, concat_axis=0, tiled=True)]
    unnamed x25 -> x2, waiting for transfers between devices: 299 us -> 118 us
    all_to_all x1 -> x0, blocking collectives: 135 us -> none  [to_owner(): lax.all_to_all(rows_out, 'dp', split_axis=0, concat_axis=0, tiled=True)]
    ppermute x0 -> x63, starting transfers between devices: none -> 63.5 us  [the longest x37 45 us: shift(): return lax.ppermute(values, 'dp', [(i, i ^ mask) for i in range(self.dp)])]
    all_to_all x3 -> x0, starting transfers between devices: 55 us -> none  [the longest x2 50.3 us: from_owner(): lax.all_to_all(rows_back.astype(jnp.bfloat16), 'dp', split_axis=0, concat...]
  transfers between devices with their start and end apart: 26 -> 64, of which waited for: 19 -> 29; matrix products, arithmetic and copies ran while one was open for 9% -> 21% of each run, Pallas kernels for 0% -> 0%
where the time goes in v1:
time: 1030 us
  waiting for transfers between devices  530 us (51%)
  matrix products  146 us (14%)
  other arithmetic  118 us (11%)
  local copies, waits for them, and re-layouts  107 us (10%)
  starting transfers between devices  63.6 us (6%)
  blocking collectives  41.8 us (4%)
  between operations  18.9 us (2%)
    ppermute x37, waiting for transfers between devices, shift(): return lax.ppermute(values, 'dp', [(i, i ^ mask) for i in range(self.dp)])  273 us
    ppermute x16, waiting for transfers between devices, shift_step(): return lax.ppermute(values, ('dp', 'tensor'), pairs)  139 us
    unnamed x2, waiting for transfers between devices  118 us
    dot_general x19, matrix products, contract(): return jnp.einsum(spec, *operands, preferred_element_type=f32)  106 us
    ppermute x37, starting transfers between devices, shift(): return lax.ppermute(values, 'dp', [(i, i ^ mask) for i in range(self.dp)])  45 us
    all_gather x1, blocking collectives, on_device(): router_full = lax.all_gather(w_router, 'dp', axis=0, tiled=True)  41.8 us
    unnamed x200, local copies, waits for them, and re-layouts  32.4 us
    another operation x4, other arithmetic  25.8 us
  transfers between devices with their start and end apart: 64, of which 29 were waited for; matrix products, arithmetic and copies ran while one was open for 21% of the time, Pallas kernels for 0%

profile of v1, /device:TPU:0, one launch (start us, length us, event | category | flops | bytes accessed | tf_op | source)
XLA Modules:
  0.0 1025.1 jit_solution(3969922000616907994)
XLA Ops:
  13.6 4.0 collective-permute-start.14
  31.9 97.1 %collective-permute-done.14 = bf16[3,1536,256]{1,2,0:T(8,128)(2,1)} collective-permute-done((bf16[3,1536,256]{1,2,0:T(8,128)(2,1)}, bf16[3,1536,256]{1,2,0:T(8,128)(2,1)}, u32[]{:S(2)}, u32[]{:S(2)}) %collective-permute-start.14) | collective-permute-done | bytes 2359328 | tf_op jit(solution)/shard_map/ppermute | solution.py:76
  130.9 5.6 collective-permute-done.1
  143.2 8.4 collective-permute-done.2
  160.0 41.8 %all-gather = bf16[16,96,16]{1,2,0:T(8,128)(2,1)S(1)} all-gather(bf16[1,96,16]{1,2,0:T(8,128)(2,1)S(1)} %bitcast.467), channel_id=1, replica_groups=mesh['dp'=16,'tensor'=2] {'dp'}, dimensions={0}, use_global_device_ids=true | all-gather | bytes 52224 | tf_op jit(solution)/shard_map/all_gather | solution.py:233
  214.0 7.7 pad_maximum_fusion.2
  230.2 3.8 gather_fusion.1
  234.0 13.5 %collective-permute-done.4 = bf16[8,96,1280]{2,1,0:T(8,128)(2,1)} collective-permute-done((bf16[8,96,1280]{2,1,0:T(8,128)(2,1)}, bf16[8,96,1280]{2,1,0:T(8,128)(2,1)}, u32[]{:S(2)}, u32[]{:S(2)}) %collective-permute-start.4) | collective-permute-done | bytes 1966112 | tf_op jit(solution)/shard_map/ppermute | solution.py:88
  250.5 5.0 gather_fusion
  255.6 4.4 convolution_convert_fusion.2
  263.1 5.1 fusion.166
  280.9 13.3 %collective-permute-done.24 = bf16[4,3,96,128]{3,2,1,0:T(8,128)(2,1)S(1)} collective-permute-done((bf16[4,3,96,128]{3,2,1,0:T(8,128)(2,1)S(1)}, bf16[4,3,96,128]{3,2,1,0:T(8,128)(2,1)S(1)}, u32[]{:S(2)}, u32[]{:S(2)}) %collective-permute-start.24) | collective-permute-done | bytes 294944 | tf_op jit(solution)/shard_map/ppermute | solution.py:76
  310.2 7.8 collective-permute-done.19
  318.0 15.3 %collective-permute-done.18 = bf16[256,1536]{1,0:T(8,128)(2,1)} collective-permute-done((bf16[256,1536]{1,0:T(8,128)(2,1)S(1)}, bf16[256,1536]{1,0:T(8,128)(2,1)}, u32[]{:S(2)}, u32[]{:S(2)}) %collective-permute-start.18) | collective-permute-done | bytes 786464 | tf_op jit(solution)/shard_map/ppermute | solution.py:76
  337.2 3.9 fusion.167
  343.2 4.0 fusion.57
  349.8 4.1 convert_bitcast_fusion.1
  358.7 14.0 %fusion.33 = f32[4,2,512,512]{2,3,1,0:T(8,128)} fusion(bf16[4,512,1536,1]{2,1,3,0:T(8,128)(2,1)} %bitcast.412, bf16[4,3,1536,256]{2,3,1,0:T(8,128)(2,1)} %collective-permute-done.16, bf16[1,3,1536,256]{2,3,1,0:T(8,128)(2,1)} %bitcast.24, bf16[1,3,1536,256]{2,3,1,0:T(8,128)(2,1)} %bitcast.23, bf16[1,3,1536,256]{2,3,1,0:T(8,128)(2,1)} %bitcast.22, ...), kind=kOutput, calls=%fused_computation.74 | convolution fusion | flops 6536822784 | bytes 33554432 | tf_op jit(solution)/shard_map/jrd,jcdf->jcrf/dot_general | solution.py:32
  372.7 4.7 multiply_multiply_fusion
  377.4 7.5 maximum_bitcast_fusion
  385.0 6.8 multiply_convert_fusion
  400.0 32.1 %collective-permute-done.27 = bf16[256,1536]{1,0:T(8,128)(2,1)S(1)} collective-permute-done((bf16[256,1536]{1,0:T(8,128)(2,1)S(1)}, bf16[256,1536]{1,0:T(8,128)(2,1)S(1)}, u32[]{:S(2)}, u32[]{:S(2)}) %collective-permute-start.27) | collective-permute-done | bytes 786464 | tf_op jit(solution)/shard_map/ppermute | solution.py:76
  441.2 16.7 %collective-permute-done.32 = bf16[256,1536]{1,0:T(8,128)(2,1)} collective-permute-done((bf16[256,1536]{1,0:T(8,128)(2,1)}, bf16[256,1536]{1,0:T(8,128)(2,1)}, u32[]{:S(2)}, u32[]{:S(2)}) %collective-permute-start.32) | collective-permute-done | bytes 786464 | tf_op jit(solution)/shard_map/ppermute | solution.py:76
  457.9 14.0 %collective-permute-done.31 = bf16[256,1536]{1,0:T(8,128)(2,1)} collective-permute-done((bf16[256,1536]{1,0:T(8,128)(2,1)}, bf16[256,1536]{1,0:T(8,128)(2,1)}, u32[]{:S(2)}, u32[]{:S(2)}) %collective-permute-start.31) | collective-permute-done | bytes 786464 | tf_op jit(solution)/shard_map/ppermute | solution.py:76
  475.7 5.8 convert_bitcast_fusion
  485.5 10.4 %fusion.54 = (bf16[4,1,512,512]{2,3,0,1:T(8,128)(2,1)S(1)}, bf16[4,1,512,512]{2,3,0,1:T(8,128)(2,1)}, f32[4,512]{1,0:T(4,128)S(1)}) fusion(f32[4,2,512,512]{2,3,1,0:T(8,128)} %fusion.33, f32[4,512]{1,0:T(4,128)S(1)} %bitcast.455, f32[4,512,512]{1,2,0:T(8,128)S(1)} %copy-done.8, bf16[4,512,1536]{2,1,0:T(8,128)(2,1)S(1)} %bitcast.406, ...), kind=kOutput, calls=%fused_computation.109 | convolution fusion | flops 3240097792 | bytes 29376512 | tf_op jit(solution)/shard_map/jrd,jdf->jrf/dot_general | solution.py:32
  495.8 6.4 convolution_bitcast_fusion.1
  502.3 14.8 %convolution_bitcast_fusion = f32[4,2,1536,512]{2,3,1,0:T(8,128)} fusion(bf16[4,512,1536,1]{2,1,3,0:T(8,128)(2,1)} %bitcast.413, bf16[4,1,512,512]{2,3,0,1:T(8,128)(2,1)} %get-tuple-element.97, bf16[4,1,512,512]{2,3,0,1:T(8,128)(2,1)S(1)} %get-tuple-element.96), kind=kOutput, calls=%fused_computation.26 | convolution fusion | flops 6444548096 | bytes 35651584 | tf_op jit(solution)/shard_map/jrd,jcrf->jcdf/dot_general | solution.py:32
  517.1 13.1 %bitcast_convert_fusion = bf16[4,512,1536]{2,1,0:T(8,128)(2,1)} fusion(bf16[4,1,512,512]{2,3,0,1:T(8,128)(2,1)} %get-tuple-element.97, bf16[4,1,512,512]{2,3,0,1:T(8,128)(2,1)} %copy-done.84, bf16[4,3,1536,256]{2,3,1,0:T(8,128)(2,1)} %collective-permute-done.16, bf16[1,3,1536,256]{2,3,1,0:T(8,128)(2,1)} %bitcast.24, bf16[1,3,1536,256]{2,3,1,0:T(8,128)(2,1)} %bitcast.23, ...), kind=kOutput, calls=%fused_computation.28 | convolution fusion | flops 6510608384 | bytes 29360128 | tf_op jit(solution)/shard_map/jcrf,jcdf->jrd/dot_general | solution.py:32
  530.1 7.2 fusion.21
  539.9 4.1 fusion.111
  554.1 6.5 concatenate.77
  567.4 10.0 fusion.4
  578.0 23.8 %collective-permute-done.33 = bf16[256,1664]{1,0:T(8,128)(2,1)S(1)} collective-permute-done((bf16[256,1664]{1,0:T(8,128)(2,1)S(1)}, bf16[256,1664]{1,0:T(8,128)(2,1)S(1)}, u32[]{:S(2)}, u32[]{:S(2)}) %collective-permute-start.33) | collective-permute-done | bytes 852000 | tf_op jit(solution)/shard_map/ppermute | solution.py:76
  615.9 118.2 %reduce-scatter.4.cloned.1.call-done = f32[96,16]{1,0:T(8,128)} async-done(((f32[1536,16]{1,0:T(8,128)}), f32[96,16]{1,0:T(8,128)}) %reduce-scatter.4.cloned.1.call-update) | async-done | bytes 6160
  743.1 4.7 convolution_convert_fusion.1
  754.5 3.9 fusion.17
  765.1 4.4 convolution_convert_fusion
  769.5 4.1 gather_fusion.4
  777.9 5.2 fusion.108
  787.0 35.8 %collective-permute-done.56 = bf16[3,96,128]{2,1,0:T(8,128)(2,1)S(1)} collective-permute-done((bf16[3,96,128]{2,1,0:T(8,128)(2,1)S(1)}, bf16[3,96,128]{2,1,0:T(8,128)(2,1)S(1)}, u32[]{:S(2)}, u32[]{:S(2)}) %collective-permute-start.56) | collective-permute-done | bytes 73760 | tf_op jit(solution)/shard_map/ppermute | solution.py:76
  837.0 13.3 %fusion.158 = (bf16[4,3,1536,256]{2,3,1,0:T(8,128)(2,1)}, f32[4,3,1536,256]{2,3,1,0:T(8,128)S(1)}) fusion(bf16[4,3,1536,256]{2,3,1,0:T(8,128)(2,1)} %collective-permute-done.59, f32[4,1,1536,512]{2,3,1,0:T(8,128)S(1)} %bitcast.402, f32[4,2,1536,512]{2,3,1,0:T(8,128)} %convolution_bitcast_fusion), kind=kLoop, calls=%fused_computation.345 | loop fusion | flops 18874368 | bytes 75497472 | tf_op jit(solution)/shard_map/convert.5
  850.3 7.8 slice_bitcast_fusion.6
  873.4 43.3 %collective-permute-done.44 = bf16[4,96,1280]{2,1,0:T(8,128)(2,1)S(1)} collective-permute-done((bf16[4,96,1280]{2,1,0:T(8,128)(2,1)S(1)}, bf16[4,96,1280]{2,1,0:T(8,128)(2,1)S(1)}, u32[]{:S(2)}, u32[]{:S(2)}) %collective-permute-start.44) | collective-permute-done | bytes 983072 | tf_op jit(solution)/shard_map/ppermute | solution.py:88
  921.2 4.0 fusion.29
  931.0 4.2 collective-permute-done.45
  939.5 61.4 %collective-permute-done.50 = bf16[1,96,768]{2,1,0:T(8,128)(2,1)} collective-permute-done((bf16[1,96,768]{2,1,0:T(8,128)(2,1)S(1)}, bf16[1,96,768]{2,1,0:T(8,128)(2,1)}, u32[]{:S(2)}, u32[]{:S(2)}) %collective-permute-start.50) | collective-permute-done | bytes 147488 | tf_op jit(solution)/shard_map/ppermute | solution.py:88
  1006.0 4.0 fusion.31
  (470 shorter events, 249.1 us)
Async XLA Ops:
  7.2 726.9 %reduce-scatter.4.cloned.1.call-start = ((), (), s32[]{:S(2)}) async-start(), calls=%async_computation.1 | async-start | bytes 835584
  13.6 115.4 %collective-permute-start.14 = (bf16[3,1536,256]{1,2,0:T(8,128)(2,1)}, bf16[3,1536,256]{1,2,0:T(8,128)(2,1)}, u32[]{:S(2)}, u32[]{:S(2)}) collective-permute-start(bf16[3,1536,256]{1,2,0:T(8,128)(2,1)} %get-tuple-element.110), channel_id=1, source_target_pairs={{0,16},{2,18},{4,20},{6,22},{8,24},{10,26},{12,28},{14,30},{16,0},... | collective-permute-start | bytes 7077896 | tf_op jit(solution)/shard_map/ppermute | solution.py:76
  17.6 194.4 %collective-permute-start.13 = (bf16[3,1536,256]{1,2,0:T(8,128)(2,1)}, bf16[3,1536,256]{1,2,0:T(8,128)(2,1)}, u32[]{:S(2)}, u32[]{:S(2)}) collective-permute-start(bf16[3,1536,256]{1,2,0:T(8,128)(2,1)} %get-tuple-element.110), channel_id=1, source_target_pairs={{0,4},{2,6},{4,0},{6,2},{8,12},{10,14},{12,8},{14,10},{16,20},{18,... | collective-permute-start | bytes 7077896 | tf_op jit(solution)/shard_map/ppermute | solution.py:76
  19.7 258.5 %collective-permute-start.11 = (s32[256,6]{0,1:T(8,128)}, s32[256,6]{0,1:T(8,128)}, u32[]{:S(2)}, u32[]{:S(2)}) collective-permute-start(s32[256,6]{0,1:T(8,128)} %constant_dynamic-slice_fusion), channel_id=1, source_target_pairs={{0,8},{2,10},{4,12},{6,14},{8,0},{10,2},{12,4},{14,6},{16,24},{18,... | collective-permute-start | bytes 18440 | tf_op jit(solution)/shard_map/ppermute | solution.py:76
  21.3 119.6 %collective-permute-start.5 = (bf16[1,96,768]{2,1,0:T(8,128)(2,1)S(1)}, bf16[1,96,768]{2,1,0:T(8,128)(2,1)}, u32[]{:S(2)}, u32[]{:S(2)}) collective-permute-start(bf16[1,96,768]{2,1,0:T(8,128)(2,1)S(1)} %bitcast.433), channel_id=1, source_target_pairs={{0,16},{1,17},{2,18},{3,19},{4,20},{5,21},{6,22},{7,23},{8,24},{9,... | collective-permute-start | bytes 442376 | tf_op jit(solution)/shard_map/ppermute | solution.py:88
  22.6 113.9 %collective-permute-start.1 = (bf16[1,96,1280]{2,1,0:T(8,128)(2,1)S(1)}, bf16[1,96,1280]{2,1,0:T(8,128)(2,1)S(1)}, u32[]{:S(2)}, u32[]{:S(2)}) collective-permute-start(bf16[1,96,1280]{2,1,0:T(8,128)(2,1)S(1)} %maximum_bitcast_fusion.1), channel_id=1, source_target_pairs={{0,16},{1,17},{2,18},{3,19},{4,20},{5,21},{6,22},{7,23},{8,24},{9,... | collective-permute-start | bytes 737288 | tf_op jit(solution)/shard_map/ppermute | solution.py:88
  129.0 85.0 %collective-permute-start.15 = (bf16[3,1536,256]{1,2,0:T(8,128)(2,1)}, bf16[3,1536,256]{1,2,0:T(8,128)(2,1)}, u32[]{:S(2)}, u32[]{:S(2)}) collective-permute-start(bf16[3,1536,256]{1,2,0:T(8,128)(2,1)} %collective-permute-done.14), channel_id=1, source_target_pairs={{0,4},{2,6},{4,0},{6,2},{8,12},{10,14},{12,8},{14,10},{16,20},{18,... | collective-permute-start | bytes 7077896 | tf_op jit(solution)/shard_map/ppermute | solution.py:76
  152.7 56.5 %collective-permute-start.3 = (bf16[4,96,1280]{2,1,0:T(8,128)(2,1)}, bf16[4,96,1280]{2,1,0:T(8,128)(2,1)}, u32[]{:S(2)}, u32[]{:S(2)}) collective-permute-start(bf16[4,96,1280]{2,1,0:T(8,128)(2,1)} %pad_maximum_fusion.16), channel_id=1, source_target_pairs={{0,4},{1,3},{2,6},{3,1},{4,0},{5,7},{6,2},{7,5},{8,12},{9,11},{10,... | collective-permute-start | bytes 2949128 | tf_op jit(solution)/shard_map/ppermute | solution.py:88
  158.7 49.2 %collective-permute-start.7 = (bf16[4,96,768]{2,1,0:T(8,128)(2,1)}, bf16[4,96,768]{2,1,0:T(8,128)(2,1)}, u32[]{:S(2)}, u32[]{:S(2)}) collective-permute-start(bf16[4,96,768]{2,1,0:T(8,128)(2,1)} %pad_maximum_fusion.20), channel_id=1, source_target_pairs={{0,4},{1,3},{2,6},{3,1},{4,0},{5,7},{6,2},{7,5},{8,12},{9,11},{10,... | collective-permute-start | bytes 1769480 | tf_op jit(solution)/shard_map/ppermute | solution.py:88
  209.2 19.9 %collective-permute-start.8 = (bf16[8,96,768]{2,1,0:T(8,128)(2,1)S(1)}, bf16[8,96,768]{2,1,0:T(8,128)(2,1)S(1)}, u32[]{:S(2)}, u32[]{:S(2)}) collective-permute-start(bf16[8,96,768]{2,1,0:T(8,128)(2,1)S(1)} %pad_maximum_fusion.11), channel_id=1, source_target_pairs={{0,2},{1,5},{2,0},{3,7},{4,6},{5,1},{6,4},{7,3},{8,10},{9,13},{10,... | collective-permute-start | bytes 3538952 | tf_op jit(solution)/shard_map/ppermute | solution.py:88
  212.0 35.5 %collective-permute-start.4 = (bf16[8,96,1280]{2,1,0:T(8,128)(2,1)}, bf16[8,96,1280]{2,1,0:T(8,128)(2,1)}, u32[]{:S(2)}, u32[]{:S(2)}) collective-permute-start(bf16[8,96,1280]{2,1,0:T(8,128)(2,1)} %pad_maximum_fusion.8), channel_id=1, source_target_pairs={{0,2},{1,5},{2,0},{3,7},{4,6},{5,1},{6,4},{7,3},{8,10},{9,13},{10,... | collective-permute-start | bytes 5898248 | tf_op jit(solution)/shard_map/ppermute | solution.py:88
  221.7 137.0 %collective-permute-start.16 = (bf16[4,3,1536,256]{2,3,1,0:T(8,128)(2,1)}, bf16[4,3,1536,256]{2,3,1,0:T(8,128)(2,1)}, u32[]{:S(2)}, u32[]{:S(2)}) collective-permute-start(bf16[4,3,1536,256]{2,3,1,0:T(8,128)(2,1)} %pad_maximum_fusion.2), channel_id=1, source_target_pairs={{0,1},{1,0},{2,3},{3,2},{4,5},{5,4},{6,7},{7,6},{8,9},{9,8},{10,11... | collective-permute-start | bytes 28311560 | tf_op jit(solution)/shard_map/ppermute | solution.py:79
  224.0 49.4 %collective-permute-start.20 = (bf16[3,96,128]{2,1,0:T(8,128)(2,1)}, bf16[3,96,128]{2,1,0:T(8,128)(2,1)}, u32[]{:S(2)}, u32[]{:S(2)}) collective-permute-start(bf16[3,96,128]{2,1,0:T(8,128)(2,1)} %get-tuple-element.124), channel_id=1, source_target_pairs={{0,2},{2,0},{4,6},{6,4},{8,10},{10,8},{12,14},{14,12},{16,18},{18,... | collective-permute-start | bytes 221192 | tf_op jit(solution)/shard_map/ppermute | solution.py:76
  229.1 45.2 %collective-permute-start.21 = (bf16[3,96,128]{2,1,0:T(8,128)(2,1)}, bf16[3,96,128]{2,1,0:T(8,128)(2,1)}, u32[]{:S(2)}, u32[]{:S(2)}) collective-permute-start(bf16[3,96,128]{2,1,0:T(8,128)(2,1)} %get-tuple-element.125), channel_id=1, source_target_pairs={{0,8},{2,10},{4,12},{6,14},{8,0},{10,2},{12,4},{14,6},{16,24},{18,... | collective-permute-start | bytes 221192 | tf_op jit(solution)/shard_map/ppermute | solution.py:76
  247.5 29.7 %collective-permute-start.22 = (bf16[3,96,128]{2,1,0:T(8,128)(2,1)S(1)}, bf16[3,96,128]{2,1,0:T(8,128)(2,1)}, u32[]{:S(2)}, u32[]{:S(2)}) collective-permute-start(bf16[3,96,128]{2,1,0:T(8,128)(2,1)S(1)} %copy-done.64), channel_id=1, source_target_pairs={{0,10},{2,8},{4,14},{6,12},{8,2},{10,0},{12,6},{14,4},{16,26},{18,... | collective-permute-start | bytes 221192 | tf_op jit(solution)/shard_map/ppermute | solution.py:76
  296.5 21.5 %collective-permute-start.19 = (bf16[256,1536]{1,0:T(8,128)(2,1)S(1)}, bf16[256,1536]{1,0:T(8,128)(2,1)}, u32[]{:S(2)}, u32[]{:S(2)}) collective-permute-start(bf16[256,1536]{1,0:T(8,128)(2,1)S(1)} %multiply_convert_fusion.7), channel_id=1, source_target_pairs={{0,10},{2,8},{4,14},{6,12},{8,2},{10,0},{12,6},{14,4},{16,26},{18,... | collective-permute-start | bytes 2359304 | tf_op jit(solution)/shard_map/ppermute | solution.py:76
  296.6 36.7 %collective-permute-start.18 = (bf16[256,1536]{1,0:T(8,128)(2,1)S(1)}, bf16[256,1536]{1,0:T(8,128)(2,1)}, u32[]{:S(2)}, u32[]{:S(2)}) collective-permute-start(bf16[256,1536]{1,0:T(8,128)(2,1)S(1)} %multiply_convert_fusion.7), channel_id=1, source_target_pairs={{0,8},{2,10},{4,12},{6,14},{8,0},{10,2},{12,4},{14,6},{16,24},{18,... | collective-permute-start | bytes 2359304 | tf_op jit(solution)/shard_map/ppermute | solution.py:76
  298.8 35.1 %collective-permute-start.17 = (bf16[256,1536]{1,0:T(8,128)(2,1)S(1)}, bf16[256,1536]{1,0:T(8,128)(2,1)}, u32[]{:S(2)}, u32[]{:S(2)}) collective-permute-start(bf16[256,1536]{1,0:T(8,128)(2,1)S(1)} %multiply_convert_fusion.7), channel_id=1, source_target_pairs={{0,2},{2,0},{4,6},{6,4},{8,10},{10,8},{12,14},{14,12},{16,18},{18,... | collective-permute-start | bytes 2359304 | tf_op jit(solution)/shard_map/ppermute | solution.py:76
  309.2 33.4 %collective-permute-start.26 = (bf16[3,1536,128]{1,2,0:T(8,128)(2,1)S(1)}, bf16[3,1536,128]{1,2,0:T(8,128)(2,1)}, u32[]{:S(2)}, u32[]{:S(2)}) collective-permute-start(bf16[3,1536,128]{1,2,0:T(8,128)(2,1)S(1)} %copy.253), channel_id=1, source_target_pairs={{0,1},{1,0},{2,3},{3,2},{4,5},{5,4},{6,7},{7,6},{8,9},{9,8},{10,11... | collective-permute-start | bytes 3538952 | tf_op jit(solution)/shard_map/ppermute | solution.py:79
  395.8 36.3 %collective-permute-start.27 = (bf16[256,1536]{1,0:T(8,128)(2,1)S(1)}, bf16[256,1536]{1,0:T(8,128)(2,1)S(1)}, u32[]{:S(2)}, u32[]{:S(2)}) collective-permute-start(bf16[256,1536]{1,0:T(8,128)(2,1)S(1)} %get-tuple-element.106), channel_id=1, source_target_pairs={{0,2},{2,0},{4,6},{6,4},{8,10},{10,8},{12,14},{14,12},{16,18},{18,... | collective-permute-start | bytes 2359304 | tf_op jit(solution)/shard_map/ppermute | solution.py:76
  396.7 35.4 %collective-permute-start.29 = (bf16[256,1536]{1,0:T(8,128)(2,1)S(1)}, bf16[256,1536]{1,0:T(8,128)(2,1)S(1)}, u32[]{:S(2)}, u32[]{:S(2)}) collective-permute-start(bf16[256,1536]{1,0:T(8,128)(2,1)S(1)} %get-tuple-element.107), channel_id=1, source_target_pairs={{0,10},{2,8},{4,14},{6,12},{8,2},{10,0},{12,6},{14,4},{16,26},{18,... | collective-permute-start | bytes 2359304 | tf_op jit(solution)/shard_map/ppermute | solution.py:76
  397.0 36.4 %collective-permute-start.28 = (bf16[256,1536]{1,0:T(8,128)(2,1)S(1)}, bf16[256,1536]{1,0:T(8,128)(2,1)S(1)}, u32[]{:S(2)}, u32[]{:S(2)}) collective-permute-start(bf16[256,1536]{1,0:T(8,128)(2,1)S(1)} %get-tuple-element.108), channel_id=1, source_target_pairs={{0,8},{2,10},{4,12},{6,14},{8,0},{10,2},{12,4},{14,6},{16,24},{18,... | collective-permute-start | bytes 2359304 | tf_op jit(solution)/shard_map/ppermute | solution.py:76
  436.2 21.7 %collective-permute-start.32 = (bf16[256,1536]{1,0:T(8,128)(2,1)}, bf16[256,1536]{1,0:T(8,128)(2,1)}, u32[]{:S(2)}, u32[]{:S(2)}) collective-permute-start(bf16[256,1536]{1,0:T(8,128)(2,1)} %fusion.156), channel_id=1, source_target_pairs={{0,10},{2,8},{4,14},{6,12},{8,2},{10,0},{12,6},{14,4},{16,26},{18,... | collective-permute-start | bytes 2359304 | tf_op jit(solution)/shard_map/ppermute | solution.py:76
  436.4 35.4 %collective-permute-start.31 = (bf16[256,1536]{1,0:T(8,128)(2,1)}, bf16[256,1536]{1,0:T(8,128)(2,1)}, u32[]{:S(2)}, u32[]{:S(2)}) collective-permute-start(bf16[256,1536]{1,0:T(8,128)(2,1)} %fusion.156), channel_id=1, source_target_pairs={{0,8},{2,10},{4,12},{6,14},{8,0},{10,2},{12,4},{14,6},{16,24},{18,... | collective-permute-start | bytes 2359304 | tf_op jit(solution)/shard_map/ppermute | solution.py:76
  438.4 34.1 %collective-permute-start.30 = (bf16[256,1536]{1,0:T(8,128)(2,1)}, bf16[256,1536]{1,0:T(8,128)(2,1)}, u32[]{:S(2)}, u32[]{:S(2)}) collective-permute-start(bf16[256,1536]{1,0:T(8,128)(2,1)} %fusion.156), channel_id=1, source_target_pairs={{0,2},{2,0},{4,6},{6,4},{8,10},{10,8},{12,14},{14,12},{16,18},{18,... | collective-permute-start | bytes 2359304 | tf_op jit(solution)/shard_map/ppermute | solution.py:76
  562.6 39.2 %collective-permute-start.33 = (bf16[256,1664]{1,0:T(8,128)(2,1)S(1)}, bf16[256,1664]{1,0:T(8,128)(2,1)S(1)}, u32[]{:S(2)}, u32[]{:S(2)}) collective-permute-start(bf16[256,1664]{1,0:T(8,128)(2,1)S(1)} %get-tuple-element.101), channel_id=1, source_target_pairs={{0,2},{2,0},{4,6},{6,4},{8,10},{10,8},{12,14},{14,12},{16,18},{18,... | collective-permute-start | bytes 2555912 | tf_op jit(solution)/shard_map/ppermute | solution.py:76
  563.5 38.3 %collective-permute-start.35 = (bf16[256,1664]{1,0:T(8,128)(2,1)S(1)}, bf16[256,1664]{1,0:T(8,128)(2,1)S(1)}, u32[]{:S(2)}, u32[]{:S(2)}) collective-permute-start(bf16[256,1664]{1,0:T(8,128)(2,1)S(1)} %get-tuple-element.102), channel_id=1, source_target_pairs={{0,10},{2,8},{4,14},{6,12},{8,2},{10,0},{12,6},{14,4},{16,26},{18,... | collective-permute-start | bytes 2555912 | tf_op jit(solution)/shard_map/ppermute | solution.py:76
  563.8 39.3 %collective-permute-start.34 = (bf16[256,1664]{1,0:T(8,128)(2,1)S(1)}, bf16[256,1664]{1,0:T(8,128)(2,1)S(1)}, u32[]{:S(2)}, u32[]{:S(2)}) collective-permute-start(bf16[256,1664]{1,0:T(8,128)(2,1)S(1)} %get-tuple-element.103), channel_id=1, source_target_pairs={{0,8},{2,10},{4,12},{6,14},{8,0},{10,2},{12,4},{14,6},{16,24},{18,... | collective-permute-start | bytes 2555912 | tf_op jit(solution)/shard_map/ppermute | solution.py:76
  567.3 41.5 %collective-permute-start.52 = (bf16[3,1536,128]{1,2,0:T(8,128)(2,1)S(1)}, bf16[3,1536,128]{1,2,0:T(8,128)(2,1)S(1)}, u32[]{:S(2)}, u32[]{:S(2)}) collective-permute-start(bf16[3,1536,128]{1,2,0:T(8,128)(2,1)S(1)} %fusion.44), channel_id=1, source_target_pairs={{0,1},{1,0},{2,3},{3,2},{4,5},{5,4},{6,7},{7,6},{8,9},{9,8},{10,11... | collective-permute-start | bytes 3538952 | tf_op jit(solution)/shard_map/ppermute | solution.py:79
  577.4 259.5 %collective-permute-start.59 = (bf16[4,3,1536,256]{2,3,1,0:T(8,128)(2,1)}, bf16[4,3,1536,256]{2,3,1,0:T(8,128)(2,1)}, u32[]{:S(2)}, u32[]{:S(2)}) collective-permute-start(bf16[4,3,1536,256]{2,3,1,0:T(8,128)(2,1)} %fusion.4), channel_id=1, source_target_pairs={{0,1},{1,0},{2,3},{3,2},{4,5},{5,4},{6,7},{7,6},{8,9},{9,8},{10,11... | collective-permute-start | bytes 28311560 | tf_op jit(solution)/shard_map/ppermute | solution.py:79
  608.8 130.5 %collective-permute-start.36 = (bf16[256,1536]{1,0:T(8,128)(2,1)}, bf16[256,1536]{1,0:T(8,128)(2,1)}, u32[]{:S(2)}, u32[]{:S(2)}) collective-permute-start(bf16[256,1536]{1,0:T(8,128)(2,1)} %get-tuple-element.90), channel_id=1, source_target_pairs={{0,1},{1,0},{2,3},{3,2},{4,5},{5,4},{6,7},{7,6},{8,9},{9,8},{10,11... | collective-permute-start | bytes 2359304 | tf_op jit(solution)/shard_map/ppermute | solution.py:79
  611.9 125.1 %collective-permute-start.54 = (bf16[4,3,96,128]{3,2,1,0:T(8,128)(2,1)S(1)}, bf16[4,3,96,128]{3,2,1,0:T(8,128)(2,1)S(1)}, u32[]{:S(2)}, u32[]{:S(2)}) collective-permute-start(bf16[4,3,96,128]{3,2,1,0:T(8,128)(2,1)S(1)} %get-tuple-element.115), channel_id=1, source_target_pairs={{0,4},{2,6},{4,0},{6,2},{8,12},{10,14},{12,8},{14,10},{16,20},{18,... | collective-permute-start | bytes 884744 | tf_op jit(solution)/shard_map/ppermute | solution.py:76
  735.6 47.7 %collective-permute-start.53 = (bf16[4,3,96,128]{3,2,1,0:T(8,128)(2,1)}, bf16[4,3,96,128]{3,2,1,0:T(8,128)(2,1)S(1)}, u32[]{:S(2)}, u32[]{:S(2)}) collective-permute-start(bf16[4,3,96,128]{3,2,1,0:T(8,128)(2,1)} %get-tuple-element.114), channel_id=1, source_target_pairs={{0,4},{2,6},{4,0},{6,2},{8,12},{10,14},{12,8},{14,10},{16,20},{18,... | collective-permute-start | bytes 884744 | tf_op jit(solution)/shard_map/ppermute | solution.py:76
  737.8 46.1 %collective-permute-start.55 = (bf16[4,3,96,128]{3,2,1,0:T(8,128)(2,1)}, bf16[4,3,96,128]{3,2,1,0:T(8,128)(2,1)}, u32[]{:S(2)}, u32[]{:S(2)}) collective-permute-start(bf16[4,3,96,128]{3,2,1,0:T(8,128)(2,1)} %fusion.106), channel_id=1, source_target_pairs={{0,16},{2,18},{4,20},{6,22},{8,24},{10,26},{12,28},{14,30},{16,0},... | collective-permute-start | bytes 884744 | tf_op jit(solution)/shard_map/ppermute | solution.py:76
  776.4 58.8 %collective-permute-start.47 = (bf16[8,96,768]{2,1,0:T(8,128)(2,1)}, bf16[8,96,768]{2,1,0:T(8,128)(2,1)S(1)}, u32[]{:S(2)}, u32[]{:S(2)}) collective-permute-start(bf16[8,96,768]{2,1,0:T(8,128)(2,1)} %gather_fusion.6), channel_id=1, source_target_pairs={{0,2},{1,5},{2,0},{3,7},{4,6},{5,1},{6,4},{7,3},{8,10},{9,13},{10,... | collective-permute-start | bytes 3538952 | tf_op jit(solution)/shard_map/ppermute | solution.py:88
  783.2 45.6 %collective-permute-start.37 = (bf16[256,1536]{1,0:T(8,128)(2,1)S(1)}, bf16[256,1536]{1,0:T(8,128)(2,1)S(1)}, u32[]{:S(2)}, u32[]{:S(2)}) collective-permute-start(bf16[256,1536]{1,0:T(8,128)(2,1)S(1)} %slice.552), channel_id=1, source_target_pairs={{0,1},{1,0},{2,3},{3,2},{4,5},{5,4},{6,7},{7,6},{8,9},{9,8},{10,11... | collective-permute-start | bytes 2359304 | tf_op jit(solution)/shard_map/ppermute | solution.py:79
  783.3 75.5 %collective-permute-start.43 = (bf16[8,96,1280]{2,1,0:T(8,128)(2,1)}, bf16[8,96,1280]{2,1,0:T(8,128)(2,1)}, u32[]{:S(2)}, u32[]{:S(2)}) collective-permute-start(bf16[8,96,1280]{2,1,0:T(8,128)(2,1)} %gather_fusion.4), channel_id=1, source_target_pairs={{0,2},{1,5},{2,0},{3,7},{4,6},{5,1},{6,4},{7,3},{8,10},{9,13},{10,... | collective-permute-start | bytes 5898248 | tf_op jit(solution)/shard_map/ppermute | solution.py:88
  786.3 36.6 %collective-permute-start.56 = (bf16[3,96,128]{2,1,0:T(8,128)(2,1)S(1)}, bf16[3,96,128]{2,1,0:T(8,128)(2,1)S(1)}, u32[]{:S(2)}, u32[]{:S(2)}) collective-permute-start(bf16[3,96,128]{2,1,0:T(8,128)(2,1)S(1)} %get-tuple-element.120), channel_id=1, source_target_pairs={{0,2},{2,0},{4,6},{6,4},{8,10},{10,8},{12,14},{14,12},{16,18},{18,... | collective-permute-start | bytes 221192 | tf_op jit(solution)/shard_map/ppermute | solution.py:76
  833.8 28.5 %collective-permute-start.39 = (f32[3,1536]{1,0:T(4,128)S(1)}, f32[3,1536]{1,0:T(4,128)S(1)}, u32[]{:S(2)}, u32[]{:S(2)}) collective-permute-start(f32[3,1536]{1,0:T(4,128)S(1)} %fusion.154), channel_id=1, source_target_pairs={{0,4},{2,6},{4,0},{6,2},{8,12},{10,14},{12,8},{14,10},{16,20},{18,... | collective-permute-start | bytes 55304 | tf_op jit(solution)/shard_map/ppermute | solution.py:76
  835.5 35.6 %collective-permute-start.48 = (bf16[4,96,768]{2,1,0:T(8,128)(2,1)S(1)}, bf16[4,96,768]{2,1,0:T(8,128)(2,1)}, u32[]{:S(2)}, u32[]{:S(2)}) collective-permute-start(bf16[4,96,768]{2,1,0:T(8,128)(2,1)S(1)} %slice.554), channel_id=1, source_target_pairs={{0,4},{1,3},{2,6},{3,1},{4,0},{5,7},{6,2},{7,5},{8,12},{9,11},{10,... | collective-permute-start | bytes 1769480 | tf_op jit(solution)/shard_map/ppermute | solution.py:88
  858.1 61.6 %collective-permute-start.61 = (bf16[3,1536,256]{1,2,0:T(8,128)(2,1)S(1)}, bf16[3,1536,256]{1,2,0:T(8,128)(2,1)S(1)}, u32[]{:S(2)}, u32[]{:S(2)}) collective-permute-start(bf16[3,1536,256]{1,2,0:T(8,128)(2,1)S(1)} %get-tuple-element.99), channel_id=1, source_target_pairs={{0,4},{2,6},{4,0},{6,2},{8,12},{10,14},{12,8},{14,10},{16,20},{18,... | collective-permute-start | bytes 7077896 | tf_op jit(solution)/shard_map/ppermute | solution.py:76
  861.1 55.5 %collective-permute-start.44 = (bf16[4,96,1280]{2,1,0:T(8,128)(2,1)S(1)}, bf16[4,96,1280]{2,1,0:T(8,128)(2,1)S(1)}, u32[]{:S(2)}, u32[]{:S(2)}) collective-permute-start(bf16[4,96,1280]{2,1,0:T(8,128)(2,1)S(1)} %slice.551), channel_id=1, source_target_pairs={{0,4},{1,3},{2,6},{3,1},{4,0},{5,7},{6,2},{7,5},{8,12},{9,11},{10,... | collective-permute-start | bytes 2949128 | tf_op jit(solution)/shard_map/ppermute | solution.py:88
  871.0 57.4 %collective-permute-start.42 = (f32[3,1536]{1,0:T(4,128)S(1)}, f32[3,1536]{1,0:T(4,128)S(1)}, u32[]{:S(2)}, u32[]{:S(2)}) collective-permute-start(f32[3,1536]{1,0:T(4,128)S(1)} %add.409), channel_id=1, source_target_pairs={{0,1},{1,0},{2,3},{3,2},{4,5},{5,4},{6,7},{7,6},{8,9},{9,8},{10,11... | collective-permute-start | bytes 55304 | tf_op jit(solution)/shard_map/ppermute | solution.py:79
  872.4 56.1 %collective-permute-start.49 = (bf16[2,96,768]{2,1,0:T(8,128)(2,1)S(1)}, bf16[2,96,768]{2,1,0:T(8,128)(2,1)}, u32[]{:S(2)}, u32[]{:S(2)}) collective-permute-start(bf16[2,96,768]{2,1,0:T(8,128)(2,1)S(1)} %slice.556), channel_id=1, source_target_pairs={{0,8},{1,9},{2,10},{3,11},{4,12},{5,13},{6,14},{7,15},{8,0},{9,1},... | collective-permute-start | bytes 884744 | tf_op jit(solution)/shard_map/ppermute | solution.py:88
  918.1 87.8 %collective-permute-start.60 = (bf16[3,1536,256]{1,2,0:T(8,128)(2,1)}, bf16[3,1536,256]{1,2,0:T(8,128)(2,1)S(1)}, u32[]{:S(2)}, u32[]{:S(2)}) collective-permute-start(bf16[3,1536,256]{1,2,0:T(8,128)(2,1)} %get-tuple-element.98), channel_id=1, source_target_pairs={{0,4},{2,6},{4,0},{6,2},{8,12},{10,14},{12,8},{14,10},{16,20},{18,... | collective-permute-start | bytes 7077896 | tf_op jit(solution)/shard_map/ppermute | solution.py:76
  925.3 80.7 %collective-permute-start.62 = (bf16[3,1536,256]{1,2,0:T(8,128)(2,1)}, bf16[3,1536,256]{1,2,0:T(8,128)(2,1)}, u32[]{:S(2)}, u32[]{:S(2)}) collective-permute-start(bf16[3,1536,256]{1,2,0:T(8,128)(2,1)} %fusion.29), channel_id=1, source_target_pairs={{0,16},{2,18},{4,20},{6,22},{8,24},{10,26},{12,28},{14,30},{16,0},... | collective-permute-start | bytes 7077896 | tf_op jit(solution)/shard_map/ppermute | solution.py:76
  929.5 71.4 %collective-permute-start.50 = (bf16[1,96,768]{2,1,0:T(8,128)(2,1)S(1)}, bf16[1,96,768]{2,1,0:T(8,128)(2,1)}, u32[]{:S(2)}, u32[]{:S(2)}) collective-permute-start(bf16[1,96,768]{2,1,0:T(8,128)(2,1)S(1)} %slice.558), channel_id=1, source_target_pairs={{0,16},{1,17},{2,18},{3,19},{4,20},{5,21},{6,22},{7,23},{8,24},{9,... | collective-permute-start | bytes 442376 | tf_op jit(solution)/shard_map/ppermute | solution.py:88
  937.1 66.4 %collective-permute-start.46 = (bf16[1,96,1280]{2,1,0:T(8,128)(2,1)}, bf16[1,96,1280]{2,1,0:T(8,128)(2,1)}, u32[]{:S(2)}, u32[]{:S(2)}) collective-permute-start(bf16[1,96,1280]{2,1,0:T(8,128)(2,1)} %slice.557), channel_id=1, source_target_pairs={{0,16},{1,17},{2,18},{3,19},{4,20},{5,21},{6,22},{7,23},{8,24},{9,... | collective-permute-start | bytes 737288 | tf_op jit(solution)/shard_map/ppermute | solution.py:88
  (108 other events, 1685.4 us)
Sparse Core Ops, SparseCore 0:
  615.3 118.8 reduce-scatter.3

commit v2 on v1

v2 whole, which is shorter than its diff:
```python
import jax
import jax.numpy as jnp
from jax import lax
from jax.experimental import pallas as pl
from jax.experimental.pallas import tpu as pltpu
from jax.sharding import PartitionSpec as P

HEAD_SIZE = 128
TOPK = 6

norm_eps = 1e-05
masked_score = -1e30
TAIL = 16
bf16 = jnp.bfloat16
f32 = jnp.float32


def product(left_side, right_side):
    return jnp.dot(left_side, right_side, preferred_element_type=f32)


def product_transposed(left_side, right_side):
    return lax.dot_general(
        left_side, right_side, (((1,), (1,)), ((), ())), preferred_element_type=f32
    )


def product_left(left_side, right_side):
    return lax.dot_general(
        left_side, right_side, (((0,), (0,)), ((), ())), preferred_element_type=f32
    )


def contract(spec, *operands):
    return jnp.einsum(spec, *operands, preferred_element_type=f32)


def normalize_rows(values, gain):
    row_scale = lax.rsqrt(jnp.mean(values * values, axis=-1, keepdims=True) + norm_eps)
    return ((values * row_scale * gain).astype(bf16), row_scale)


def normalize_back(values, row_scale, gain, grad_normed):
    scaled = grad_normed * gain
    inner_mean = jnp.mean(scaled * values, axis=-1, keepdims=True)
    grad_values = row_scale * (scaled - values * row_scale * row_scale * inner_mean)
    grad_gain = jnp.sum(grad_normed * values * row_scale, axis=0)
    return (grad_values, grad_gain)


def swish_back(pre_gate, pre_up, grad_act):
    logistic = jax.nn.sigmoid(pre_gate)
    grad_gate = grad_act * pre_up * logistic * (1.0 + pre_gate * (1.0 - logistic))
    grad_up = grad_act * pre_gate * logistic
    return grad_gate.astype(bf16), grad_up.astype(bf16)


def subset_masks(bits):
    masks = [0]
    for bit in bits:
        masks = masks + [mask | (1 << bit) for mask in masks]
    return masks


def behind(values, *others):
    return lax.optimization_barrier((values,) + others)[0]


class Tree:
    def __init__(self, lay, shard):
        self.lay, self.halves, self.marks = lay, (shard[None],), []

    def step(self, *others):
        held = jnp.concatenate(self.halves, axis=0)
        if others:
            held = behind(held, *others)
        self.marks.append(self.lay.shift_step(held, self.lay.steps[len(self.marks)]))
        self.halves = (held, self.marks[-1])
        return self.marks[-1]


class Sum:
    def __init__(self, lay, halves):
        self.lay, (self.keep, self.send), self.marks = lay, halves, []

    def step(self, *others):
        got = self.lay.shift(self.send, 1 << self.lay.back_bits[-1 - len(self.marks)])
        if others:
            got = behind(got, *others)
        self.marks.append(got)
        self.total = self.keep.astype(f32) + got.astype(f32)
        half = self.total.shape[0] // 2
        self.keep, self.send = self.total[:half], self.total[half:].astype(bf16)
        return got


class Layout:
    def __init__(self):
        self.dp = lax.axis_size("dp")
        self.tp = lax.axis_size("tensor")
        self.place = lax.axis_index("dp")
        self.core = lax.axis_index("tensor")
        bits = self.dp.bit_length() - 1
        self.w_bits = [bit for bit in (1, 3) if bit < bits]
        self.g_bits = [bit for bit in range(bits) if bit not in self.w_bits]
        self.w_masks = subset_masks(self.w_bits)
        self.g_masks = subset_masks(self.g_bits)
        self.steps = [(bit, bit) for bit in range(bits - 1, 1, -1)] + [(1, 0), (0, 1)]
        self.back_bits = list(range(bits - 1, -1, -1))

    def shift(self, values, mask):
        return lax.ppermute(values, "dp", [(i, i ^ mask) for i in range(self.dp)])

    def w_groups(self):
        groups = []
        for i in range(self.dp):
            if all(i & mask == 0 for mask in self.w_masks):
                places = sorted(i ^ mask for mask in self.w_masks)
                groups.append([place * self.tp + c for place in places for c in range(self.tp)])
        return groups

    def w_spots(self):
        bits = [(self.place >> bit) & 1 for bit in self.w_bits]
        rows = []
        for k in range(len(self.w_masks)):
            spot = sum((bit ^ ((k >> n) & 1)) << n for n, bit in enumerate(bits))
            rows.append(jnp.stack([spot * self.tp + (self.core ^ c) for c in range(self.tp)]))
        return jnp.stack(rows).astype(jnp.int32)

    def shift_core(self, values, mask):
        return lax.ppermute(values, "tensor", [(i, i ^ mask) for i in range(self.tp)])

    def shift_step(self, values, step):
        even, odd = step
        pairs = []
        for i in range(self.dp):
            for c in range(self.tp):
                target = i ^ (1 << (odd if c % 2 else even))
                pairs.append((i * self.tp + c, target * self.tp + c))
        return lax.ppermute(values, ("dp", "tensor"), pairs)

    def step_bit(self, step):
        even, odd = step
        return even if even == odd else jnp.where(self.core % 2 == 1, odd, even)

    def gather_order(self):
        apart = self.place ^ jnp.arange(self.dp)
        return sum(((apart >> self.step_bit(step)) & 1) << k for k, step in enumerate(self.steps))

    def scatter_order(self):
        apart = self.place ^ jnp.arange(self.dp)
        return sum(((apart >> bit) & 1) << k for k, bit in enumerate(self.back_bits))

    def in_order(self, halves):
        whole = jnp.concatenate(halves, axis=0)[self.gather_order()]
        return whole.reshape((-1,) + whole.shape[2:])

    def in_halves(self, whole):
        blocks = whole.astype(bf16).reshape((self.dp, -1) + whole.shape[1:])
        rel = jnp.arange(self.dp)
        apart = sum(((rel >> k) & 1) << bit for k, bit in enumerate(self.back_bits))
        at = self.place ^ apart
        return blocks[at[: self.dp // 2]], blocks[at[self.dp // 2 :]]

    def gather_g(self, values):
        return [values] + [self.shift(values, mask) for mask in self.g_masks[1:]]

    def scatter_w(self, blocks, after):
        near, far = (1 << bit for bit in self.w_bits)
        both = jnp.stack([blocks[3], blocks[1]]).astype(bf16)
        far_one, own = behind(self.shift(both, near), after)
        far_one = self.shift((blocks[2].astype(f32) + far_one.astype(f32)).astype(bf16), far)
        return blocks[0].astype(f32) + own.astype(f32) + far_one.astype(f32)

    def gather_core(self, values):
        return [values] + [self.shift_core(values, k) for k in range(1, self.tp)]

    def scatter_core(self, blocks):
        total = blocks[0].astype(f32)
        for k in range(1, self.tp):
            total = total + self.shift_core(blocks[k].astype(bf16), k).astype(f32)
        return total

    def sum_all(self, values, marks):
        for bit, mark in enumerate(marks):
            values = behind(values, mark)
            values = values + self.shift(values, 1 << bit)
        for bit in range(self.tp.bit_length() - 1):
            values = values + self.shift_core(values, 1 << bit)
        return values

    def chunk(self, mask):
        place = self.place ^ mask
        return sum(((place >> bit) & 1) << k for k, bit in enumerate(self.g_bits))

    def rows_order(self):
        apart = self.place ^ jnp.arange(self.dp)
        g = sum(((apart >> bit) & 1) << k for k, bit in enumerate(self.g_bits))
        w = sum(((apart >> bit) & 1) << k for k, bit in enumerate(self.w_bits))
        return g * len(self.w_masks) + w

    def rows_apart(self):
        masks = jnp.array([g | w for g in self.g_masks for w in self.w_masks], jnp.int32)
        return self.place ^ masks


def slots_of(position, capacity):
    slots = jnp.arange(capacity, dtype=f32)[:, None]
    return (position[:, :, None, :] == slots).astype(bf16)


def experts_forward_plain(position, gate, spots, capacity, tokens, shares, init):
    (held, groups, rows), width = position.shape, tokens.shape[1]
    taken = slots_of(position, capacity)
    work = contract("jgct,gtd->jgcd", taken, tokens.reshape(groups, rows, width)).astype(bf16)
    work = work.reshape(held, groups * capacity, width)
    scale = jnp.sum(taken.astype(f32) * gate[:, :, None, :], axis=-1).reshape(held, -1, 1)
    pre, made = [], 0.0
    for c in range(spots.shape[1]):
        weight = shares[spots[:, c]]
        pre.append(contract("jrd,jsdf->jsrf", work, weight[:, :2]))
        act = (jax.nn.silu(pre[-1][:, 0]) * pre[-1][:, 1]).astype(bf16)
        made = made + contract("jrf,jdf->jrd", act, weight[:, 2])
    made = (made * scale).astype(bf16).reshape(held, groups, capacity, width)
    total = init.reshape(groups, rows, width) + contract("jgct,jgcd->gtd", taken, made)
    return total.astype(bf16), work, jnp.stack(pre, axis=1)


def experts_backward_plain(position, gate, spots, capacity, tokens, work, pre, shares, init):
    (held, groups, rows), width = position.shape, tokens.shape[1]
    taken = slots_of(position, capacity)
    grad_rows = contract("jgct,gtd->jgcd", taken, tokens.reshape(groups, rows, width)).astype(bf16)
    grad_rows = grad_rows.reshape(held, groups * capacity, width)
    scale = jnp.sum(taken.astype(f32) * gate[:, :, None, :], axis=-1).reshape(held, -1, 1)
    chosen, made, grads = 0.0, 0.0, jnp.zeros(shares.shape, bf16)
    for c in range(spots.shape[1]):
        weight = shares[spots[:, c]]
        back = contract("jrd,jdf->jrf", grad_rows, weight[:, 2])
        activated = jax.nn.silu(pre[:, c, 0]) * pre[:, c, 1]
        chosen = chosen + jnp.sum(back * activated, axis=-1)
        grad_pre = jnp.stack(swish_back(pre[:, c, 0], pre[:, c, 1], back * scale), axis=1)
        made = made + contract("jsrf,jsdf->jrd", grad_pre, weight[:, :2])
        grad_in = contract("jrd,jsrf->jsdf", work, grad_pre).astype(bf16)
        grad_out = contract("jrd,jrf->jdf", grad_rows, (activated * scale).astype(bf16)).astype(bf16)
        grads = grads.at[spots[:, c]].set(jnp.concatenate([grad_in, grad_out[:, None]], axis=1))
    made = made.astype(bf16).reshape(held, groups, capacity, width)
    total = init.reshape(groups, rows, width) + contract("jgct,jgcd->gtd", taken, made)
    chosen = jnp.sum(taken.astype(f32) * chosen.reshape(held, groups, capacity, 1), axis=2)
    tail = chosen.transpose(1, 0, 2)
    high = tail.astype(bf16).astype(f32)
    tail = jnp.concatenate([high, tail - high], axis=1)
    tail = jnp.pad(tail, ((0, 0), (0, TAIL - tail.shape[1]), (0, width - rows)))
    return jnp.concatenate([total, tail], axis=1).astype(bf16), grads


def dot_rows(left, right):
    return lax.dot_general(left, right, (((0,), (0,)), ((), ())), preferred_element_type=f32)


def slot_matrix(position, capacity):
    slots = lax.broadcasted_iota(jnp.int32, (capacity, position.shape[1]), 0).astype(f32)
    return slots == position


def block_copies(order, whole, halves, sems, inward):
    blocks, rows = halves[0].shape[0], halves[0].shape[1]
    for i in range(2 * blocks):
        part = whole.at[pl.ds(i * rows, rows)]
        for k, half in enumerate(halves):

            @pl.when((order[i] >= k * blocks) & (order[i] < (k + 1) * blocks))
            def _():
                block = half.at[order[i] - k * blocks]
                source, target = (block, part) if inward else (part, block)
                pltpu.make_async_copy(source, target, sems.at[i]).start()


def block_waits(whole, halves, sems, inward):
    blocks, rows = halves[0].shape[0], halves[0].shape[1]
    for i in range(2 * blocks):
        part = whole.at[pl.ds(i * rows, rows)]
        source, target = (halves[0].at[0], part) if inward else (part, halves[0].at[0])
        pltpu.make_async_copy(source, target, sems.at[i]).wait()


def score_mask(core, length, rows):
    row = lax.broadcasted_iota(jnp.int32, (rows, rows), 0)
    col = lax.broadcasted_iota(jnp.int32, (rows, rows), 1)
    first = core * (rows // 2)
    row = jnp.where(row < rows // 2, row + first, row - first)
    col = jnp.where(col < rows // 2, col + first, col - first)
    return (col <= row) & (col < length)


anywhere = pl.BlockSpec(memory_space=pl.ANY)
scalars = pl.BlockSpec(memory_space=pltpu.SMEM)
in_vmem = pl.BlockSpec(memory_space=pltpu.VMEM)
no_cost = pl.CostEstimate(flops=0, transcendentals=0, bytes_accessed=0)
room = pltpu.CompilerParams(vmem_limit_bytes=56 * 1024 * 1024)


def attend(order, spot, own, other, gain, halves, head_count, kv_count):
    rows, width = own.shape
    total, columns = 2 * rows, halves[0].shape[2]
    group = head_count // kv_count

    def kernel(order, spot, own, other, gain, near, far, normed, made, mixed, logs, weight, sems):
        block_copies(order, weight, (near, far), sems, True)
        for k, part in enumerate((own, other)):
            values = part[...].astype(f32)
            scale = lax.rsqrt(jnp.mean(values * values, axis=1, keepdims=True) + norm_eps)
            normed[pl.ds(k * rows, rows), :] = (values * scale * gain[...]).astype(bf16)
        block_waits(weight, (near, far), sems, True)
        made[...] = product(normed[...], weight[...]).astype(bf16)
        allowed = score_mask(spot[0], spot[1], total)
        for h in range(head_count):
            key = pl.ds((head_count + h // group) * HEAD_SIZE, HEAD_SIZE)
            value = pl.ds((head_count + kv_count + h // group) * HEAD_SIZE, HEAD_SIZE)
            at = pl.ds(h * HEAD_SIZE, HEAD_SIZE)
            scores = product_transposed(made[:, at], made[:, key]) * HEAD_SIZE ** (-0.5)
            scores = jnp.where(allowed, scores, masked_score)
            most = jnp.max(scores, axis=1, keepdims=True)
            terms = jnp.exp(scores - most)
            together = jnp.sum(terms, axis=1, keepdims=True)
            probs = (terms * (1.0 / together)).astype(bf16)
            mixed[:, at] = product(probs, made[:, value]).astype(bf16)
            logs[h] = most + jnp.log(together)

    return pl.pallas_call(
        kernel,
        in_specs=[scalars, scalars, in_vmem, in_vmem, in_vmem, anywhere, anywhere],
        out_specs=[in_vmem] * 4,
        out_shape=[
            jax.ShapeDtypeStruct((total, width), bf16),
            jax.ShapeDtypeStruct((total, columns), bf16),
            jax.ShapeDtypeStruct((total, head_count * HEAD_SIZE), bf16),
            jax.ShapeDtypeStruct((head_count, total, 1), f32),
        ],
        scratch_shapes=[
            pltpu.VMEM((width, columns), bf16),
            pltpu.SemaphoreType.DMA((2 * halves[0].shape[0],)),
        ],
        compiler_params=room,
        cost_estimate=no_cost,
    )(order, spot, own, other, gain[None], *halves)


def project_out(order, mixed, halves):
    total, columns = mixed.shape
    width = 2 * halves[0].shape[0] * halves[0].shape[1]
    rows = total // 2

    def kernel(order, mixed, near, far, own, other, weight, sems):
        block_copies(order, weight, (near, far), sems, True)
        block_waits(weight, (near, far), sems, True)
        other[...] = product_transposed(mixed[pl.ds(rows, rows), :], weight[:, :columns]).astype(bf16)
        own[...] = product_transposed(mixed[pl.ds(0, rows), :], weight[:, :columns])

    return pl.pallas_call(
        kernel,
        in_specs=[scalars, in_vmem, anywhere, anywhere],
        out_specs=[in_vmem] * 3,
        out_shape=[
            jax.ShapeDtypeStruct((rows, width), f32),
            jax.ShapeDtypeStruct((rows, width), bf16),
            jax.ShapeDtypeStruct((width, halves[0].shape[2]), bf16),
        ],
        scratch_shapes=[pltpu.SemaphoreType.DMA((2 * halves[0].shape[0],))],
        compiler_params=room,
        cost_estimate=no_cost,
    )(order, mixed, *halves)


def half_shapes(places, width, columns):
    block = jax.ShapeDtypeStruct((places // 2, width // places, columns), bf16)
    return [block, block]


def project_out_back(order, own, other, weight, mixed, router):
    total, columns = mixed.shape
    rows, width = own.shape
    places = order.shape[0]

    def kernel(order, own, other, weight, mixed, router, grad_mixed, near, far, grads, both, sems):
        both[pl.ds(0, rows), :] = own[...]
        both[pl.ds(rows, rows), :] = other[...]
        grads[:, :columns] = dot_rows(both[...], mixed[...]).astype(bf16)
        grads[:, columns:] = router[...]
        block_copies(order, grads, (near, far), sems, False)
        grad_mixed[...] = product(both[...], weight[:, :columns]).astype(bf16)
        block_waits(grads, (near, far), sems, False)

    return pl.pallas_call(
        kernel,
        in_specs=[scalars] + [in_vmem] * 5,
        out_specs=[in_vmem, anywhere, anywhere],
        out_shape=[jax.ShapeDtypeStruct((total, columns), bf16)]
        + half_shapes(places, width, weight.shape[1]),
        scratch_shapes=[
            pltpu.VMEM(weight.shape, bf16),
            pltpu.VMEM((total, width), bf16),
            pltpu.SemaphoreType.DMA((places,)),
        ],
        compiler_params=room,
        cost_estimate=no_cost,
    )(order, own, other, weight, mixed, router)


def attend_back(order, spot, grad_mixed, normed, made, logs, head_count, kv_count):
    total, width = normed.shape
    columns, group = made.shape[1], head_count // kv_count
    places = order.shape[0]

    def kernel(order, spot, grad_mixed, normed, made, logs, grad_made, near, far, grads, sems):
        allowed = score_mask(spot[0], spot[1], total)
        for v in range(kv_count):
            key = pl.ds((head_count + v) * HEAD_SIZE, HEAD_SIZE)
            value = pl.ds((head_count + kv_count + v) * HEAD_SIZE, HEAD_SIZE)
            grad_key, grad_value = 0.0, 0.0
            for h in range(v * group, (v + 1) * group):
                at = pl.ds(h * HEAD_SIZE, HEAD_SIZE)
                scores = product_transposed(made[:, at], made[:, key]) * HEAD_SIZE ** (-0.5)
                probs = jnp.where(allowed, jnp.exp(scores - logs[h]), 0.0)
                grad_value = grad_value + dot_rows(probs.astype(bf16), grad_mixed[:, at])
                grad_probs = product_transposed(grad_mixed[:, at], made[:, value])
                delta = jnp.sum(probs * grad_probs, axis=1, keepdims=True)
                grad_scores = (probs * (grad_probs - delta)).astype(bf16)
                grad_query = product(grad_scores, made[:, key]) * HEAD_SIZE ** (-0.5)
                grad_made[:, at] = grad_query.astype(bf16)
                grad_key = grad_key + dot_rows(grad_scores, made[:, at]) * HEAD_SIZE ** (-0.5)
            grad_made[:, key] = grad_key.astype(bf16)
            grad_made[:, value] = grad_value.astype(bf16)
        grads[...] = dot_rows(normed[...], grad_made[...]).astype(bf16)
        block_copies(order, grads, (near, far), sems, False)
        block_waits(grads, (near, far), sems, False)

    return pl.pallas_call(
        kernel,
        in_specs=[scalars, scalars] + [in_vmem] * 4,
        out_specs=[in_vmem, anywhere, anywhere],
        out_shape=[jax.ShapeDtypeStruct((total, columns), bf16)]
        + half_shapes(places, width, columns),
        scratch_shapes=[
            pltpu.VMEM((width, columns), bf16),
            pltpu.SemaphoreType.DMA((places,)),
        ],
        compiler_params=room,
        cost_estimate=no_cost,
    )(order, spot, grad_mixed, normed, made, logs)


def normed_back(order, grad_made, halves):
    total, columns = grad_made.shape
    width = 2 * halves[0].shape[0] * halves[0].shape[1]
    rows = total // 2

    def kernel(order, grad_made, near, far, own, other, weight, sems):
        block_copies(order, weight, (near, far), sems, True)
        block_waits(weight, (near, far), sems, True)
        other[...] = product_transposed(grad_made[pl.ds(rows, rows), :], weight[...]).astype(bf16)
        own[...] = product_transposed(grad_made[pl.ds(0, rows), :], weight[...])

    return pl.pallas_call(
        kernel,
        in_specs=[scalars, in_vmem, anywhere, anywhere],
        out_specs=[in_vmem] * 2,
        out_shape=[
            jax.ShapeDtypeStruct((rows, width), f32),
            jax.ShapeDtypeStruct((rows, width), bf16),
        ],
        scratch_shapes=[
            pltpu.VMEM((width, columns), bf16),
            pltpu.SemaphoreType.DMA((2 * halves[0].shape[0],)),
        ],
        compiler_params=room,
        cost_estimate=no_cost,
    )(order, grad_made, *halves)


class Experts:
    def __init__(self, held, cores, groups, rows, capacity):
        self.held, self.cores, self.groups = held, cores, groups
        self.rows, self.capacity = rows, capacity

    def fetch(self, spots, shares, weight, sems, k):
        return [
            pltpu.make_async_copy(
                shares.at[spots[k, c]], weight.at[k % 2, c], sems.at[k % 2, c]
            )
            for c in range(self.cores)
        ]

    def weights_of(self, step, spots, shares, weight, sems):
        for k in range(self.held):

            @pl.when(step == k)
            def _():
                if k == 0:
                    for copy in self.fetch(spots, shares, weight, sems, 0):
                        copy.start()
                if k + 1 < self.held:
                    for copy in self.fetch(spots, shares, weight, sems, k + 1):
                        copy.start()

    def wait_weights(self, step, spots, shares, weight, sems):
        for k in range(self.held):

            @pl.when(step == k)
            def _():
                for copy in self.fetch(spots, shares, weight, sems, k):
                    copy.wait()

    def taken(self, position, k, g):
        return slot_matrix(position[k, g : g + 1, :], self.capacity)

    def dispatch(self, position, tokens, into):
        for g in range(self.groups):
            found = [self.taken(position, k, g).astype(bf16) for k in range(self.held)]
            found = jnp.concatenate(found, axis=0)
            found = product(found, tokens[pl.ds(g * self.rows, self.rows), :]).astype(bf16)
            for k in range(self.held):
                part = found[k * self.capacity : (k + 1) * self.capacity]
                into[k, pl.ds(g * self.capacity, self.capacity), :] = part

    def scales(self, position, gate, step):
        columns = []
        for g in range(self.groups):
            taken = slot_matrix(position[step, pl.ds(g, 1), :], self.capacity)
            gates = jnp.where(taken, gate[step, pl.ds(g, 1), :], 0.0)
            columns.append(jnp.sum(gates, axis=1, keepdims=True))
        return jnp.concatenate(columns, axis=0)

    def keep(self, made, step, into):
        for g in range(self.groups):
            part = made[g * self.capacity : (g + 1) * self.capacity]
            at = pl.ds(pl.multiple_of(step * self.capacity, self.capacity), self.capacity)
            into[g, at, :] = part

    def combine(self, position, made, init, slots, sems, write):
        def start(g):
            return pltpu.make_async_copy(init.at[g], slots.at[g % 2], sems.at[g % 2])

        start(0).start()
        for g in range(self.groups):
            if g + 1 < self.groups:
                start(g + 1).start()
            found = [self.taken(position, k, g).astype(bf16) for k in range(self.held)]
            found = dot_rows(jnp.concatenate(found, axis=0), made[g])
            start(g).wait()
            write(g, found + slots[g % 2])


def experts_forward(position, gate, spots, capacity, tokens, shares, init):
    (held, groups, rows), (_, _, width, hidden) = position.shape, shares.shape
    cores, slots = spots.shape[1], groups * capacity
    plan = Experts(held, cores, groups, rows, capacity)

    def kernel(spots, position, gate, tokens, shares, init, out, work, pre, weight, rows_all, made, sums, sems, sum_sems):
        step = pl.program_id(0)
        plan.weights_of(step, spots, shares, weight, sems)

        @pl.when(step == 0)
        def _():
            plan.dispatch(position, tokens, rows_all)

        plan.wait_weights(step, spots, shares, weight, sems)
        slot = lax.rem(step, 2)
        mine = rows_all[step]
        work[0] = mine
        produced = 0.0
        for c in range(cores):
            pre_gate = product(mine, weight[slot, c, 0])
            pre_up = product(mine, weight[slot, c, 1])
            pre[0, c, 0], pre[0, c, 1] = pre_gate, pre_up
            act = (pre_gate * (1.0 / (1.0 + jnp.exp(-pre_gate))) * pre_up).astype(bf16)
            produced = produced + product_transposed(act, weight[slot, c, 2])
        plan.keep((produced * plan.scales(position, gate, step)).astype(bf16), step, made)

        @pl.when(step == held - 1)
        def _():
            def write(g, total):
                out[g] = total.astype(bf16)

            plan.combine(position, made, init, sums, sum_sems, write)

    whole = pl.BlockSpec(position.shape, lambda j: (0, 0, 0))
    return pl.pallas_call(
        kernel,
        grid=(held,),
        in_specs=[
            scalars,
            whole,
            whole,
            pl.BlockSpec(tokens.shape, lambda j: (0, 0), pipeline_mode=pl.Buffered(1)),
            anywhere,
            anywhere,
        ],
        out_specs=[
            pl.BlockSpec((groups, rows, width), lambda j: (0, 0, 0)),
            pl.BlockSpec((1, slots, width), lambda j: (j, 0, 0)),
            pl.BlockSpec((1, cores, 2, slots, hidden), lambda j: (j, 0, 0, 0, 0)),
        ],
        out_shape=[
            jax.ShapeDtypeStruct((groups, rows, width), bf16),
            jax.ShapeDtypeStruct((held, slots, width), bf16),
            jax.ShapeDtypeStruct((held, cores, 2, slots, hidden), f32),
        ],
        scratch_shapes=[
            pltpu.VMEM((2, cores, 3, width, hidden), bf16),
            pltpu.VMEM((held, slots, width), bf16),
            pltpu.VMEM((groups, held * capacity, width), bf16),
            pltpu.VMEM((2, rows, width), f32),
            pltpu.SemaphoreType.DMA((2, cores)),
            pltpu.SemaphoreType.DMA((2,)),
        ],
        compiler_params=room,
        cost_estimate=no_cost,
    )(spots, position, gate, tokens, shares, init.reshape(groups, rows, width))


def experts_backward(position, gate, spots, capacity, tokens, work, pre, shares, init):
    (held, groups, rows), (_, _, width, hidden) = position.shape, shares.shape
    cores, slots = spots.shape[1], groups * capacity
    plan = Experts(held, cores, groups, rows, capacity)

    def kernel(
        spots, position, gate, tokens, work, pre, shares, init, out, grads, weight, rows_all, made, sums, fresh,
        found, sems, sum_sems, out_sems,
    ):
        step = pl.program_id(0)
        plan.weights_of(step, spots, shares, weight, sems)

        @pl.when(step == 0)
        def _():
            plan.dispatch(position, tokens, rows_all)

        plan.wait_weights(step, spots, shares, weight, sems)
        slot = lax.rem(step, 2)
        scale = plan.scales(position, gate, step)
        mine, produced, chosen, acts, pres = rows_all[step], 0.0, 0.0, [], []
        for c in range(cores):
            back = product(mine, weight[slot, c, 2])
            pre_gate, pre_up = pre[0, c, 0], pre[0, c, 1]
            logistic = 1.0 / (1.0 + jnp.exp(-pre_gate))
            activated = pre_gate * logistic * pre_up
            chosen = chosen + jnp.sum(back * activated, axis=1, keepdims=True)
            acts.append((activated * scale).astype(bf16))
            back = back * scale
            grad_gate = back * pre_up * logistic * (1.0 + pre_gate * (1.0 - logistic))
            pres.append((grad_gate.astype(bf16), (back * pre_gate * logistic).astype(bf16)))
            for s in range(2):
                produced = produced + product_transposed(pres[c][s], weight[slot, c, s])
        plan.keep(produced.astype(bf16), step, made)
        for g in range(groups):
            taken = slot_matrix(position[step, pl.ds(g, 1), :], capacity)
            part = chosen[g * capacity : (g + 1) * capacity]
            found[step, pl.ds(g, 1), :] = jnp.sum(jnp.where(taken, part, 0.0), axis=0, keepdims=True)

        def store(k):
            return [
                pltpu.make_async_copy(fresh.at[c], grads.at[spots[k, c]], out_sems.at[c])
                for c in range(cores)
            ]

        for k in range(1, held):

            @pl.when(step == k)
            def _():
                for copy in store(k - 1):
                    copy.wait()

        for c in range(cores):
            for s in range(2):
                fresh[c, s] = dot_rows(work[0], pres[c][s]).astype(bf16)
            fresh[c, 2] = dot_rows(mine, acts[c]).astype(bf16)
        for k in range(held):

            @pl.when(step == k)
            def _():
                for copy in store(k):
                    copy.start()

        @pl.when(step == held - 1)
        def _():
            def write(g, total):
                out[g, pl.ds(0, rows), :] = total.astype(bf16)
                tail = jnp.concatenate([found[k, g : g + 1, :] for k in range(held)], axis=0)
                high = tail.astype(bf16).astype(f32)
                tail = [high, tail - high, jnp.zeros((TAIL - 2 * held, rows), f32)]
                out[g, pl.ds(rows, TAIL), pl.ds(0, rows)] = jnp.concatenate(tail, axis=0).astype(bf16)

            plan.combine(position, made, init, sums, sum_sems, write)
            for copy in store(held - 1):
                copy.wait()

    whole = pl.BlockSpec(position.shape, lambda j: (0, 0, 0))
    return pl.pallas_call(
        kernel,
        grid=(held,),
        in_specs=[
            scalars,
            whole,
            whole,
            pl.BlockSpec(tokens.shape, lambda j: (0, 0), pipeline_mode=pl.Buffered(1)),
            pl.BlockSpec((1, slots, width), lambda j: (j, 0, 0)),
            pl.BlockSpec((1, cores, 2, slots, hidden), lambda j: (j, 0, 0, 0, 0)),
            anywhere,
            anywhere,
        ],
        out_specs=[pl.BlockSpec((groups, rows + TAIL, width), lambda j: (0, 0, 0)), anywhere],
        out_shape=[
            jax.ShapeDtypeStruct((groups, rows + TAIL, width), bf16),
            jax.ShapeDtypeStruct(shares.shape, bf16),
        ],
        scratch_shapes=[
            pltpu.VMEM((2, cores, 3, width, hidden), bf16),
            pltpu.VMEM((held, slots, width), bf16),
            pltpu.VMEM((groups, held * capacity, width), bf16),
            pltpu.VMEM((2, rows, width), f32),
            pltpu.VMEM((cores, 3, width, hidden), bf16),
            pltpu.VMEM(position.shape, f32),
            pltpu.SemaphoreType.DMA((2, cores)),
            pltpu.SemaphoreType.DMA((2,)),
            pltpu.SemaphoreType.DMA((cores,)),
        ],
        compiler_params=room,
        cost_estimate=no_cost,
    )(spots, position, gate, tokens, work, pre, shares, init.reshape(groups, rows, width))


def spread_shared(lay, shared_in, shared_out, member):
    rows, hidden = shared_out.shape
    part = hidden // len(lay.g_masks)
    stacked = jnp.concatenate([shared_in, shared_out[None]], axis=0)
    stacked = stacked.reshape(3 * rows, hidden)
    member_rows = member.reshape(-1, part)

    def piece(mask):
        chunk = lax.dynamic_slice_in_dim(stacked, lay.chunk(mask) * part, part, 1)
        return jnp.concatenate([chunk, member_rows], axis=0)

    pieces = [piece(0)] + [lay.shift(piece(m), m) for m in lay.g_masks[1:]]
    chunks = jnp.stack([p[: 3 * rows].reshape(3, rows, part) for p in pieces])
    return chunks, jnp.stack([p[3 * rows :].reshape(member.shape) for p in pieces])


def gather_shared(lay, blocks):
    _, _, matrices, rows, part = (len(blocks),) + blocks[0].shape
    everyone = jnp.stack(blocks, axis=1)
    natural = everyone.reshape((lay.dp, matrices, rows, part))[lay.rows_order()]
    return natural.transpose(1, 0, 2, 3).reshape(matrices, lay.dp * rows, part)


def scatter_shared(lay, grads, after):
    part = grads.shape[2] // lay.tp
    rows = grads.shape[1] // lay.dp
    own = lay.scatter_core([grads[:, :, k * part : (k + 1) * part] for k in range(lay.tp)])
    natural = own.astype(bf16).reshape(3, lay.dp, rows, part).transpose(1, 0, 2, 3)
    blocks = natural[lay.rows_apart()].reshape(len(lay.g_masks), len(lay.w_masks), 3, rows, part)
    summed = lay.scatter_w([blocks[:, k] for k in range(len(lay.w_masks))], after[0])
    summed = behind(summed, after[2])
    out = jnp.zeros((3, rows, part * len(lay.g_masks)), f32)
    for k, mask in enumerate(lay.g_masks):
        got = summed[k] if k == 0 else lay.shift(summed[k].astype(bf16), mask).astype(f32)
        out = lax.dynamic_update_slice_in_dim(out, got, lay.chunk(mask) * part, 2)
    return out


def scatter_parts(lay, parts):
    return [lay.shift(part, mask) if mask else part for part, mask in zip(parts, lay.g_masks)]


def on_device(
    block_input,
    teacher,
    lengths,
    routes,
    gain_attn,
    w_query,
    key_value_weight,
    w_out,
    gain_moe,
    w_router,
    w_shared_in,
    w_shared_out,
    w_expert_in,
    w_expert_out,
):
    lay = Layout()
    own_rows, width = block_input.shape
    tp, dp = lay.tp, lay.dp
    sequence_length = own_rows * tp
    experts = w_expert_in.shape[0] * dp
    capacity = max(2, own_rows * TOPK * 4 // (3 * experts))
    n_g, n_w = len(lay.g_masks), len(lay.w_masks)
    length = lengths[lay.place]
    slices = jnp.array(range(tp), jnp.int32) ^ lay.core
    positions = (slices[:, None] * own_rows + jnp.arange(own_rows)[None, :]).reshape(-1)
    own_valid = (positions[:own_rows] < length).astype(f32)[:, None]
    head_count = w_query.shape[1] // HEAD_SIZE
    kv_count = key_value_weight.shape[2] // HEAD_SIZE
    head_group = head_count // kv_count
    q_dim, kv_dim = head_count * HEAD_SIZE, kv_count * HEAD_SIZE
    in_kernel = n_g * own_rows <= 1024
    forward = experts_forward if in_kernel else experts_forward_plain
    backward = experts_backward if in_kernel else experts_backward_plain

    own_routes = lax.dynamic_slice_in_dim(routes, lay.core * own_rows, own_rows, 0)
    expert_ids = jnp.arange(experts, dtype=jnp.int32)
    member = jnp.any(own_routes.T[None, :, :] == expert_ids[:, None, None], axis=1)
    held_ids = lay.place ^ jnp.array(lay.w_masks, jnp.int32)
    held_hot = (held_ids[:, None] == expert_ids).astype(f32)
    shared_parts, group_member = spread_shared(
        lay, w_shared_in, w_shared_out, member.astype(bf16)
    )
    held_member = contract("je,get->jgt", held_hot.astype(bf16), group_member)
    before = jnp.triu(jnp.ones((own_rows, own_rows), bf16), 1)
    position = contract("jgu,ut->jgt", held_member.astype(bf16), before)
    position = jnp.where(held_member > 0, position, -1.0)

    near, far = (1 << bit for bit in lay.w_bits)
    input_slices = lay.gather_core(block_input)
    qkv = Tree(lay, jnp.concatenate([w_query, key_value_weight[0], key_value_weight[1]], axis=1))
    router_pad = jnp.zeros((w_router.shape[0], -experts % 128), bf16)
    out = Tree(lay, jnp.concatenate([w_out, w_router, router_pad], axis=1))
    expert_shares = lax.all_gather(
        jnp.concatenate([w_expert_in[0], w_expert_out], axis=0),
        ("dp", "tensor"),
        axis_index_groups=lay.w_groups(),
    )
    steps = len(lay.steps)
    qkv.step()
    out.step(qkv.marks[0])
    qkv.step(shared_parts, input_slices, group_member)
    shared_far = lay.shift(behind(shared_parts, out.marks[0]), far)
    out.step(qkv.marks[1])
    for k in range(2, steps):
        gates = [out.marks[min(k - 2, 1)]] + ([shared_far] if k == steps - 1 else [])
        qkv.step(*gates)
    for k in range(2, steps):
        out.step(qkv.marks[-1])
    shared_near = lay.shift(behind(jnp.stack([shared_parts, shared_far]), qkv.marks[-1]), near)

    spot = jnp.stack([lay.core, length]).astype(jnp.int32)
    in_order = lay.gather_order()
    residual = block_input.astype(f32)
    _, scale_attn = normalize_rows(residual, gain_attn)

    def by_core(rows):
        return [rows[k * own_rows : (k + 1) * own_rows] for k in range(tp)]

    if in_kernel:
        normed_all, projected, mixed_heads, logs = attend(
            in_order, spot, *input_slices, gain_attn, qkv.halves, head_count, kv_count
        )
        *attn_parts, out_router = project_out(
            behind(in_order, shared_near), mixed_heads, out.halves
        )
    else:
        qkv_full, out_router = lay.in_order(qkv.halves), lay.in_order(out.halves)
        normed_all, _ = normalize_rows(
            jnp.concatenate(input_slices, axis=0).astype(f32), gain_attn
        )
        projected = product(normed_all, qkv_full).astype(bf16)
        queries = projected[:, :q_dim].reshape(sequence_length, kv_count, head_group, HEAD_SIZE)
        key_row_table = projected[:, q_dim : q_dim + kv_dim].reshape(
            sequence_length, kv_count, HEAD_SIZE
        )
        value_row_table = projected[:, q_dim + kv_dim :].reshape(
            sequence_length, kv_count, HEAD_SIZE
        )
        allowed = (positions[None, :] <= positions[:, None]) & (positions[None, :] < length)
        scores = contract("qvgd,kvd->vgqk", queries, key_row_table) * HEAD_SIZE ** (-0.5)
        scores = jnp.where(allowed, scores, masked_score)
        row_max = jnp.max(scores, axis=-1, keepdims=True)
        exponent_terms = jnp.exp(scores - row_max)
        row_sum = jnp.sum(exponent_terms, axis=-1, keepdims=True)
        probs_full = exponent_terms / row_sum
        probs_low = probs_full.astype(bf16)
        mixed_heads = (
            contract("vgqk,kvd->qvgd", probs_low, value_row_table)
            .astype(bf16)
            .reshape(sequence_length, q_dim)
        )
        attn_parts = by_core(product_transposed(mixed_heads, out_router[:, :q_dim]))
    router_full = out_router[:, q_dim : q_dim + experts]
    hidden = residual + lay.scatter_core(attn_parts)
    moe_own, scale_moe = normalize_rows(hidden, gain_moe)

    arrived = lay.gather_g(moe_own)
    shared_own = gather_shared(lay, [shared_parts, shared_near[0], shared_far, shared_near[1]])
    shared_full = jnp.concatenate(lay.gather_core(shared_own), axis=2)
    shared_in_full, shared_out_full = shared_full[:2], shared_full[2]

    group_rows = jnp.concatenate(arrived, axis=0)
    logits = lax.dot_general(
        router_full, group_rows, (((0,), (1,)), ((), ())), preferred_element_type=f32
    )
    shown = jnp.where(
        group_member.transpose(1, 0, 2).reshape(experts, -1) > 0, logits, masked_score
    )
    gate_terms = jnp.exp(shown - jnp.max(shown, axis=0, keepdims=True))
    gates = gate_terms / jnp.sum(gate_terms, axis=0, keepdims=True)
    own_gates = gates[:, :own_rows]
    held_gates = jnp.sum(held_hot[:, :, None] * gates[None], axis=1).reshape(n_w, n_g, own_rows)
    shared_pre = contract("td,cdf->ctf", group_rows, shared_in_full)
    shared_act = (jax.nn.silu(shared_pre[0]) * shared_pre[1]).astype(bf16)
    total = product_transposed(shared_act, shared_out_full)
    spots = lay.w_spots()
    total, work, pre = forward(
        position, held_gates, spots, capacity, group_rows, expert_shares, total
    )

    def scatter_g(parts):
        return sum(part.astype(f32) for part in scatter_parts(lay, parts))

    out_rows = (hidden + scatter_g([total[k] for k in range(n_g)])) * own_valid
    residual_error = (out_rows - teacher.astype(f32)) * own_valid
    loss_part = 0.5 * jnp.sum(residual_error * residual_error)

    group_grad = jnp.concatenate(lay.gather_g(residual_error.astype(bf16)), axis=0)
    grad_shared_act = product(group_grad, shared_out_full)
    grad_shared_out = product_left(group_grad, shared_act)
    grad_shared_pre = jnp.stack(swish_back(shared_pre[0], shared_pre[1], grad_shared_act))
    grad_shared_in = contract("td,ctf->cdf", group_rows, grad_shared_pre)
    total = contract("ctf,cdf->td", grad_shared_pre, shared_in_full)
    total, grad_shares = backward(
        position, held_gates, spots, capacity, group_grad, work, pre, expert_shares, total
    )
    grad_expert = lax.psum_scatter(
        grad_shares, ("dp", "tensor"), axis_index_groups=lay.w_groups()
    ).astype(f32)
    received = scatter_parts(lay, [total[k] for k in range(n_g)])
    returned = received[0][:own_rows].astype(f32)
    for part in received[1:]:
        returned = returned + part[:own_rows].astype(f32)
    gate_rows = [part[own_rows:, :own_rows].astype(f32) for part in received]
    gate_rows = [rows[:n_w] + rows[n_w : 2 * n_w] for rows in gate_rows]
    ids = lay.place ^ jnp.array([g ^ w for g in lay.g_masks for w in lay.w_masks], jnp.int32)
    placed = (expert_ids[:, None] == ids).astype(f32)[:, :, None]
    grad_gates = jnp.sum(placed * jnp.concatenate(gate_rows, axis=0)[None], axis=1)
    grad_logits = (
        own_gates * (grad_gates - jnp.sum(own_gates * grad_gates, axis=0, keepdims=True))
    ).astype(bf16)
    grad_router_part = lax.dot_general(
        moe_own, grad_logits, (((0,), (1,)), ((), ())), preferred_element_type=f32
    )
    grad_normed_own = returned + lax.dot_general(
        grad_logits, router_full, (((0,), (1,)), ((), ())), preferred_element_type=f32
    )

    grad_from_moe, grad_gain_moe_part = normalize_back(hidden, scale_moe, gain_moe, grad_normed_own)
    grad_hidden = residual_error + grad_from_moe
    grad_slices = lay.gather_core(grad_hidden.astype(bf16))
    grad_router_part = jnp.pad(
        lay.scatter_core([grad_router_part] * tp).astype(bf16), ((0, 0), (0, -experts % 128))
    )
    if in_kernel:
        grad_mixed, *out_back_halves = project_out_back(
            lay.scatter_order(), *grad_slices, out_router, mixed_heads, grad_router_part
        )
        grad_projected, *qkv_back_halves = attend_back(
            lay.scatter_order(), spot, grad_mixed, normed_all, projected, logs, head_count, kv_count
        )
        normed_parts = normed_back(in_order, grad_projected, qkv.halves)
    else:
        grad_attn = jnp.concatenate(grad_slices, axis=0)
        grad_mixed = (
            product(grad_attn, out_router[:, :q_dim])
            .astype(bf16)
            .reshape(sequence_length, kv_count, head_group, HEAD_SIZE)
        )
        grad_values = contract("vgqk,qvgd->kvd", probs_low, grad_mixed)
        grad_probs = contract("qvgd,kvd->vgqk", grad_mixed, value_row_table)
        delta_sum = jnp.sum(probs_full * grad_probs, axis=-1, keepdims=True)
        grad_scores = (probs_full * (grad_probs - delta_sum)).astype(bf16)
        grad_queries = contract("vgqk,kvd->qvgd", grad_scores, key_row_table) * HEAD_SIZE ** (-0.5)
        grad_keys = contract("vgqk,qvgd->kvd", grad_scores, queries) * HEAD_SIZE ** (-0.5)
        grad_projected = jnp.concatenate(
            [
                grad_queries.astype(bf16).reshape(sequence_length, q_dim),
                grad_keys.astype(bf16).reshape(sequence_length, kv_dim),
                grad_values.astype(bf16).reshape(sequence_length, kv_dim),
            ],
            axis=1,
        )
        out_back_halves = lay.in_halves(
            jnp.concatenate([product_left(grad_attn, mixed_heads).astype(bf16), grad_router_part], axis=1)
        )
        qkv_back_halves = lay.in_halves(product_left(normed_all, grad_projected))
        normed_parts = by_core(product_transposed(grad_projected, qkv_full))
    out_back = Sum(lay, out_back_halves)
    keep, send = qkv_back_halves
    send = behind(send, out_back.step(grad_projected))
    qkv_back = Sum(lay, (keep, send))
    qkv_back.step()
    for k in range(1, steps):
        out_back.step(qkv_back.marks[k - 1] if k > 1 else grad_projected)
        qkv_back.step()
    grad_qkv, grad_out_router = qkv_back.total[0], out_back.total[0]
    qkv_back = qkv_back.marks
    grad_normed_attn = lay.scatter_core(normed_parts)
    grad_from_attn, grad_gain_attn_part = normalize_back(
        residual, scale_attn, gain_attn, grad_normed_attn
    )
    input_grad = grad_hidden + grad_from_attn
    grad_w_kv = jnp.stack(
        [grad_qkv[:, q_dim : q_dim + kv_dim], grad_qkv[:, q_dim + kv_dim :]], axis=0
    )
    small = jnp.stack(
        [grad_gain_attn_part, grad_gain_moe_part, jnp.full((width,), loss_part, f32)], axis=0
    )
    small = lay.sum_all(small, qkv_back)
    loss = small[2, 0] / (jnp.sum(lengths).astype(f32) * width)
    grad_shared = scatter_shared(
        lay, jnp.concatenate([grad_shared_in, grad_shared_out[None]]), qkv_back
    )
    return (
        out_rows.astype(bf16),
        loss,
        input_grad,
        small[0],
        grad_qkv[:, :q_dim],
        grad_w_kv,
        grad_out_router[:, :q_dim],
        small[1],
        grad_out_router[:, q_dim : q_dim + experts],
        grad_shared[:2],
        grad_shared[2],
        grad_expert[None, :2],
        grad_expert[2:],
    )


def solution(mesh):
    rows, weights = P(("dp", "tensor"), None), P("dp", "tensor")
    stacked = P(None, "dp", "tensor")
    expert_in, expert_out = P("dp", None, None, "tensor"), P("dp", None, "tensor")
    return jax.shard_map(
        on_device,
        mesh=mesh,
        in_specs=(
            rows,
            rows,
            P(),
            P("dp", None),
            P(),
            weights,
            stacked,
            weights,
            P(),
            P("dp", None),
            stacked,
            weights,
            expert_in,
            expert_out,
        ),
        out_specs=(
            rows,
            P(),
            rows,
            P(),
            weights,
            stacked,
            weights,
            P(),
            P("dp", None),
            stacked,
            weights,
            expert_in,
            expert_out,
        ),
        check_vma=False,
    )
```

time: 1030 us -> 729 us (0.71)
  Pallas kernels: 0 us -> 124 us
  matrix products: 146 us -> 26.4 us
  waiting for transfers between devices: 530 us -> 421 us
  other arithmetic: 118 us -> 38.5 us
  local copies, waits for them, and re-layouts: 107 us -> 31.3 us
  blocking collectives: 41.8 us -> 0 us
    pallas_call x0 -> x7, Pallas kernels: none -> 124 us  [the longest x1 53.4 us: experts_backward(): pl.pallas_call(kernel, grid=(held,), in_specs=[scalars, whole, whole, pl....]
    unnamed x2, waiting for transfers between devices: 118 us -> 0.03 us
    dot_general x19 -> x5, matrix products: 106 us -> 12.3 us  [contract(): return jnp.einsum(spec, *operands, preferred_element_type=f32)]
    another operation x13 -> x10, other arithmetic: 47.6 us -> 5.62 us  [the longest x3 1.25 us: w_spots(): return jnp.stack(rows).astype(jnp.int32)]
    all_gather x1 -> x0, blocking collectives: 41.8 us -> none  [on_device(): router_full = lax.all_gather(w_router, 'dp', axis=0, tiled=True)]
    unnamed x200 -> x114, local copies, waits for them, and re-layouts: 32.4 us -> 6.02 us
    gather x7 -> x1, local copies, waits for them, and re-layouts: 24.2 us -> 0.77 us  [gather_shared(): natural = everyone.reshape((lay.dp, matrices, rows, part))[lay.rows_order()]]
    ppermute x37 -> x34, waiting for transfers between devices: 273 us -> 293 us  [shift(): return lax.ppermute(values, 'dp', [(i, i ^ mask) for i in range(self.dp)])]
  transfers between devices with their start and end apart: 64 -> 52, of which waited for: 29 -> 33; matrix products, arithmetic and copies ran while one was open for 21% -> 10% of each run, Pallas kernels for 0% -> 6%
where the time goes in v2:
time: 729 us; the launch traced here: 720 us
  waiting for transfers between devices  421 us (58%)
  Pallas kernels  124 us (17%)
  starting transfers between devices  60.4 us (8%)
  other arithmetic  38.5 us (5%)
  local copies, waits for them, and re-layouts  31.3 us (4%)
  matrix products  26.4 us (4%)
  between operations  18.9 us (3%)
    ppermute x34, waiting for transfers between devices, shift(): return lax.ppermute(values, 'dp', [(i, i ^ mask) for i in range(self.dp)])  293 us
    ppermute x8, waiting for transfers between devices, shift_step(): return lax.ppermute(values, ('dp', 'tensor'), pairs)  128 us
    pallas_call x1, Pallas kernels, experts_backward(): pl.pallas_call(kernel, grid=(held,), in_specs=[scalars, whole, whole, pl....  53.4 us
    ppermute x34, starting transfers between devices, shift(): return lax.ppermute(values, 'dp', [(i, i ^ mask) for i in range(self.dp)])  34.5 us
    pallas_call x1, Pallas kernels, experts_forward(): pl.pallas_call(kernel, grid=(held,), in_specs=[scalars, whole, whole, pl....  24 us
    ppermute x8, starting transfers between devices, shift_step(): return lax.ppermute(values, ('dp', 'tensor'), pairs)  15.8 us
  transfers between devices with their start and end apart: 52, of which 33 were waited for; matrix products, arithmetic and copies ran while one was open for 10% of the time, Pallas kernels for 6%

profile of v2, /device:TPU:0, one launch (start us, length us, event | category | flops | bytes accessed | tf_op | source)
XLA Modules:
  0.0 720.5 jit_solution(11185035736625899501)
XLA Ops:
  7.2 3.3 pad_maximum_fusion.3
  11.7 3.0 collective-permute-start
  16.4 3.1 collective-permute-start.3
  23.2 36.7 %collective-permute-done.3 = bf16[1,96,1280]{2,1,0:T(8,128)(2,1)S(1)} collective-permute-done((bf16[1,96,1280]{2,1,0:T(8,128)(2,1)S(1)}, bf16[1,96,1280]{2,1,0:T(8,128)(2,1)S(1)}, u32[]{:S(2)}, u32[]{:S(2)}) %collective-permute-start.3) | collective-permute-done | bytes 245792 | tf_op jit(solution)/shard_map/ppermute | solution.py:140
  59.9 2.8 collective-permute-start.7
  62.9 3.4 collective-permute-start.4
  66.4 29.7 %collective-permute-done.7 = bf16[2,96,1280]{2,1,0:T(8,128)(2,1)S(1)} collective-permute-done((bf16[2,96,1280]{2,1,0:T(8,128)(2,1)S(1)}, bf16[2,96,1280]{2,1,0:T(8,128)(2,1)S(1)}, u32[]{:S(2)}, u32[]{:S(2)}) %collective-permute-start.7) | collective-permute-done | bytes 491552 | tf_op jit(solution)/shard_map/ppermute | solution.py:140
  98.0 4.0 collective-permute-start.5
  102.0 29.3 %collective-permute-done.8 = bf16[4,96,1280]{2,1,0:T(8,128)(2,1)S(1)} collective-permute-done((bf16[4,96,1280]{2,1,0:T(8,128)(2,1)S(1)}, bf16[4,96,1280]{2,1,0:T(8,128)(2,1)S(1)}, u32[]{:S(2)}, u32[]{:S(2)}) %collective-permute-start.8) | collective-permute-done | bytes 983072 | tf_op jit(solution)/shard_map/ppermute | solution.py:140
  131.5 38.6 %collective-permute-done.5 = bf16[4,3,96,128]{3,2,1,0:T(8,128)(2,1)S(1)} collective-permute-done((bf16[4,3,96,128]{3,2,1,0:T(8,128)(2,1)S(1)}, bf16[4,3,96,128]{3,2,1,0:T(8,128)(2,1)S(1)}, u32[]{:S(2)}, u32[]{:S(2)}) %collective-permute-start.5) | collective-permute-done | bytes 294944 | tf_op jit(solution)/shard_map/ppermute | solution.py:112
  171.9 22.8 %collective-permute-done.10.far = bf16[8,96,1280]{2,1,0:T(8,128)(2,1)S(1)} collective-permute-done((bf16[8,96,1280]{2,1,0:T(8,128)(2,1)S(1)}, bf16[8,96,1280]{2,1,0:T(8,128)(2,1)S(1)}, u32[]{:S(2)}, u32[]{:S(2)}) %collective-permute-start.10) | collective-permute-done | bytes 1966112 | tf_op jit(solution)/shard_map/ppermute | solution.py:140
  196.0 9.7 %collective-permute-done.12 = bf16[4,96,896]{2,1,0:T(8,128)(2,1)S(1)} collective-permute-done((bf16[4,96,896]{2,1,0:T(8,128)(2,1)S(1)}, bf16[4,96,896]{2,1,0:T(8,128)(2,1)S(1)}, u32[]{:S(2)}, u32[]{:S(2)}) %collective-permute-start.12) | collective-permute-done | bytes 688160 | tf_op jit(solution)/shard_map/ppermute | solution.py:140
  213.3 10.7 %shard_map.273 = (bf16[512,1536]{1,0:T(8,128)(2,1)}, bf16[512,1280]{1,0:T(8,128)(2,1)}, bf16[512,768]{1,0:T(8,128)(2,1)}, f32[6,512,1]{2,1,0:T(8,128)}) custom-call(s32[16]{0:T(128)} %shift-left_add_fusion.1.order, s32[2]{0:T(128)} %pad_add_fusion.1.spot, bf16[256,1536]{1,0:T(8,128)(2,1)} %own.1, bf16[256,1536]{1,0:T(8,128)(2,1)} %copy-done.33, ...), custom_call_target="tpu_custom_call" | custom-call | tf_op jit(solution)/shard_map/pallas_call | solution.py:329
  226.2 6.3 shard_map.274
  232.4 9.0 %collective-permute-start.14 = (bf16[256,1536]{1,0:T(8,128)(2,1)}, bf16[256,1536]{1,0:T(8,128)(2,1)}, u32[]{:S(2)}, u32[]{:S(2)}) collective-permute-start(bf16[256,1536]{1,0:T(8,128)(2,1)} %get-tuple-element.66), channel_id=1, source_target_pairs={{0,1},{1,0},{2,3},{3,2},{4,5},{5,4},{6,7},{7,6},{8,9},{9,8},{10,11... | collective-permute-start | bytes 2359304 | tf_op jit(solution)/shard_map/ppermute | solution.py:131
  253.0 14.8 %collective-permute-done.15 = bf16[256,1536]{1,0:T(8,128)(2,1)S(1)} collective-permute-done((bf16[256,1536]{1,0:T(8,128)(2,1)S(1)}, bf16[256,1536]{1,0:T(8,128)(2,1)S(1)}, u32[]{:S(2)}, u32[]{:S(2)}) %collective-permute-start.15) | collective-permute-done | bytes 786464 | tf_op jit(solution)/shard_map/ppermute | solution.py:112
  269.7 16.1 %collective-permute-done.17 = bf16[256,1536]{1,0:T(8,128)(2,1)S(1)} collective-permute-done((bf16[256,1536]{1,0:T(8,128)(2,1)S(1)}, bf16[256,1536]{1,0:T(8,128)(2,1)S(1)}, u32[]{:S(2)}, u32[]{:S(2)}) %collective-permute-start.17) | collective-permute-done | bytes 786464 | tf_op jit(solution)/shard_map/ppermute | solution.py:112
  286.1 3.5 fusion.10
  296.9 4.9 fusion.46.init
  301.8 24.0 %shard_map.275 = (bf16[4,256,1536]{2,1,0:T(8,128)(2,1)}, bf16[4,512,1536]{2,1,0:T(8,128)(2,1)}, f32[4,2,2,512,256]{4,3,2,1,0:T(8,128)}) custom-call(s32[4,2]{1,0:T(4,128)} %pad_add_fusion.spots, f32[4,4,256]{2,1,0:T(4,128)} %convolution_select_fusion.1.position, f32[4,4,256]{2,1,0:T(4,128)} %reshape.239.gate, bf16[1024,1536]{1,0:T(8,128)(2,1)} %copy-done.2, ...), custom_call_target="tpu_custom_call" | custom-call | tf_op jit(solution)/shard_map/pallas_call | solution.py:587
  332.0 15.4 %collective-permute-done.19 = bf16[256,1536]{1,0:T(8,128)(2,1)S(1)} collective-permute-done((bf16[256,1536]{1,0:T(8,128)(2,1)S(1)}, bf16[256,1536]{1,0:T(8,128)(2,1)S(1)}, u32[]{:S(2)}, u32[]{:S(2)}) %collective-permute-start.19) | collective-permute-done | bytes 786464 | tf_op jit(solution)/shard_map/ppermute | solution.py:112
  347.4 2.3 collective-permute-done.20
  349.8 14.9 %collective-permute-done.21 = bf16[256,1536]{1,0:T(8,128)(2,1)S(1)} collective-permute-done((bf16[256,1536]{1,0:T(8,128)(2,1)S(1)}, bf16[256,1536]{1,0:T(8,128)(2,1)S(1)}, u32[]{:S(2)}, u32[]{:S(2)}) %collective-permute-start.21) | collective-permute-done | bytes 786464 | tf_op jit(solution)/shard_map/ppermute | solution.py:112
  364.7 2.6 multiply_reduce_fusion
  371.1 16.1 %collective-permute-done.22 = bf16[256,1536]{1,0:T(8,128)(2,1)S(1)} collective-permute-done((bf16[256,1536]{1,0:T(8,128)(2,1)S(1)}, bf16[256,1536]{1,0:T(8,128)(2,1)S(1)}, u32[]{:S(2)}, u32[]{:S(2)}) %collective-permute-start.22) | collective-permute-done | bytes 786464 | tf_op jit(solution)/shard_map/ppermute | solution.py:112
  387.1 2.3 collective-permute-done.23
  389.5 13.7 %collective-permute-done.24 = bf16[256,1536]{1,0:T(8,128)(2,1)S(1)} collective-permute-done((bf16[256,1536]{1,0:T(8,128)(2,1)S(1)}, bf16[256,1536]{1,0:T(8,128)(2,1)S(1)}, u32[]{:S(2)}, u32[]{:S(2)}) %collective-permute-start.24) | collective-permute-done | bytes 786464 | tf_op jit(solution)/shard_map/ppermute | solution.py:112
  403.5 2.6 fusion.55
  406.1 6.0 fusion.24
  412.0 53.4 %shard_map.276 = (bf16[4,272,1536]{2,1,0:T(8,128)(2,1)}, bf16[8,3,1536,256]{3,2,1,0:T(8,128)(2,1)}) custom-call(s32[4,2]{1,0:T(4,128)} %pad_add_fusion.spots, f32[4,4,256]{2,1,0:T(4,128)} %convolution_select_fusion.1.position, f32[4,4,256]{2,1,0:T(4,128)} %reshape.239.gate, bf16[1024,1536]{1,0:T(8,128)(2,1)} %copy-done.8, ...), custom_call_target="tpu_custom_call" | custom-call | tf_op jit(solution)/shard_map/pallas_call | solution.py:697
  474.3 16.7 %collective-permute-done.27 = bf16[272,1536]{1,0:T(8,128)(2,1)S(1)} collective-permute-done((bf16[272,1536]{1,0:T(8,128)(2,1)S(1)}, bf16[272,1536]{1,0:T(8,128)(2,1)S(1)}, u32[]{:S(2)}, u32[]{:S(2)}) %collective-permute-start.27) | collective-permute-done | bytes 835616 | tf_op jit(solution)/shard_map/ppermute | solution.py:112
  491.0 15.1 %collective-permute-done.26 = bf16[272,1536]{1,0:T(8,128)(2,1)S(1)} collective-permute-done((bf16[272,1536]{1,0:T(8,128)(2,1)S(1)}, bf16[272,1536]{1,0:T(8,128)(2,1)S(1)}, u32[]{:S(2)}, u32[]{:S(2)}) %collective-permute-start.26) | collective-permute-done | bytes 835616 | tf_op jit(solution)/shard_map/ppermute | solution.py:112
  518.5 7.9 %shard_map.277 = (bf16[512,768]{1,0:T(8,128)(2,1)}, bf16[8,96,896]{2,1,0:T(8,128)(2,1)}, bf16[8,96,896]{2,1,0:T(8,128)(2,1)}) custom-call(s32[16]{0:T(128)} %shift-left_add_fusion.order, bf16[256,1536]{1,0:T(8,128)(2,1)} %get-tuple-element.168.own, bf16[256,1536]{1,0:T(8,128)(2,1)} %collective-permute-done.28.other, ...), custom_call_target="tpu_custom_call" | custom-call | tf_op jit(solution)/shard_map/pallas_call | solution.py:393
  530.2 14.0 %shard_map.278 = (bf16[512,1280]{1,0:T(8,128)(2,1)}, bf16[8,96,1280]{2,1,0:T(8,128)(2,1)}, bf16[8,96,1280]{2,1,0:T(8,128)(2,1)}) custom-call(s32[16]{0:T(128)} %shift-left_add_fusion.order, s32[2]{0:T(128)} %pad_add_fusion.1.spot, bf16[512,768]{1,0:T(8,128)(2,1)} %get-tuple-element.72.grad_mixed, bf16[512,1536]{1,0:T(8,128)(2,1)} %get-tuple-element.73.normed, ...), custom_call_target="tpu_custom_call" | custom-call | tf_op jit(solution)/shard_map/pallas_call | solution.py:437
  544.2 7.4 %shard_map.279 = (f32[256,1536]{1,0:T(8,128)}, bf16[256,1536]{1,0:T(8,128)(2,1)}) custom-call(s32[16]{0:T(128)} %shift-left_add_fusion.1.order, bf16[512,1280]{1,0:T(8,128)(2,1)} %get-tuple-element.76.grad_made, bf16[8,96,1280]{2,1,0:T(8,128)(2,1)} %copy-done.6, bf16[8,96,1280]{2,1,0:T(8,128)(2,1)} %copy-done.13), custom_call_target="tpu_custom_call" | custom-call | tf_op jit(solution)/shard_map/pallas_call | solution.py:463
  551.6 7.7 %collective-permute-done.31 = bf16[8,96,896]{2,1,0:T(8,128)(2,1)} collective-permute-done((bf16[8,96,896]{2,1,0:T(8,128)(2,1)}, bf16[8,96,896]{2,1,0:T(8,128)(2,1)}, u32[]{:S(2)}, u32[]{:S(2)}) %collective-permute-start.31) | collective-permute-done | bytes 1376288 | tf_op jit(solution)/shard_map/ppermute | solution.py:112
  559.6 2.6 fusion.5
  568.5 3.0 fusion.22
  574.8 29.3 %collective-permute-done.32 = bf16[8,96,1280]{2,1,0:T(8,128)(2,1)} collective-permute-done((bf16[8,96,1280]{2,1,0:T(8,128)(2,1)}, bf16[8,96,1280]{2,1,0:T(8,128)(2,1)}, u32[]{:S(2)}, u32[]{:S(2)}) %collective-permute-start.32) | collective-permute-done | bytes 1966112 | tf_op jit(solution)/shard_map/ppermute | solution.py:112
  607.8 6.9 collective-permute-done.41
  618.8 28.4 %collective-permute-done.34 = bf16[4,96,1280]{2,1,0:T(8,128)(2,1)S(1)} collective-permute-done((bf16[4,96,1280]{2,1,0:T(8,128)(2,1)S(1)}, bf16[4,96,1280]{2,1,0:T(8,128)(2,1)S(1)}, u32[]{:S(2)}, u32[]{:S(2)}) %collective-permute-start.34) | collective-permute-done | bytes 983072 | tf_op jit(solution)/shard_map/ppermute | solution.py:112
  647.6 15.1 %collective-permute-done.46 = bf16[4,3,96,128]{3,2,1,0:T(8,128)(2,1)S(1)} collective-permute-done((bf16[4,3,96,128]{3,2,1,0:T(8,128)(2,1)S(1)}, bf16[4,3,96,128]{3,2,1,0:T(8,128)(2,1)S(1)}, u32[]{:S(2)}, u32[]{:S(2)}) %collective-permute-start.46) | collective-permute-done | bytes 294944 | tf_op jit(solution)/shard_map/ppermute | solution.py:112
  663.1 3.6 collective-permute-done.35
  668.2 7.7 %collective-permute-done.43 = bf16[1,96,896]{2,1,0:T(8,128)(2,1)S(1)} collective-permute-done((bf16[1,96,896]{2,1,0:T(8,128)(2,1)S(1)}, bf16[1,96,896]{2,1,0:T(8,128)(2,1)S(1)}, u32[]{:S(2)}, u32[]{:S(2)}) %collective-permute-start.43) | collective-permute-done | bytes 172064 | tf_op jit(solution)/shard_map/ppermute | solution.py:112
  679.8 2.8 collective-permute-done.37
  684.4 3.1 collective-permute-done.49
  689.0 8.7 %collective-permute-done.38 = bf16[1,96,1280]{2,1,0:T(8,128)(2,1)S(1)} collective-permute-done((bf16[1,96,1280]{2,1,0:T(8,128)(2,1)S(1)}, bf16[1,96,1280]{2,1,0:T(8,128)(2,1)S(1)}, u32[]{:S(2)}, u32[]{:S(2)}) %collective-permute-start.38) | collective-permute-done | bytes 245792 | tf_op jit(solution)/shard_map/ppermute | solution.py:112
  697.8 4.6 collective-permute-done.39
  (333 shorter events, 111.9 us)
Async XLA Ops:
  7.2 294.6 %all-gather.3.cloned.1.call-start = ((), (), s32[]{:S(2)}) async-start(), calls=%async_computation.2 | async-start | bytes 21233664 | tf_op jit(solution)/shard_map/all_gather | solution.py:826
  10.6 695.2 %reduce-scatter.2.cloned.1.call-start = ((), (), s32[]{:S(2)}) async-start(), calls=%async_computation.1 | async-start | bytes 21233664 | tf_op jit(solution)/shard_map/reduce_scatter | solution.py:930
  11.7 7.7 %collective-permute-start = (bf16[320,128]{1,0:T(8,128)(2,1)S(1)}, bf16[320,128]{1,0:T(8,128)(2,1)S(1)}, u32[]{:S(2)}, u32[]{:S(2)}) collective-permute-start(bf16[320,128]{1,0:T(8,128)(2,1)S(1)} %get-tuple-element.203), channel_id=1, source_target_pairs={{0,2},{2,0},{4,6},{6,4},{8,10},{10,8},{12,14},{14,12},{16,18},{18,... | collective-permute-start | bytes 245768 | tf_op jit(solution)/shard_map/ppermute | solution.py:112
  14.7 5.2 collective-permute-start.1
  16.3 5.3 collective-permute-start.2
  16.3 43.6 %collective-permute-start.6 = (bf16[256,1536]{1,0:T(8,128)(2,1)S(1)}, bf16[256,1536]{1,0:T(8,128)(2,1)S(1)}, u32[]{:S(2)}, u32[]{:S(2)}) collective-permute-start(bf16[256,1536]{1,0:T(8,128)(2,1)S(1)} %copy-done.10), channel_id=1, source_target_pairs={{0,1},{1,0},{2,3},{3,2},{4,5},{5,4},{6,7},{7,6},{8,9},{9,8},{10,11... | collective-permute-start | bytes 2359304 | tf_op jit(solution)/shard_map/ppermute | solution.py:131
  16.4 43.5 %collective-permute-start.3 = (bf16[1,96,1280]{2,1,0:T(8,128)(2,1)S(1)}, bf16[1,96,1280]{2,1,0:T(8,128)(2,1)S(1)}, u32[]{:S(2)}, u32[]{:S(2)}) collective-permute-start(bf16[1,96,1280]{2,1,0:T(8,128)(2,1)S(1)} %maximum_bitcast_fusion), channel_id=1, source_target_pairs={{0,16},{1,17},{2,18},{3,19},{4,20},{5,21},{6,22},{7,23},{8,24},{9,... | collective-permute-start | bytes 737288 | tf_op jit(solution)/shard_map/ppermute | solution.py:140
  59.9 36.2 %collective-permute-start.7 = (bf16[2,96,1280]{2,1,0:T(8,128)(2,1)S(1)}, bf16[2,96,1280]{2,1,0:T(8,128)(2,1)S(1)}, u32[]{:S(2)}, u32[]{:S(2)}) collective-permute-start(bf16[2,96,1280]{2,1,0:T(8,128)(2,1)S(1)} %pad_maximum_fusion.15), channel_id=1, source_target_pairs={{0,8},{1,9},{2,10},{3,11},{4,12},{5,13},{6,14},{7,15},{8,0},{9,1},... | collective-permute-start | bytes 1474568 | tf_op jit(solution)/shard_map/ppermute | solution.py:140
  62.9 33.3 %collective-permute-start.4 = (bf16[1,96,896]{2,1,0:T(8,128)(2,1)S(1)}, bf16[1,96,896]{2,1,0:T(8,128)(2,1)S(1)}, u32[]{:S(2)}, u32[]{:S(2)}) collective-permute-start(bf16[1,96,896]{2,1,0:T(8,128)(2,1)S(1)} %maximum_bitcast_fusion.1), channel_id=1, source_target_pairs={{0,16},{1,17},{2,18},{3,19},{4,20},{5,21},{6,22},{7,23},{8,24},{9,... | collective-permute-start | bytes 516104 | tf_op jit(solution)/shard_map/ppermute | solution.py:140
  96.2 35.1 %collective-permute-start.8 = (bf16[4,96,1280]{2,1,0:T(8,128)(2,1)S(1)}, bf16[4,96,1280]{2,1,0:T(8,128)(2,1)S(1)}, u32[]{:S(2)}, u32[]{:S(2)}) collective-permute-start(bf16[4,96,1280]{2,1,0:T(8,128)(2,1)S(1)} %pad_maximum_fusion.8), channel_id=1, source_target_pairs={{0,4},{1,3},{2,6},{3,1},{4,0},{5,7},{6,2},{7,5},{8,12},{9,11},{10,... | collective-permute-start | bytes 2949128 | tf_op jit(solution)/shard_map/ppermute | solution.py:140
  97.9 72.2 %collective-permute-start.9 = (bf16[2,96,896]{2,1,0:T(8,128)(2,1)S(1)}, bf16[2,96,896]{2,1,0:T(8,128)(2,1)S(1)}, u32[]{:S(2)}, u32[]{:S(2)}) collective-permute-start(bf16[2,96,896]{2,1,0:T(8,128)(2,1)S(1)} %pad_maximum_fusion.16), channel_id=1, source_target_pairs={{0,8},{1,9},{2,10},{3,11},{4,12},{5,13},{6,14},{7,15},{8,0},{9,1},... | collective-permute-start | bytes 1032200 | tf_op jit(solution)/shard_map/ppermute | solution.py:140
  98.0 72.1 %collective-permute-start.5 = (bf16[4,3,96,128]{3,2,1,0:T(8,128)(2,1)S(1)}, bf16[4,3,96,128]{3,2,1,0:T(8,128)(2,1)S(1)}, u32[]{:S(2)}, u32[]{:S(2)}) collective-permute-start(bf16[4,3,96,128]{3,2,1,0:T(8,128)(2,1)S(1)} %copy-done.38), channel_id=1, source_target_pairs={{0,16},{2,18},{4,20},{6,22},{8,24},{10,26},{12,28},{14,30},{16,0},... | collective-permute-start | bytes 884744 | tf_op jit(solution)/shard_map/ppermute | solution.py:112
  170.1 24.6 %collective-permute-start.10 = (bf16[8,96,1280]{2,1,0:T(8,128)(2,1)S(1)}, bf16[8,96,1280]{2,1,0:T(8,128)(2,1)S(1)}, u32[]{:S(2)}, u32[]{:S(2)}) collective-permute-start(bf16[8,96,1280]{2,1,0:T(8,128)(2,1)S(1)} %pad_maximum_fusion.4.near), channel_id=1, source_target_pairs={{0,2},{1,5},{2,0},{3,7},{4,6},{5,1},{6,4},{7,3},{8,10},{9,13},{10,... | collective-permute-start | bytes 5898248 | tf_op jit(solution)/shard_map/ppermute | solution.py:140
  194.7 10.9 %collective-permute-start.12 = (bf16[4,96,896]{2,1,0:T(8,128)(2,1)S(1)}, bf16[4,96,896]{2,1,0:T(8,128)(2,1)S(1)}, u32[]{:S(2)}, u32[]{:S(2)}) collective-permute-start(bf16[4,96,896]{2,1,0:T(8,128)(2,1)S(1)} %pad_maximum_fusion.10), channel_id=1, source_target_pairs={{0,4},{1,3},{2,6},{3,1},{4,0},{5,7},{6,2},{7,5},{8,12},{9,11},{10,... | collective-permute-start | bytes 2064392 | tf_op jit(solution)/shard_map/ppermute | solution.py:140
  205.8 19.3 %collective-permute-start.13 = (bf16[8,96,896]{2,1,0:T(8,128)(2,1)S(1)}, bf16[8,96,896]{2,1,0:T(8,128)(2,1)S(1)}, u32[]{:S(2)}, u32[]{:S(2)}) collective-permute-start(bf16[8,96,896]{2,1,0:T(8,128)(2,1)S(1)} %pad_maximum_fusion.5.near), channel_id=1, source_target_pairs={{0,2},{1,5},{2,0},{3,7},{4,6},{5,1},{6,4},{7,3},{8,10},{9,13},{10,... | collective-permute-start | bytes 4128776 | tf_op jit(solution)/shard_map/ppermute | solution.py:140
  208.5 16.6 %collective-permute-start.11 = (bf16[2,4,3,96,128]{4,3,2,1,0:T(8,128)(2,1)}, bf16[2,4,3,96,128]{4,3,2,1,0:T(8,128)(2,1)}, u32[]{:S(2)}, u32[]{:S(2)}) collective-permute-start(bf16[2,4,3,96,128]{4,3,2,1,0:T(8,128)(2,1)} %pad_maximum_fusion.13), channel_id=1, source_target_pairs={{0,4},{2,6},{4,0},{6,2},{8,12},{10,14},{12,8},{14,10},{16,20},{18,... | collective-permute-start | bytes 1769480 | tf_op jit(solution)/shard_map/ppermute | solution.py:112
  232.4 13.4 %collective-permute-start.14 = (bf16[256,1536]{1,0:T(8,128)(2,1)}, bf16[256,1536]{1,0:T(8,128)(2,1)}, u32[]{:S(2)}, u32[]{:S(2)}) collective-permute-start(bf16[256,1536]{1,0:T(8,128)(2,1)} %get-tuple-element.66), channel_id=1, source_target_pairs={{0,1},{1,0},{2,3},{3,2},{4,5},{5,4},{6,7},{7,6},{8,9},{9,8},{10,11... | collective-permute-start | bytes 2359304 | tf_op jit(solution)/shard_map/ppermute | solution.py:131
  245.8 40.3 %collective-permute-start.18 = (bf16[3,1536,128]{1,2,0:T(8,128)(2,1)}, bf16[3,1536,128]{1,2,0:T(8,128)(2,1)S(1)}, u32[]{:S(2)}, u32[]{:S(2)}) collective-permute-start(bf16[3,1536,128]{1,2,0:T(8,128)(2,1)} %copy.128), channel_id=1, source_target_pairs={{0,1},{1,0},{2,3},{3,2},{4,5},{5,4},{6,7},{7,6},{8,9},{9,8},{10,11... | collective-permute-start | bytes 3538952 | tf_op jit(solution)/shard_map/ppermute | solution.py:131
  247.8 20.0 %collective-permute-start.15 = (bf16[256,1536]{1,0:T(8,128)(2,1)S(1)}, bf16[256,1536]{1,0:T(8,128)(2,1)S(1)}, u32[]{:S(2)}, u32[]{:S(2)}) collective-permute-start(bf16[256,1536]{1,0:T(8,128)(2,1)S(1)} %multiply_convert_fusion), channel_id=1, source_target_pairs={{0,2},{2,0},{4,6},{6,4},{8,10},{10,8},{12,14},{14,12},{16,18},{18,... | collective-permute-start | bytes 2359304 | tf_op jit(solution)/shard_map/ppermute | solution.py:112
  249.3 20.4 %collective-permute-start.16 = (bf16[256,1536]{1,0:T(8,128)(2,1)S(1)}, bf16[256,1536]{1,0:T(8,128)(2,1)S(1)}, u32[]{:S(2)}, u32[]{:S(2)}) collective-permute-start(bf16[256,1536]{1,0:T(8,128)(2,1)S(1)} %multiply_convert_fusion), channel_id=1, source_target_pairs={{0,8},{2,10},{4,12},{6,14},{8,0},{10,2},{12,4},{14,6},{16,24},{18,... | collective-permute-start | bytes 2359304 | tf_op jit(solution)/shard_map/ppermute | solution.py:112
  249.3 36.5 %collective-permute-start.17 = (bf16[256,1536]{1,0:T(8,128)(2,1)S(1)}, bf16[256,1536]{1,0:T(8,128)(2,1)S(1)}, u32[]{:S(2)}, u32[]{:S(2)}) collective-permute-start(bf16[256,1536]{1,0:T(8,128)(2,1)S(1)} %multiply_convert_fusion), channel_id=1, source_target_pairs={{0,10},{2,8},{4,14},{6,12},{8,2},{10,0},{12,6},{14,4},{16,26},{18,... | collective-permute-start | bytes 2359304 | tf_op jit(solution)/shard_map/ppermute | solution.py:112
  327.8 19.6 %collective-permute-start.19 = (bf16[256,1536]{1,0:T(8,128)(2,1)S(1)}, bf16[256,1536]{1,0:T(8,128)(2,1)S(1)}, u32[]{:S(2)}, u32[]{:S(2)}) collective-permute-start(bf16[256,1536]{1,0:T(8,128)(2,1)S(1)} %get-tuple-element.180), channel_id=1, source_target_pairs={{0,2},{2,0},{4,6},{6,4},{8,10},{10,8},{12,14},{14,12},{16,18},{18,... | collective-permute-start | bytes 2359304 | tf_op jit(solution)/shard_map/ppermute | solution.py:112
  329.3 20.5 %collective-permute-start.20 = (bf16[256,1536]{1,0:T(8,128)(2,1)S(1)}, bf16[256,1536]{1,0:T(8,128)(2,1)S(1)}, u32[]{:S(2)}, u32[]{:S(2)}) collective-permute-start(bf16[256,1536]{1,0:T(8,128)(2,1)S(1)} %get-tuple-element.182), channel_id=1, source_target_pairs={{0,8},{2,10},{4,12},{6,14},{8,0},{10,2},{12,4},{14,6},{16,24},{18,... | collective-permute-start | bytes 2359304 | tf_op jit(solution)/shard_map/ppermute | solution.py:112
  329.6 35.1 %collective-permute-start.21 = (bf16[256,1536]{1,0:T(8,128)(2,1)S(1)}, bf16[256,1536]{1,0:T(8,128)(2,1)S(1)}, u32[]{:S(2)}, u32[]{:S(2)}) collective-permute-start(bf16[256,1536]{1,0:T(8,128)(2,1)S(1)} %get-tuple-element.181), channel_id=1, source_target_pairs={{0,10},{2,8},{4,14},{6,12},{8,2},{10,0},{12,6},{14,4},{16,26},{18,... | collective-permute-start | bytes 2359304 | tf_op jit(solution)/shard_map/ppermute | solution.py:112
  367.5 19.6 %collective-permute-start.22 = (bf16[256,1536]{1,0:T(8,128)(2,1)S(1)}, bf16[256,1536]{1,0:T(8,128)(2,1)S(1)}, u32[]{:S(2)}, u32[]{:S(2)}) collective-permute-start(bf16[256,1536]{1,0:T(8,128)(2,1)S(1)} %fusion.85), channel_id=1, source_target_pairs={{0,2},{2,0},{4,6},{6,4},{8,10},{10,8},{12,14},{14,12},{16,18},{18,... | collective-permute-start | bytes 2359304 | tf_op jit(solution)/shard_map/ppermute | solution.py:112
  369.0 20.5 %collective-permute-start.23 = (bf16[256,1536]{1,0:T(8,128)(2,1)S(1)}, bf16[256,1536]{1,0:T(8,128)(2,1)S(1)}, u32[]{:S(2)}, u32[]{:S(2)}) collective-permute-start(bf16[256,1536]{1,0:T(8,128)(2,1)S(1)} %fusion.85), channel_id=1, source_target_pairs={{0,8},{2,10},{4,12},{6,14},{8,0},{10,2},{12,4},{14,6},{16,24},{18,... | collective-permute-start | bytes 2359304 | tf_op jit(solution)/shard_map/ppermute | solution.py:112
  369.6 33.6 %collective-permute-start.24 = (bf16[256,1536]{1,0:T(8,128)(2,1)S(1)}, bf16[256,1536]{1,0:T(8,128)(2,1)S(1)}, u32[]{:S(2)}, u32[]{:S(2)}) collective-permute-start(bf16[256,1536]{1,0:T(8,128)(2,1)S(1)} %fusion.85), channel_id=1, source_target_pairs={{0,10},{2,8},{4,14},{6,12},{8,2},{10,0},{12,6},{14,4},{16,26},{18,... | collective-permute-start | bytes 2359304 | tf_op jit(solution)/shard_map/ppermute | solution.py:112
  468.4 22.5 %collective-permute-start.27 = (bf16[272,1536]{1,0:T(8,128)(2,1)S(1)}, bf16[272,1536]{1,0:T(8,128)(2,1)S(1)}, u32[]{:S(2)}, u32[]{:S(2)}) collective-permute-start(bf16[272,1536]{1,0:T(8,128)(2,1)S(1)} %get-tuple-element.175), channel_id=1, source_target_pairs={{0,10},{2,8},{4,14},{6,12},{8,2},{10,0},{12,6},{14,4},{16,26},{18,... | collective-permute-start | bytes 2506760 | tf_op jit(solution)/shard_map/ppermute | solution.py:112
  470.3 35.8 %collective-permute-start.26 = (bf16[272,1536]{1,0:T(8,128)(2,1)S(1)}, bf16[272,1536]{1,0:T(8,128)(2,1)S(1)}, u32[]{:S(2)}, u32[]{:S(2)}) collective-permute-start(bf16[272,1536]{1,0:T(8,128)(2,1)S(1)} %get-tuple-element.176), channel_id=1, source_target_pairs={{0,8},{2,10},{4,12},{6,14},{8,0},{10,2},{12,4},{14,6},{16,24},{18,... | collective-permute-start | bytes 2506760 | tf_op jit(solution)/shard_map/ppermute | solution.py:112
  471.4 34.7 %collective-permute-start.25 = (bf16[272,1536]{1,0:T(8,128)(2,1)S(1)}, bf16[272,1536]{1,0:T(8,128)(2,1)S(1)}, u32[]{:S(2)}, u32[]{:S(2)}) collective-permute-start(bf16[272,1536]{1,0:T(8,128)(2,1)S(1)} %get-tuple-element.177), channel_id=1, source_target_pairs={{0,2},{2,0},{4,6},{6,4},{8,10},{10,8},{12,14},{14,12},{16,18},{18,... | collective-permute-start | bytes 2506760 | tf_op jit(solution)/shard_map/ppermute | solution.py:112
  506.5 8.6 %collective-permute-start.29 = (bf16[1536,16]{0,1:T(8,128)(2,1)S(1)}, bf16[1536,16]{0,1:T(8,128)(2,1)S(1)}, u32[]{:S(2)}, u32[]{:S(2)}) collective-permute-start(bf16[1536,16]{0,1:T(8,128)(2,1)S(1)} %get-tuple-element.215), channel_id=1, source_target_pairs={{0,1},{1,0},{2,3},{3,2},{4,5},{5,4},{6,7},{7,6},{8,9},{9,8},{10,11... | collective-permute-start | bytes 147464 | tf_op jit(solution)/shard_map/ppermute | solution.py:131
  511.2 7.3 %collective-permute-start.28 = (bf16[256,1536]{1,0:T(8,128)(2,1)}, bf16[256,1536]{1,0:T(8,128)(2,1)}, u32[]{:S(2)}, u32[]{:S(2)}) collective-permute-start(bf16[256,1536]{1,0:T(8,128)(2,1)} %get-tuple-element.168.own), channel_id=1, source_target_pairs={{0,1},{1,0},{2,3},{3,2},{4,5},{5,4},{6,7},{7,6},{8,9},{9,8},{10,11... | collective-permute-start | bytes 2359304 | tf_op jit(solution)/shard_map/ppermute | solution.py:131
  526.5 32.9 %collective-permute-start.31 = (bf16[8,96,896]{2,1,0:T(8,128)(2,1)}, bf16[8,96,896]{2,1,0:T(8,128)(2,1)}, u32[]{:S(2)}, u32[]{:S(2)}) collective-permute-start(bf16[8,96,896]{2,1,0:T(8,128)(2,1)} %get-tuple-element.80), channel_id=1, source_target_pairs={{0,2},{2,0},{4,6},{6,4},{8,10},{10,8},{12,14},{14,12},{16,18},{18,... | collective-permute-start | bytes 4128776 | tf_op jit(solution)/shard_map/ppermute | solution.py:112
  527.7 31.9 %collective-permute-start.44 = (bf16[3,1536,128]{1,2,0:T(8,128)(2,1)}, bf16[3,1536,128]{1,2,0:T(8,128)(2,1)}, u32[]{:S(2)}, u32[]{:S(2)}) collective-permute-start(bf16[3,1536,128]{1,2,0:T(8,128)(2,1)} %fusion.6), channel_id=1, source_target_pairs={{0,1},{1,0},{2,3},{3,2},{4,5},{5,4},{6,7},{7,6},{8,9},{9,8},{10,11... | collective-permute-start | bytes 3538952 | tf_op jit(solution)/shard_map/ppermute | solution.py:131
  551.5 14.9 %collective-permute-start.30 = (bf16[256,1536]{1,0:T(8,128)(2,1)}, bf16[256,1536]{1,0:T(8,128)(2,1)}, u32[]{:S(2)}, u32[]{:S(2)}) collective-permute-start(bf16[256,1536]{1,0:T(8,128)(2,1)} %get-tuple-element.78), channel_id=1, source_target_pairs={{0,1},{1,0},{2,3},{3,2},{4,5},{5,4},{6,7},{7,6},{8,9},{9,8},{10,11... | collective-permute-start | bytes 2359304 | tf_op jit(solution)/shard_map/ppermute | solution.py:131
  559.4 44.7 %collective-permute-start.32 = (bf16[8,96,1280]{2,1,0:T(8,128)(2,1)}, bf16[8,96,1280]{2,1,0:T(8,128)(2,1)}, u32[]{:S(2)}, u32[]{:S(2)}) collective-permute-start(bf16[8,96,1280]{2,1,0:T(8,128)(2,1)} %get-tuple-element.82), channel_id=1, source_target_pairs={{0,2},{2,0},{4,6},{6,4},{8,10},{10,8},{12,14},{14,12},{16,18},{18,... | collective-permute-start | bytes 5898248 | tf_op jit(solution)/shard_map/ppermute | solution.py:112
  565.0 49.9 %collective-permute-start.45 = (bf16[2,4,3,96,128]{4,3,2,1,0:T(8,128)(2,1)S(1)}, bf16[2,4,3,96,128]{4,3,2,1,0:T(8,128)(2,1)S(1)}, u32[]{:S(2)}, u32[]{:S(2)}) collective-permute-start(bf16[2,4,3,96,128]{4,3,2,1,0:T(8,128)(2,1)S(1)} %pad_maximum_fusion.14), channel_id=1, source_target_pairs={{0,4},{2,6},{4,0},{6,2},{8,12},{10,14},{12,8},{14,10},{16,20},{18,... | collective-permute-start | bytes 1769480 | tf_op jit(solution)/shard_map/ppermute | solution.py:112
  573.3 41.4 %collective-permute-start.41 = (bf16[4,96,896]{2,1,0:T(8,128)(2,1)S(1)}, bf16[4,96,896]{2,1,0:T(8,128)(2,1)S(1)}, u32[]{:S(2)}, u32[]{:S(2)}) collective-permute-start(bf16[4,96,896]{2,1,0:T(8,128)(2,1)S(1)} %slice.480), channel_id=1, source_target_pairs={{0,4},{2,6},{4,0},{6,2},{8,12},{10,14},{12,8},{14,10},{16,20},{18,... | collective-permute-start | bytes 2064392 | tf_op jit(solution)/shard_map/ppermute | solution.py:112
  606.2 41.0 %collective-permute-start.34 = (bf16[4,96,1280]{2,1,0:T(8,128)(2,1)S(1)}, bf16[4,96,1280]{2,1,0:T(8,128)(2,1)S(1)}, u32[]{:S(2)}, u32[]{:S(2)}) collective-permute-start(bf16[4,96,1280]{2,1,0:T(8,128)(2,1)S(1)} %slice.479), channel_id=1, source_target_pairs={{0,4},{2,6},{4,0},{6,2},{8,12},{10,14},{12,8},{14,10},{16,20},{18,... | collective-permute-start | bytes 2949128 | tf_op jit(solution)/shard_map/ppermute | solution.py:112
  614.8 48.0 %collective-permute-start.42 = (bf16[2,96,896]{2,1,0:T(8,128)(2,1)S(1)}, bf16[2,96,896]{2,1,0:T(8,128)(2,1)S(1)}, u32[]{:S(2)}, u32[]{:S(2)}) collective-permute-start(bf16[2,96,896]{2,1,0:T(8,128)(2,1)S(1)} %slice.482), channel_id=1, source_target_pairs={{0,8},{2,10},{4,12},{6,14},{8,0},{10,2},{12,4},{14,6},{16,24},{18,... | collective-permute-start | bytes 1032200 | tf_op jit(solution)/shard_map/ppermute | solution.py:112
  616.7 46.0 %collective-permute-start.46 = (bf16[4,3,96,128]{3,2,1,0:T(8,128)(2,1)S(1)}, bf16[4,3,96,128]{3,2,1,0:T(8,128)(2,1)S(1)}, u32[]{:S(2)}, u32[]{:S(2)}) collective-permute-start(bf16[4,3,96,128]{3,2,1,0:T(8,128)(2,1)S(1)} %fusion.50), channel_id=1, source_target_pairs={{0,16},{2,18},{4,20},{6,22},{8,24},{10,26},{12,28},{14,30},{16,0},... | collective-permute-start | bytes 884744 | tf_op jit(solution)/shard_map/ppermute | solution.py:112
  647.5 19.2 %collective-permute-start.36 = (bf16[2,96,1280]{2,1,0:T(8,128)(2,1)S(1)}, bf16[2,96,1280]{2,1,0:T(8,128)(2,1)S(1)}, u32[]{:S(2)}, u32[]{:S(2)}) collective-permute-start(bf16[2,96,1280]{2,1,0:T(8,128)(2,1)S(1)} %slice.481), channel_id=1, source_target_pairs={{0,8},{2,10},{4,12},{6,14},{8,0},{10,2},{12,4},{14,6},{16,24},{18,... | collective-permute-start | bytes 1474568 | tf_op jit(solution)/shard_map/ppermute | solution.py:112
  663.0 12.9 %collective-permute-start.43 = (bf16[1,96,896]{2,1,0:T(8,128)(2,1)S(1)}, bf16[1,96,896]{2,1,0:T(8,128)(2,1)S(1)}, u32[]{:S(2)}, u32[]{:S(2)}) collective-permute-start(bf16[1,96,896]{2,1,0:T(8,128)(2,1)S(1)} %slice.484), channel_id=1, source_target_pairs={{0,16},{2,18},{4,20},{6,22},{8,24},{10,26},{12,28},{14,30},{16,0},... | collective-permute-start | bytes 516104 | tf_op jit(solution)/shard_map/ppermute | solution.py:112
  666.8 15.8 %collective-permute-start.47 = (bf16[3,96,128]{2,1,0:T(8,128)(2,1)S(1)}, bf16[3,96,128]{2,1,0:T(8,128)(2,1)S(1)}, u32[]{:S(2)}, u32[]{:S(2)}) collective-permute-start(bf16[3,96,128]{2,1,0:T(8,128)(2,1)S(1)} %get-tuple-element.193), channel_id=1, source_target_pairs={{0,2},{2,0},{4,6},{6,4},{8,10},{10,8},{12,14},{14,12},{16,18},{18,... | collective-permute-start | bytes 221192 | tf_op jit(solution)/shard_map/ppermute | solution.py:112
  675.9 6.6 collective-permute-start.37
  676.9 7.5 %collective-permute-start.48 = (bf16[3,96,128]{2,1,0:T(8,128)(2,1)S(1)}, bf16[3,96,128]{2,1,0:T(8,128)(2,1)S(1)}, u32[]{:S(2)}, u32[]{:S(2)}) collective-permute-start(bf16[3,96,128]{2,1,0:T(8,128)(2,1)S(1)} %get-tuple-element.192), channel_id=1, source_target_pairs={{0,8},{2,10},{4,12},{6,14},{8,0},{10,2},{12,4},{14,6},{16,24},{18,... | collective-permute-start | bytes 221192 | tf_op jit(solution)/shard_map/ppermute | solution.py:112
  678.9 8.6 %collective-permute-start.49 = (bf16[3,96,128]{2,1,0:T(8,128)(2,1)S(1)}, bf16[3,96,128]{2,1,0:T(8,128)(2,1)S(1)}, u32[]{:S(2)}, u32[]{:S(2)}) collective-permute-start(bf16[3,96,128]{2,1,0:T(8,128)(2,1)S(1)} %get-tuple-element.191), channel_id=1, source_target_pairs={{0,10},{2,8},{4,14},{6,12},{8,2},{10,0},{12,6},{14,4},{16,26},{18,... | collective-permute-start | bytes 221192 | tf_op jit(solution)/shard_map/ppermute | solution.py:112
  679.7 18.1 %collective-permute-start.38 = (bf16[1,96,1280]{2,1,0:T(8,128)(2,1)S(1)}, bf16[1,96,1280]{2,1,0:T(8,128)(2,1)S(1)}, u32[]{:S(2)}, u32[]{:S(2)}) collective-permute-start(bf16[1,96,1280]{2,1,0:T(8,128)(2,1)S(1)} %slice.483), channel_id=1, source_target_pairs={{0,16},{2,18},{4,20},{6,22},{8,24},{10,26},{12,28},{14,30},{16,0},... | collective-permute-start | bytes 737288 | tf_op jit(solution)/shard_map/ppermute | solution.py:112
  (60 other events, 864.7 us)
Sparse Core Ops, SparseCore 0:
  10.7 204.8 all-gather.2
  465.6 234.0 reduce-scatter.1

commit v3 on v2

--- a/solution.py
+++ b/solution.py
@@ -74,7 +74,7 @@
         held = jnp.concatenate(self.halves, axis=0)
         if others:
             held = behind(held, *others)
-        self.marks.append(self.lay.shift_step(held, self.lay.steps[len(self.marks)]))
+        self.marks.append(self.lay.shift(held, 1 << self.lay.tree_bits[len(self.marks)]))
         self.halves = (held, self.marks[-1])
         return self.marks[-1]
 
@@ -84,7 +84,7 @@
         self.lay, (self.keep, self.send), self.marks = lay, halves, []
 
     def step(self, *others):
-        got = self.lay.shift(self.send, 1 << self.lay.back_bits[-1 - len(self.marks)])
+        got = self.lay.shift(self.send, 1 << self.lay.tree_bits[-1 - len(self.marks)])
         if others:
             got = behind(got, *others)
         self.marks.append(got)
@@ -105,8 +105,7 @@
         self.g_bits = [bit for bit in range(bits) if bit not in self.w_bits]
         self.w_masks = subset_masks(self.w_bits)
         self.g_masks = subset_masks(self.g_bits)
-        self.steps = [(bit, bit) for bit in range(bits - 1, 1, -1)] + [(1, 0), (0, 1)]
-        self.back_bits = list(range(bits - 1, -1, -1))
+        self.tree_bits = list(range(bits - 1, -1, -1))
 
     def shift(self, values, mask):
         return lax.ppermute(values, "dp", [(i, i ^ mask) for i in range(self.dp)])
@@ -130,35 +129,18 @@
     def shift_core(self, values, mask):
         return lax.ppermute(values, "tensor", [(i, i ^ mask) for i in range(self.tp)])
 
-    def shift_step(self, values, step):
-        even, odd = step
-        pairs = []
-        for i in range(self.dp):
-            for c in range(self.tp):
-                target = i ^ (1 << (odd if c % 2 else even))
-                pairs.append((i * self.tp + c, target * self.tp + c))
-        return lax.ppermute(values, ("dp", "tensor"), pairs)
-
-    def step_bit(self, step):
-        even, odd = step
-        return even if even == odd else jnp.where(self.core % 2 == 1, odd, even)
-
-    def gather_order(self):
+    def tree_order(self):
         apart = self.place ^ jnp.arange(self.dp)
-        return sum(((apart >> self.step_bit(step)) & 1) << k for k, step in enumerate(self.steps))
-
-    def scatter_order(self):
-        apart = self.place ^ jnp.arange(self.dp)
-        return sum(((apart >> bit) & 1) << k for k, bit in enumerate(self.back_bits))
+        return sum(((apart >> bit) & 1) << k for k, bit in enumerate(self.tree_bits))
 
     def in_order(self, halves):
-        whole = jnp.concatenate(halves, axis=0)[self.gather_order()]
+        whole = jnp.concatenate(halves, axis=0)[self.tree_order()]
         return whole.reshape((-1,) + whole.shape[2:])
 
     def in_halves(self, whole):
         blocks = whole.astype(bf16).reshape((self.dp, -1) + whole.shape[1:])
         rel = jnp.arange(self.dp)
-        apart = sum(((rel >> k) & 1) << bit for k, bit in enumerate(self.back_bits))
+        apart = sum(((rel >> k) & 1) << bit for k, bit in enumerate(self.tree_bits))
         at = self.place ^ apart
         return blocks[at[: self.dp // 2]], blocks[at[self.dp // 2 :]]
 
@@ -670,9 +652,11 @@
                     copy.wait()
 
         for c in range(cores):
-            for s in range(2):
-                fresh[c, s] = dot_rows(work[0], pres[c][s]).astype(bf16)
-            fresh[c, 2] = dot_rows(mine, acts[c]).astype(bf16)
+            both = dot_rows(work[0], jnp.concatenate(pres[c], axis=1)).astype(bf16)
+            fresh[c, 0], fresh[c, 1] = both[:, :hidden], both[:, hidden:]
+        both = dot_rows(mine, jnp.concatenate(acts, axis=1)).astype(bf16)
+        for c in range(cores):
+            fresh[c, 2] = both[:, c * hidden : (c + 1) * hidden]
         for k in range(held):
 
             @pl.when(step == k)
@@ -823,26 +807,24 @@
     qkv = Tree(lay, jnp.concatenate([w_query, key_value_weight[0], key_value_weight[1]], axis=1))
     router_pad = jnp.zeros((w_router.shape[0], -experts % 128), bf16)
     out = Tree(lay, jnp.concatenate([w_out, w_router, router_pad], axis=1))
-    expert_shares = lax.all_gather(
-        jnp.concatenate([w_expert_in[0], w_expert_out], axis=0),
-        ("dp", "tensor"),
-        axis_index_groups=lay.w_groups(),
-    )
-    steps = len(lay.steps)
+    steps = len(lay.tree_bits)
     qkv.step()
     out.step(qkv.marks[0])
     qkv.step(shared_parts, input_slices, group_member)
-    shared_far = lay.shift(behind(shared_parts, out.marks[0]), far)
     out.step(qkv.marks[1])
     for k in range(2, steps):
-        gates = [out.marks[min(k - 2, 1)]] + ([shared_far] if k == steps - 1 else [])
-        qkv.step(*gates)
-    for k in range(2, steps):
-        out.step(qkv.marks[-1])
-    shared_near = lay.shift(behind(jnp.stack([shared_parts, shared_far]), qkv.marks[-1]), near)
+        qkv.step(out.marks[k - 2])
+        out.step(qkv.marks[k])
+    expert_shares = lax.all_gather(
+        behind(jnp.concatenate([w_expert_in[0], w_expert_out], axis=0), qkv.marks[2]),
+        ("dp", "tensor"),
+        axis_index_groups=lay.w_groups(),
+    )
+    shared_far = lay.shift(behind(shared_parts, qkv.marks[-2], out.marks[1]), far)
+    shared_near = lay.shift(behind(jnp.stack([shared_parts, shared_far]), out.marks[-2]), near)
 
     spot = jnp.stack([lay.core, length]).astype(jnp.int32)
-    in_order = lay.gather_order()
+    in_order = lay.tree_order()
     residual = block_input.astype(f32)
     _, scale_attn = normalize_rows(residual, gain_attn)
 
@@ -854,7 +836,7 @@
             in_order, spot, *input_slices, gain_attn, qkv.halves, head_count, kv_count
         )
         *attn_parts, out_router = project_out(
-            behind(in_order, shared_near), mixed_heads, out.halves
+            in_order, mixed_heads, out.halves
         )
     else:
         qkv_full, out_router = lay.in_order(qkv.halves), lay.in_order(out.halves)
@@ -957,10 +939,10 @@
     )
     if in_kernel:
         grad_mixed, *out_back_halves = project_out_back(
-            lay.scatter_order(), *grad_slices, out_router, mixed_heads, grad_router_part
+            lay.tree_order(), *grad_slices, out_router, mixed_heads, grad_router_part
         )
         grad_projected, *qkv_back_halves = attend_back(
-            lay.scatter_order(), spot, grad_mixed, normed_all, projected, logs, head_count, kv_count
+            lay.tree_order(), spot, grad_mixed, normed_all, projected, logs, head_count, kv_count
         )
         normed_parts = normed_back(in_order, grad_projected, qkv.halves)
     else:

time: 729 us -> 705 us (0.967)
  waiting for transfers between devices: 421 us -> 383 us
  starting transfers between devices: 60.4 us -> 70.1 us
    ppermute x8 -> x0, waiting for transfers between devices: 128 us -> none  [shift_step(): return lax.ppermute(values, ('dp', 'tensor'), pairs)]
    ppermute x34 -> x42, waiting for transfers between devices: 293 us -> 383 us  [shift(): return lax.ppermute(values, 'dp', [(i, i ^ mask) for i in range(self.dp)])]
    ppermute x34 -> x42, starting transfers between devices: 34.5 us -> 68.1 us  [shift(): return lax.ppermute(values, 'dp', [(i, i ^ mask) for i in range(self.dp)])]
    ppermute x8 -> x0, starting transfers between devices: 15.8 us -> none  [shift_step(): return lax.ppermute(values, ('dp', 'tensor'), pairs)]
    ppermute x8, starting transfers between devices: 10 us -> 1.96 us  [shift_core(): lax.ppermute(values, 'tensor', [(i, i ^ mask) for i in range(self.tp)])]
  transfers between devices with their start and end apart: 52 -> 52, of which waited for: 33 -> 35; matrix products, arithmetic and copies ran while one was open for 10% -> 11% of each run, Pallas kernels for 6% -> 7%
where the time goes in v3:
time: 705 us; the launch traced here: 696 us
  waiting for transfers between devices  383 us (54%)
  Pallas kernels  123 us (17%)
  starting transfers between devices  70.1 us (10%)
  other arithmetic  43.9 us (6%)
  local copies, waits for them, and re-layouts  31.1 us (4%)
  matrix products  26.4 us (4%)
  between operations  18.8 us (3%)
    ppermute x42, waiting for transfers between devices, shift(): return lax.ppermute(values, 'dp', [(i, i ^ mask) for i in range(self.dp)])  383 us
    ppermute x42, starting transfers between devices, shift(): return lax.ppermute(values, 'dp', [(i, i ^ mask) for i in range(self.dp)])  68.1 us
    pallas_call x1, Pallas kernels, experts_backward(): pl.pallas_call(kernel, grid=(held,), in_specs=[scalars, whole, whole, pl....  53.3 us
    pallas_call x1, Pallas kernels, experts_forward(): pl.pallas_call(kernel, grid=(held,), in_specs=[scalars, whole, whole, pl....  24 us
  transfers between devices with their start and end apart: 52, of which 35 were waited for; matrix products, arithmetic and copies ran while one was open for 11% of the time, Pallas kernels for 7%

profile of v3, /device:TPU:0, one launch (start us, length us, event | category | flops | bytes accessed | tf_op | source)
XLA Modules:
  0.0 696.4 jit_solution(2889064076572915953)
XLA Ops:
  9.1 3.0 collective-permute-start.2
  13.7 3.1 collective-permute-start.1
  20.6 8.0 %collective-permute-done.1 = bf16[1,96,1280]{2,1,0:T(8,128)(2,1)S(1)} collective-permute-done((bf16[1,96,1280]{2,1,0:T(8,128)(2,1)S(1)}, bf16[1,96,1280]{2,1,0:T(8,128)(2,1)S(1)}, u32[]{:S(2)}, u32[]{:S(2)}) %collective-permute-start.1) | collective-permute-done | bytes 245792 | tf_op jit(solution)/shard_map/ppermute | solution.py:111
  31.4 3.4 collective-permute-start.6
  34.8 10.9 %collective-permute-done.5 = bf16[2,96,1280]{2,1,0:T(8,128)(2,1)} collective-permute-done((bf16[2,96,1280]{2,1,0:T(8,128)(2,1)S(1)}, bf16[2,96,1280]{2,1,0:T(8,128)(2,1)}, u32[]{:S(2)}, u32[]{:S(2)}) %collective-permute-start.5) | collective-permute-done | bytes 491552 | tf_op jit(solution)/shard_map/ppermute | solution.py:111
  48.2 2.8 pad_maximum_fusion.3
  51.0 18.7 %collective-permute-done.7 = bf16[4,96,1280]{2,1,0:T(8,128)(2,1)} collective-permute-done((bf16[4,96,1280]{2,1,0:T(8,128)(2,1)S(1)}, bf16[4,96,1280]{2,1,0:T(8,128)(2,1)}, u32[]{:S(2)}, u32[]{:S(2)}) %collective-permute-start.7) | collective-permute-done | bytes 983072 | tf_op jit(solution)/shard_map/ppermute | solution.py:111
  72.9 5.5 collective-permute-done.8
  81.6 28.3 %collective-permute-done.10 = bf16[4,96,896]{2,1,0:T(8,128)(2,1)S(1)} collective-permute-done((bf16[4,96,896]{2,1,0:T(8,128)(2,1)S(1)}, bf16[4,96,896]{2,1,0:T(8,128)(2,1)S(1)}, u32[]{:S(2)}, u32[]{:S(2)}) %collective-permute-start.10) | collective-permute-done | bytes 688160 | tf_op jit(solution)/shard_map/ppermute | solution.py:111
  110.0 11.0 %collective-permute-done.9.far = bf16[8,96,1280]{2,1,0:T(8,128)(2,1)S(1)} collective-permute-done((bf16[8,96,1280]{2,1,0:T(8,128)(2,1)S(1)}, bf16[8,96,1280]{2,1,0:T(8,128)(2,1)S(1)}, u32[]{:S(2)}, u32[]{:S(2)}) %collective-permute-start.9) | collective-permute-done | bytes 1966112 | tf_op jit(solution)/shard_map/ppermute | solution.py:111
  126.4 16.6 %collective-permute-done.16 = bf16[4,3,96,128]{3,2,1,0:T(8,128)(2,1)} collective-permute-done((bf16[4,3,96,128]{3,2,1,0:T(8,128)(2,1)}, bf16[4,3,96,128]{3,2,1,0:T(8,128)(2,1)}, u32[]{:S(2)}, u32[]{:S(2)}) %collective-permute-start.16) | collective-permute-done | bytes 294944 | tf_op jit(solution)/shard_map/ppermute | solution.py:111
  148.9 10.4 %shard_map.273 = (bf16[512,1536]{1,0:T(8,128)(2,1)}, bf16[512,1280]{1,0:T(8,128)(2,1)}, bf16[512,768]{1,0:T(8,128)(2,1)}, f32[6,512,1]{2,1,0:T(8,128)}) custom-call(s32[16]{0:T(128)} %shift-left_add_fusion.order, s32[2]{0:T(128)} %pad_add_fusion.1.spot, bf16[256,1536]{1,0:T(8,128)(2,1)} %own.1, bf16[256,1536]{1,0:T(8,128)(2,1)} %collective-permute-done.other, ...), custom_call_target="tpu_custom_call" | custom-call | tf_op jit(solution)/shard_map/pallas_call | solution.py:311
  159.4 6.3 shard_map.274
  174.5 2.7 collective-permute-start.15
  178.8 14.4 %collective-permute-done.13 = bf16[256,1536]{1,0:T(8,128)(2,1)S(1)} collective-permute-done((bf16[256,1536]{1,0:T(8,128)(2,1)S(1)}, bf16[256,1536]{1,0:T(8,128)(2,1)S(1)}, u32[]{:S(2)}, u32[]{:S(2)}) %collective-permute-start.13) | collective-permute-done | bytes 786464 | tf_op jit(solution)/shard_map/ppermute | solution.py:111
  193.2 17.8 %collective-permute-done.14 = bf16[256,1536]{1,0:T(8,128)(2,1)S(1)} collective-permute-done((bf16[256,1536]{1,0:T(8,128)(2,1)S(1)}, bf16[256,1536]{1,0:T(8,128)(2,1)S(1)}, u32[]{:S(2)}, u32[]{:S(2)}) %collective-permute-start.14) | collective-permute-done | bytes 786464 | tf_op jit(solution)/shard_map/ppermute | solution.py:111
  211.0 49.8 %collective-permute-done.15 = bf16[256,1536]{1,0:T(8,128)(2,1)S(1)} collective-permute-done((bf16[256,1536]{1,0:T(8,128)(2,1)S(1)}, bf16[256,1536]{1,0:T(8,128)(2,1)S(1)}, u32[]{:S(2)}, u32[]{:S(2)}) %collective-permute-start.15) | collective-permute-done | bytes 786464 | tf_op jit(solution)/shard_map/ppermute | solution.py:111
  261.1 3.5 fusion.10
  271.9 4.9 fusion.46.init
  276.8 24.0 %shard_map.275 = (bf16[4,256,1536]{2,1,0:T(8,128)(2,1)}, bf16[4,512,1536]{2,1,0:T(8,128)(2,1)}, f32[4,2,2,512,256]{4,3,2,1,0:T(8,128)}) custom-call(s32[4,2]{1,0:T(4,128)} %pad_add_fusion.spots, f32[4,4,256]{2,1,0:T(4,128)} %convolution_select_fusion.1.position, f32[4,4,256]{2,1,0:T(4,128)} %reshape.239.gate, bf16[1024,1536]{1,0:T(8,128)(2,1)} %copy-done.2, ...), custom_call_target="tpu_custom_call" | custom-call | tf_op jit(solution)/shard_map/pallas_call | solution.py:569
  303.3 2.9 collective-permute-start.21
  307.0 15.4 %collective-permute-done.19 = bf16[256,1536]{1,0:T(8,128)(2,1)S(1)} collective-permute-done((bf16[256,1536]{1,0:T(8,128)(2,1)S(1)}, bf16[256,1536]{1,0:T(8,128)(2,1)S(1)}, u32[]{:S(2)}, u32[]{:S(2)}) %collective-permute-start.19) | collective-permute-done | bytes 786464 | tf_op jit(solution)/shard_map/ppermute | solution.py:111
  323.8 15.4 %collective-permute-done.21 = bf16[256,1536]{1,0:T(8,128)(2,1)S(1)} collective-permute-done((bf16[256,1536]{1,0:T(8,128)(2,1)S(1)}, bf16[256,1536]{1,0:T(8,128)(2,1)S(1)}, u32[]{:S(2)}, u32[]{:S(2)}) %collective-permute-start.21) | collective-permute-done | bytes 786464 | tf_op jit(solution)/shard_map/ppermute | solution.py:111
  339.2 2.6 multiply_reduce_fusion
  342.9 2.7 collective-permute-start.24
  345.6 16.1 %collective-permute-done.22 = bf16[256,1536]{1,0:T(8,128)(2,1)S(1)} collective-permute-done((bf16[256,1536]{1,0:T(8,128)(2,1)S(1)}, bf16[256,1536]{1,0:T(8,128)(2,1)S(1)}, u32[]{:S(2)}, u32[]{:S(2)}) %collective-permute-start.22) | collective-permute-done | bytes 786464 | tf_op jit(solution)/shard_map/ppermute | solution.py:111
  363.1 14.2 %collective-permute-done.24 = bf16[256,1536]{1,0:T(8,128)(2,1)S(1)} collective-permute-done((bf16[256,1536]{1,0:T(8,128)(2,1)S(1)}, bf16[256,1536]{1,0:T(8,128)(2,1)S(1)}, u32[]{:S(2)}, u32[]{:S(2)}) %collective-permute-start.24) | collective-permute-done | bytes 786464 | tf_op jit(solution)/shard_map/ppermute | solution.py:111
  380.1 6.0 fusion.24
  386.1 53.3 %shard_map.276 = (bf16[4,272,1536]{2,1,0:T(8,128)(2,1)}, bf16[8,3,1536,256]{3,2,1,0:T(8,128)(2,1)}) custom-call(s32[4,2]{1,0:T(4,128)} %pad_add_fusion.spots, f32[4,4,256]{2,1,0:T(4,128)} %convolution_select_fusion.1.position, f32[4,4,256]{2,1,0:T(4,128)} %reshape.239.gate, bf16[1024,1536]{1,0:T(8,128)(2,1)} %copy-done.8, ...), custom_call_target="tpu_custom_call" | custom-call | tf_op jit(solution)/shard_map/pallas_call | solution.py:681
  448.2 16.7 %collective-permute-done.27 = bf16[272,1536]{1,0:T(8,128)(2,1)S(1)} collective-permute-done((bf16[272,1536]{1,0:T(8,128)(2,1)S(1)}, bf16[272,1536]{1,0:T(8,128)(2,1)S(1)}, u32[]{:S(2)}, u32[]{:S(2)}) %collective-permute-start.27) | collective-permute-done | bytes 835616 | tf_op jit(solution)/shard_map/ppermute | solution.py:111
  464.9 12.5 %collective-permute-done.26 = bf16[272,1536]{1,0:T(8,128)(2,1)S(1)} collective-permute-done((bf16[272,1536]{1,0:T(8,128)(2,1)S(1)}, bf16[272,1536]{1,0:T(8,128)(2,1)S(1)}, u32[]{:S(2)}, u32[]{:S(2)}) %collective-permute-start.26) | collective-permute-done | bytes 835616 | tf_op jit(solution)/shard_map/ppermute | solution.py:111
  490.7 7.9 %shard_map.277 = (bf16[512,768]{1,0:T(8,128)(2,1)}, bf16[8,96,896]{2,1,0:T(8,128)(2,1)}, bf16[8,96,896]{2,1,0:T(8,128)(2,1)}) custom-call(s32[16]{0:T(128)} %shift-left_add_fusion.order, bf16[256,1536]{1,0:T(8,128)(2,1)} %get-tuple-element.168.own, bf16[256,1536]{1,0:T(8,128)(2,1)} %collective-permute-done.28.other, ...), custom_call_target="tpu_custom_call" | custom-call | tf_op jit(solution)/shard_map/pallas_call | solution.py:375
  503.0 13.8 %shard_map.278 = (bf16[512,1280]{1,0:T(8,128)(2,1)}, bf16[8,96,1280]{2,1,0:T(8,128)(2,1)}, bf16[8,96,1280]{2,1,0:T(8,128)(2,1)}) custom-call(s32[16]{0:T(128)} %shift-left_add_fusion.order, s32[2]{0:T(128)} %pad_add_fusion.1.spot, bf16[512,768]{1,0:T(8,128)(2,1)} %get-tuple-element.72.grad_mixed, bf16[512,1536]{1,0:T(8,128)(2,1)} %get-tuple-element.73.normed, ...), custom_call_target="tpu_custom_call" | custom-call | tf_op jit(solution)/shard_map/pallas_call | solution.py:419
  516.8 7.2 %shard_map.279 = (f32[256,1536]{1,0:T(8,128)}, bf16[256,1536]{1,0:T(8,128)(2,1)}) custom-call(s32[16]{0:T(128)} %shift-left_add_fusion.order, bf16[512,1280]{1,0:T(8,128)(2,1)} %get-tuple-element.76.grad_made, bf16[8,96,1280]{2,1,0:T(8,128)(2,1)} %copy-done.6, bf16[8,96,1280]{2,1,0:T(8,128)(2,1)} %copy-done.13), custom_call_target="tpu_custom_call" | custom-call | tf_op jit(solution)/shard_map/pallas_call | solution.py:445
  524.7 6.8 collective-permute-done.31
  532.5 2.8 fusion.5
  537.9 4.3 collective-permute-start.45
  544.3 3.0 fusion.22
  550.6 25.6 %collective-permute-done.32 = bf16[8,96,1280]{2,1,0:T(8,128)(2,1)} collective-permute-done((bf16[8,96,1280]{2,1,0:T(8,128)(2,1)}, bf16[8,96,1280]{2,1,0:T(8,128)(2,1)}, u32[]{:S(2)}, u32[]{:S(2)}) %collective-permute-start.32) | collective-permute-done | bytes 1966112 | tf_op jit(solution)/shard_map/ppermute | solution.py:111
  578.3 4.6 collective-permute-start.34
  583.0 7.3 %collective-permute-done.41 = bf16[4,96,896]{2,1,0:T(8,128)(2,1)S(1)} collective-permute-done((bf16[4,96,896]{2,1,0:T(8,128)(2,1)S(1)}, bf16[4,96,896]{2,1,0:T(8,128)(2,1)S(1)}, u32[]{:S(2)}, u32[]{:S(2)}) %collective-permute-start.41) | collective-permute-done | bytes 688160 | tf_op jit(solution)/shard_map/ppermute | solution.py:111
  594.4 30.5 %collective-permute-done.34 = bf16[4,96,1280]{2,1,0:T(8,128)(2,1)S(1)} collective-permute-done((bf16[4,96,1280]{2,1,0:T(8,128)(2,1)S(1)}, bf16[4,96,1280]{2,1,0:T(8,128)(2,1)S(1)}, u32[]{:S(2)}, u32[]{:S(2)}) %collective-permute-start.34) | collective-permute-done | bytes 983072 | tf_op jit(solution)/shard_map/ppermute | solution.py:111
  627.8 12.3 %collective-permute-start.35 = (f32[3,1536]{1,0:T(4,128)S(1)}, f32[3,1536]{1,0:T(4,128)S(1)}, u32[]{:S(2)}, u32[]{:S(2)}) collective-permute-start(f32[3,1536]{1,0:T(4,128)S(1)} %add.336), channel_id=1, source_target_pairs={{0,4},{2,6},{4,0},{6,2},{8,12},{10,14},{12,8},{14,10},{16,20},{18,... | collective-permute-start | bytes 55304 | tf_op jit(solution)/shard_map/ppermute | solution.py:111
  642.0 2.9 collective-permute-done.36
  645.8 7.7 %collective-permute-done.43 = bf16[1,96,896]{2,1,0:T(8,128)(2,1)S(1)} collective-permute-done((bf16[1,96,896]{2,1,0:T(8,128)(2,1)S(1)}, bf16[1,96,896]{2,1,0:T(8,128)(2,1)S(1)}, u32[]{:S(2)}, u32[]{:S(2)}) %collective-permute-start.43) | collective-permute-done | bytes 172064 | tf_op jit(solution)/shard_map/ppermute | solution.py:111
  660.2 5.0 collective-permute-done.49
  666.6 7.0 %collective-permute-done.38 = bf16[1,96,1280]{2,1,0:T(8,128)(2,1)S(1)} collective-permute-done((bf16[1,96,1280]{2,1,0:T(8,128)(2,1)S(1)}, bf16[1,96,1280]{2,1,0:T(8,128)(2,1)S(1)}, u32[]{:S(2)}, u32[]{:S(2)}) %collective-permute-start.38) | collective-permute-done | bytes 245792 | tf_op jit(solution)/shard_map/ppermute | solution.py:111
  673.7 4.6 collective-permute-done.39
  (320 shorter events, 121.6 us)
Async XLA Ops:
  7.2 269.5 %all-gather.3.cloned.1.call-start = ((), (), s32[]{:S(2)}) async-start(), calls=%async_computation.2 | async-start | bytes 21233664 | tf_op jit(solution)/shard_map/all_gather | solution.py:818
  9.1 7.7 %collective-permute-start.2 = (bf16[320,128]{1,0:T(8,128)(2,1)S(1)}, bf16[320,128]{1,0:T(8,128)(2,1)S(1)}, u32[]{:S(2)}, u32[]{:S(2)}) collective-permute-start(bf16[320,128]{1,0:T(8,128)(2,1)S(1)} %get-tuple-element.203), channel_id=1, source_target_pairs={{0,2},{2,0},{4,6},{6,4},{8,10},{10,8},{12,14},{14,12},{16,18},{18,... | collective-permute-start | bytes 245768 | tf_op jit(solution)/shard_map/ppermute | solution.py:111
  12.1 5.2 collective-permute-start.3
  13.6 5.3 collective-permute-start.4
  13.7 15.1 %collective-permute-start = (bf16[256,1536]{1,0:T(8,128)(2,1)S(1)}, bf16[256,1536]{1,0:T(8,128)(2,1)}, u32[]{:S(2)}, u32[]{:S(2)}) collective-permute-start(bf16[256,1536]{1,0:T(8,128)(2,1)S(1)} %copy-done.10), channel_id=1, source_target_pairs={{0,1},{1,0},{2,3},{3,2},{4,5},{5,4},{6,7},{7,6},{8,9},{9,8},{10,11... | collective-permute-start | bytes 2359304 | tf_op jit(solution)/shard_map/ppermute | solution.py:130
  13.7 14.9 %collective-permute-start.1 = (bf16[1,96,1280]{2,1,0:T(8,128)(2,1)S(1)}, bf16[1,96,1280]{2,1,0:T(8,128)(2,1)S(1)}, u32[]{:S(2)}, u32[]{:S(2)}) collective-permute-start(bf16[1,96,1280]{2,1,0:T(8,128)(2,1)S(1)} %maximum_bitcast_fusion), channel_id=1, source_target_pairs={{0,16},{2,18},{4,20},{6,22},{8,24},{10,26},{12,28},{14,30},{16,0},... | collective-permute-start | bytes 737288 | tf_op jit(solution)/shard_map/ppermute | solution.py:111
  28.7 16.9 %collective-permute-start.5 = (bf16[2,96,1280]{2,1,0:T(8,128)(2,1)S(1)}, bf16[2,96,1280]{2,1,0:T(8,128)(2,1)}, u32[]{:S(2)}, u32[]{:S(2)}) collective-permute-start(bf16[2,96,1280]{2,1,0:T(8,128)(2,1)S(1)} %pad_maximum_fusion.15), channel_id=1, source_target_pairs={{0,8},{2,10},{4,12},{6,14},{8,0},{10,2},{12,4},{14,6},{16,24},{18,... | collective-permute-start | bytes 1474568 | tf_op jit(solution)/shard_map/ppermute | solution.py:111
  31.4 15.4 %collective-permute-start.6 = (bf16[1,96,896]{2,1,0:T(8,128)(2,1)S(1)}, bf16[1,96,896]{2,1,0:T(8,128)(2,1)S(1)}, u32[]{:S(2)}, u32[]{:S(2)}) collective-permute-start(bf16[1,96,896]{2,1,0:T(8,128)(2,1)S(1)} %maximum_bitcast_fusion.1), channel_id=1, source_target_pairs={{0,16},{2,18},{4,20},{6,22},{8,24},{10,26},{12,28},{14,30},{16,0},... | collective-permute-start | bytes 516104 | tf_op jit(solution)/shard_map/ppermute | solution.py:111
  46.8 22.9 %collective-permute-start.7 = (bf16[4,96,1280]{2,1,0:T(8,128)(2,1)S(1)}, bf16[4,96,1280]{2,1,0:T(8,128)(2,1)}, u32[]{:S(2)}, u32[]{:S(2)}) collective-permute-start(bf16[4,96,1280]{2,1,0:T(8,128)(2,1)S(1)} %pad_maximum_fusion.8), channel_id=1, source_target_pairs={{0,4},{2,6},{4,0},{6,2},{8,12},{10,14},{12,8},{14,10},{16,20},{18,... | collective-permute-start | bytes 2949128 | tf_op jit(solution)/shard_map/ppermute | solution.py:111
  69.7 612.0 %reduce-scatter.2.cloned.1.call-start = ((), (), s32[]{:S(2)}) async-start(), calls=%async_computation.1 | async-start | bytes 21233664 | tf_op jit(solution)/shard_map/reduce_scatter | solution.py:912
  69.8 8.6 %collective-permute-start.8 = (bf16[2,96,896]{2,1,0:T(8,128)(2,1)S(1)}, bf16[2,96,896]{2,1,0:T(8,128)(2,1)S(1)}, u32[]{:S(2)}, u32[]{:S(2)}) collective-permute-start(bf16[2,96,896]{2,1,0:T(8,128)(2,1)S(1)} %pad_maximum_fusion.16), channel_id=1, source_target_pairs={{0,8},{2,10},{4,12},{6,14},{8,0},{10,2},{12,4},{14,6},{16,24},{18,... | collective-permute-start | bytes 1032200 | tf_op jit(solution)/shard_map/ppermute | solution.py:111
  78.4 42.6 %collective-permute-start.9 = (bf16[8,96,1280]{2,1,0:T(8,128)(2,1)S(1)}, bf16[8,96,1280]{2,1,0:T(8,128)(2,1)S(1)}, u32[]{:S(2)}, u32[]{:S(2)}) collective-permute-start(bf16[8,96,1280]{2,1,0:T(8,128)(2,1)S(1)} %pad_maximum_fusion.4.near), channel_id=1, source_target_pairs={{0,2},{2,0},{4,6},{6,4},{8,10},{10,8},{12,14},{14,12},{16,18},{18,... | collective-permute-start | bytes 5898248 | tf_op jit(solution)/shard_map/ppermute | solution.py:111
  80.0 29.9 %collective-permute-start.10 = (bf16[4,96,896]{2,1,0:T(8,128)(2,1)S(1)}, bf16[4,96,896]{2,1,0:T(8,128)(2,1)S(1)}, u32[]{:S(2)}, u32[]{:S(2)}) collective-permute-start(bf16[4,96,896]{2,1,0:T(8,128)(2,1)S(1)} %pad_maximum_fusion.10), channel_id=1, source_target_pairs={{0,4},{2,6},{4,0},{6,2},{8,12},{10,14},{12,8},{14,10},{16,20},{18,... | collective-permute-start | bytes 2064392 | tf_op jit(solution)/shard_map/ppermute | solution.py:111
  121.0 38.3 %collective-permute-start.11 = (bf16[8,96,896]{2,1,0:T(8,128)(2,1)S(1)}, bf16[8,96,896]{2,1,0:T(8,128)(2,1)}, u32[]{:S(2)}, u32[]{:S(2)}) collective-permute-start(bf16[8,96,896]{2,1,0:T(8,128)(2,1)S(1)} %pad_maximum_fusion.5.near), channel_id=1, source_target_pairs={{0,2},{2,0},{4,6},{6,4},{8,10},{10,8},{12,14},{14,12},{16,18},{18,... | collective-permute-start | bytes 4128776 | tf_op jit(solution)/shard_map/ppermute | solution.py:111
  122.8 20.2 %collective-permute-start.16 = (bf16[4,3,96,128]{3,2,1,0:T(8,128)(2,1)}, bf16[4,3,96,128]{3,2,1,0:T(8,128)(2,1)}, u32[]{:S(2)}, u32[]{:S(2)}) collective-permute-start(bf16[4,3,96,128]{3,2,1,0:T(8,128)(2,1)} %get-tuple-element.66), channel_id=1, source_target_pairs={{0,16},{2,18},{4,20},{6,22},{8,24},{10,26},{12,28},{14,30},{16,0},... | collective-permute-start | bytes 884744 | tf_op jit(solution)/shard_map/ppermute | solution.py:111
  144.9 21.5 %collective-permute-start.17 = (bf16[2,4,3,96,128]{4,3,2,1,0:T(8,128)(2,1)}, bf16[2,4,3,96,128]{4,3,2,1,0:T(8,128)(2,1)}, u32[]{:S(2)}, u32[]{:S(2)}) collective-permute-start(bf16[2,4,3,96,128]{4,3,2,1,0:T(8,128)(2,1)} %pad_maximum_fusion.13), channel_id=1, source_target_pairs={{0,4},{2,6},{4,0},{6,2},{8,12},{10,14},{12,8},{14,10},{16,20},{18,... | collective-permute-start | bytes 1769480 | tf_op jit(solution)/shard_map/ppermute | solution.py:111
  165.7 6.0 collective-permute-start.12
  171.2 89.9 %collective-permute-start.18 = (bf16[3,1536,128]{1,2,0:T(8,128)(2,1)}, bf16[3,1536,128]{1,2,0:T(8,128)(2,1)S(1)}, u32[]{:S(2)}, u32[]{:S(2)}) collective-permute-start(bf16[3,1536,128]{1,2,0:T(8,128)(2,1)} %copy.128), channel_id=1, source_target_pairs={{0,1},{1,0},{2,3},{3,2},{4,5},{5,4},{6,7},{7,6},{8,9},{9,8},{10,11... | collective-permute-start | bytes 3538952 | tf_op jit(solution)/shard_map/ppermute | solution.py:130
  173.6 19.6 %collective-permute-start.13 = (bf16[256,1536]{1,0:T(8,128)(2,1)S(1)}, bf16[256,1536]{1,0:T(8,128)(2,1)S(1)}, u32[]{:S(2)}, u32[]{:S(2)}) collective-permute-start(bf16[256,1536]{1,0:T(8,128)(2,1)S(1)} %multiply_convert_fusion), channel_id=1, source_target_pairs={{0,2},{2,0},{4,6},{6,4},{8,10},{10,8},{12,14},{14,12},{16,18},{18,... | collective-permute-start | bytes 2359304 | tf_op jit(solution)/shard_map/ppermute | solution.py:111
  174.2 36.8 %collective-permute-start.14 = (bf16[256,1536]{1,0:T(8,128)(2,1)S(1)}, bf16[256,1536]{1,0:T(8,128)(2,1)S(1)}, u32[]{:S(2)}, u32[]{:S(2)}) collective-permute-start(bf16[256,1536]{1,0:T(8,128)(2,1)S(1)} %multiply_convert_fusion), channel_id=1, source_target_pairs={{0,8},{2,10},{4,12},{6,14},{8,0},{10,2},{12,4},{14,6},{16,24},{18,... | collective-permute-start | bytes 2359304 | tf_op jit(solution)/shard_map/ppermute | solution.py:111
  174.5 86.3 %collective-permute-start.15 = (bf16[256,1536]{1,0:T(8,128)(2,1)S(1)}, bf16[256,1536]{1,0:T(8,128)(2,1)S(1)}, u32[]{:S(2)}, u32[]{:S(2)}) collective-permute-start(bf16[256,1536]{1,0:T(8,128)(2,1)S(1)} %multiply_convert_fusion), channel_id=1, source_target_pairs={{0,10},{2,8},{4,14},{6,12},{8,2},{10,0},{12,6},{14,4},{16,26},{18,... | collective-permute-start | bytes 2359304 | tf_op jit(solution)/shard_map/ppermute | solution.py:111
  302.7 19.6 %collective-permute-start.19 = (bf16[256,1536]{1,0:T(8,128)(2,1)S(1)}, bf16[256,1536]{1,0:T(8,128)(2,1)S(1)}, u32[]{:S(2)}, u32[]{:S(2)}) collective-permute-start(bf16[256,1536]{1,0:T(8,128)(2,1)S(1)} %get-tuple-element.180), channel_id=1, source_target_pairs={{0,2},{2,0},{4,6},{6,4},{8,10},{10,8},{12,14},{14,12},{16,18},{18,... | collective-permute-start | bytes 2359304 | tf_op jit(solution)/shard_map/ppermute | solution.py:111
  303.3 20.5 %collective-permute-start.20 = (bf16[256,1536]{1,0:T(8,128)(2,1)S(1)}, bf16[256,1536]{1,0:T(8,128)(2,1)S(1)}, u32[]{:S(2)}, u32[]{:S(2)}) collective-permute-start(bf16[256,1536]{1,0:T(8,128)(2,1)S(1)} %get-tuple-element.182), channel_id=1, source_target_pairs={{0,8},{2,10},{4,12},{6,14},{8,0},{10,2},{12,4},{14,6},{16,24},{18,... | collective-permute-start | bytes 2359304 | tf_op jit(solution)/shard_map/ppermute | solution.py:111
  303.3 35.9 %collective-permute-start.21 = (bf16[256,1536]{1,0:T(8,128)(2,1)S(1)}, bf16[256,1536]{1,0:T(8,128)(2,1)S(1)}, u32[]{:S(2)}, u32[]{:S(2)}) collective-permute-start(bf16[256,1536]{1,0:T(8,128)(2,1)S(1)} %get-tuple-element.181), channel_id=1, source_target_pairs={{0,10},{2,8},{4,14},{6,12},{8,2},{10,0},{12,6},{14,4},{16,26},{18,... | collective-permute-start | bytes 2359304 | tf_op jit(solution)/shard_map/ppermute | solution.py:111
  342.0 19.6 %collective-permute-start.22 = (bf16[256,1536]{1,0:T(8,128)(2,1)S(1)}, bf16[256,1536]{1,0:T(8,128)(2,1)S(1)}, u32[]{:S(2)}, u32[]{:S(2)}) collective-permute-start(bf16[256,1536]{1,0:T(8,128)(2,1)S(1)} %fusion.85), channel_id=1, source_target_pairs={{0,2},{2,0},{4,6},{6,4},{8,10},{10,8},{12,14},{14,12},{16,18},{18,... | collective-permute-start | bytes 2359304 | tf_op jit(solution)/shard_map/ppermute | solution.py:111
  342.6 20.5 %collective-permute-start.23 = (bf16[256,1536]{1,0:T(8,128)(2,1)S(1)}, bf16[256,1536]{1,0:T(8,128)(2,1)S(1)}, u32[]{:S(2)}, u32[]{:S(2)}) collective-permute-start(bf16[256,1536]{1,0:T(8,128)(2,1)S(1)} %fusion.85), channel_id=1, source_target_pairs={{0,8},{2,10},{4,12},{6,14},{8,0},{10,2},{12,4},{14,6},{16,24},{18,... | collective-permute-start | bytes 2359304 | tf_op jit(solution)/shard_map/ppermute | solution.py:111
  342.9 34.4 %collective-permute-start.24 = (bf16[256,1536]{1,0:T(8,128)(2,1)S(1)}, bf16[256,1536]{1,0:T(8,128)(2,1)S(1)}, u32[]{:S(2)}, u32[]{:S(2)}) collective-permute-start(bf16[256,1536]{1,0:T(8,128)(2,1)S(1)} %fusion.85), channel_id=1, source_target_pairs={{0,10},{2,8},{4,14},{6,12},{8,2},{10,0},{12,6},{14,4},{16,26},{18,... | collective-permute-start | bytes 2359304 | tf_op jit(solution)/shard_map/ppermute | solution.py:111
  442.4 22.5 %collective-permute-start.27 = (bf16[272,1536]{1,0:T(8,128)(2,1)S(1)}, bf16[272,1536]{1,0:T(8,128)(2,1)S(1)}, u32[]{:S(2)}, u32[]{:S(2)}) collective-permute-start(bf16[272,1536]{1,0:T(8,128)(2,1)S(1)} %get-tuple-element.175), channel_id=1, source_target_pairs={{0,10},{2,8},{4,14},{6,12},{8,2},{10,0},{12,6},{14,4},{16,26},{18,... | collective-permute-start | bytes 2506760 | tf_op jit(solution)/shard_map/ppermute | solution.py:111
  443.0 34.4 %collective-permute-start.26 = (bf16[272,1536]{1,0:T(8,128)(2,1)S(1)}, bf16[272,1536]{1,0:T(8,128)(2,1)S(1)}, u32[]{:S(2)}, u32[]{:S(2)}) collective-permute-start(bf16[272,1536]{1,0:T(8,128)(2,1)S(1)} %get-tuple-element.176), channel_id=1, source_target_pairs={{0,8},{2,10},{4,12},{6,14},{8,0},{10,2},{12,4},{14,6},{16,24},{18,... | collective-permute-start | bytes 2506760 | tf_op jit(solution)/shard_map/ppermute | solution.py:111
  444.4 33.8 %collective-permute-start.25 = (bf16[272,1536]{1,0:T(8,128)(2,1)S(1)}, bf16[272,1536]{1,0:T(8,128)(2,1)S(1)}, u32[]{:S(2)}, u32[]{:S(2)}) collective-permute-start(bf16[272,1536]{1,0:T(8,128)(2,1)S(1)} %get-tuple-element.177), channel_id=1, source_target_pairs={{0,2},{2,0},{4,6},{6,4},{8,10},{10,8},{12,14},{14,12},{16,18},{18,... | collective-permute-start | bytes 2506760 | tf_op jit(solution)/shard_map/ppermute | solution.py:111
  478.7 8.6 %collective-permute-start.29 = (bf16[1536,16]{0,1:T(8,128)(2,1)S(1)}, bf16[1536,16]{0,1:T(8,128)(2,1)S(1)}, u32[]{:S(2)}, u32[]{:S(2)}) collective-permute-start(bf16[1536,16]{0,1:T(8,128)(2,1)S(1)} %get-tuple-element.215), channel_id=1, source_target_pairs={{0,1},{1,0},{2,3},{3,2},{4,5},{5,4},{6,7},{7,6},{8,9},{9,8},{10,11... | collective-permute-start | bytes 147464 | tf_op jit(solution)/shard_map/ppermute | solution.py:130
  483.4 7.3 %collective-permute-start.28 = (bf16[256,1536]{1,0:T(8,128)(2,1)}, bf16[256,1536]{1,0:T(8,128)(2,1)}, u32[]{:S(2)}, u32[]{:S(2)}) collective-permute-start(bf16[256,1536]{1,0:T(8,128)(2,1)} %get-tuple-element.168.own), channel_id=1, source_target_pairs={{0,1},{1,0},{2,3},{3,2},{4,5},{5,4},{6,7},{7,6},{8,9},{9,8},{10,11... | collective-permute-start | bytes 2359304 | tf_op jit(solution)/shard_map/ppermute | solution.py:130
  498.6 32.9 %collective-permute-start.31 = (bf16[8,96,896]{2,1,0:T(8,128)(2,1)}, bf16[8,96,896]{2,1,0:T(8,128)(2,1)}, u32[]{:S(2)}, u32[]{:S(2)}) collective-permute-start(bf16[8,96,896]{2,1,0:T(8,128)(2,1)} %get-tuple-element.80), channel_id=1, source_target_pairs={{0,2},{2,0},{4,6},{6,4},{8,10},{10,8},{12,14},{14,12},{16,18},{18,... | collective-permute-start | bytes 4128776 | tf_op jit(solution)/shard_map/ppermute | solution.py:111
  500.9 31.6 %collective-permute-start.44 = (bf16[3,1536,128]{1,2,0:T(8,128)(2,1)}, bf16[3,1536,128]{1,2,0:T(8,128)(2,1)}, u32[]{:S(2)}, u32[]{:S(2)}) collective-permute-start(bf16[3,1536,128]{1,2,0:T(8,128)(2,1)} %fusion.6), channel_id=1, source_target_pairs={{0,1},{1,0},{2,3},{3,2},{4,5},{5,4},{6,7},{7,6},{8,9},{9,8},{10,11... | collective-permute-start | bytes 3538952 | tf_op jit(solution)/shard_map/ppermute | solution.py:130
  524.0 18.3 %collective-permute-start.30 = (bf16[256,1536]{1,0:T(8,128)(2,1)}, bf16[256,1536]{1,0:T(8,128)(2,1)}, u32[]{:S(2)}, u32[]{:S(2)}) collective-permute-start(bf16[256,1536]{1,0:T(8,128)(2,1)} %get-tuple-element.78), channel_id=1, source_target_pairs={{0,1},{1,0},{2,3},{3,2},{4,5},{5,4},{6,7},{7,6},{8,9},{9,8},{10,11... | collective-permute-start | bytes 2359304 | tf_op jit(solution)/shard_map/ppermute | solution.py:130
  531.5 44.7 %collective-permute-start.32 = (bf16[8,96,1280]{2,1,0:T(8,128)(2,1)}, bf16[8,96,1280]{2,1,0:T(8,128)(2,1)}, u32[]{:S(2)}, u32[]{:S(2)}) collective-permute-start(bf16[8,96,1280]{2,1,0:T(8,128)(2,1)} %get-tuple-element.82), channel_id=1, source_target_pairs={{0,2},{2,0},{4,6},{6,4},{8,10},{10,8},{12,14},{14,12},{16,18},{18,... | collective-permute-start | bytes 5898248 | tf_op jit(solution)/shard_map/ppermute | solution.py:111
  537.9 52.5 %collective-permute-start.45 = (bf16[2,4,3,96,128]{4,3,2,1,0:T(8,128)(2,1)S(1)}, bf16[2,4,3,96,128]{4,3,2,1,0:T(8,128)(2,1)S(1)}, u32[]{:S(2)}, u32[]{:S(2)}) collective-permute-start(bf16[2,4,3,96,128]{4,3,2,1,0:T(8,128)(2,1)S(1)} %pad_maximum_fusion.14), channel_id=1, source_target_pairs={{0,4},{2,6},{4,0},{6,2},{8,12},{10,14},{12,8},{14,10},{16,20},{18,... | collective-permute-start | bytes 1769480 | tf_op jit(solution)/shard_map/ppermute | solution.py:111
  549.1 41.1 %collective-permute-start.41 = (bf16[4,96,896]{2,1,0:T(8,128)(2,1)S(1)}, bf16[4,96,896]{2,1,0:T(8,128)(2,1)S(1)}, u32[]{:S(2)}, u32[]{:S(2)}) collective-permute-start(bf16[4,96,896]{2,1,0:T(8,128)(2,1)S(1)} %slice.480), channel_id=1, source_target_pairs={{0,4},{2,6},{4,0},{6,2},{8,12},{10,14},{12,8},{14,10},{16,20},{18,... | collective-permute-start | bytes 2064392 | tf_op jit(solution)/shard_map/ppermute | solution.py:111
  578.3 46.6 %collective-permute-start.34 = (bf16[4,96,1280]{2,1,0:T(8,128)(2,1)S(1)}, bf16[4,96,1280]{2,1,0:T(8,128)(2,1)S(1)}, u32[]{:S(2)}, u32[]{:S(2)}) collective-permute-start(bf16[4,96,1280]{2,1,0:T(8,128)(2,1)S(1)} %slice.479), channel_id=1, source_target_pairs={{0,4},{2,6},{4,0},{6,2},{8,12},{10,14},{12,8},{14,10},{16,20},{18,... | collective-permute-start | bytes 2949128 | tf_op jit(solution)/shard_map/ppermute | solution.py:111
  590.4 37.4 %collective-permute-start.42 = (bf16[2,96,896]{2,1,0:T(8,128)(2,1)S(1)}, bf16[2,96,896]{2,1,0:T(8,128)(2,1)S(1)}, u32[]{:S(2)}, u32[]{:S(2)}) collective-permute-start(bf16[2,96,896]{2,1,0:T(8,128)(2,1)S(1)} %slice.482), channel_id=1, source_target_pairs={{0,8},{2,10},{4,12},{6,14},{8,0},{10,2},{12,4},{14,6},{16,24},{18,... | collective-permute-start | bytes 1032200 | tf_op jit(solution)/shard_map/ppermute | solution.py:111
  592.0 35.7 %collective-permute-start.46 = (bf16[4,3,96,128]{3,2,1,0:T(8,128)(2,1)S(1)}, bf16[4,3,96,128]{3,2,1,0:T(8,128)(2,1)S(1)}, u32[]{:S(2)}, u32[]{:S(2)}) collective-permute-start(bf16[4,3,96,128]{3,2,1,0:T(8,128)(2,1)S(1)} %fusion.50), channel_id=1, source_target_pairs={{0,16},{2,18},{4,20},{6,22},{8,24},{10,26},{12,28},{14,30},{16,0},... | collective-permute-start | bytes 884744 | tf_op jit(solution)/shard_map/ppermute | solution.py:111
  625.1 19.7 %collective-permute-start.36 = (bf16[2,96,1280]{2,1,0:T(8,128)(2,1)S(1)}, bf16[2,96,1280]{2,1,0:T(8,128)(2,1)S(1)}, u32[]{:S(2)}, u32[]{:S(2)}) collective-permute-start(bf16[2,96,1280]{2,1,0:T(8,128)(2,1)S(1)} %slice.481), channel_id=1, source_target_pairs={{0,8},{2,10},{4,12},{6,14},{8,0},{10,2},{12,4},{14,6},{16,24},{18,... | collective-permute-start | bytes 1474568 | tf_op jit(solution)/shard_map/ppermute | solution.py:111
  627.8 14.1 %collective-permute-start.35 = (f32[3,1536]{1,0:T(4,128)S(1)}, f32[3,1536]{1,0:T(4,128)S(1)}, u32[]{:S(2)}, u32[]{:S(2)}) collective-permute-start(f32[3,1536]{1,0:T(4,128)S(1)} %add.336), channel_id=1, source_target_pairs={{0,4},{2,6},{4,0},{6,2},{8,12},{10,14},{12,8},{14,10},{16,20},{18,... | collective-permute-start | bytes 55304 | tf_op jit(solution)/shard_map/ppermute | solution.py:111
  640.2 13.3 %collective-permute-start.43 = (bf16[1,96,896]{2,1,0:T(8,128)(2,1)S(1)}, bf16[1,96,896]{2,1,0:T(8,128)(2,1)S(1)}, u32[]{:S(2)}, u32[]{:S(2)}) collective-permute-start(bf16[1,96,896]{2,1,0:T(8,128)(2,1)S(1)} %slice.484), channel_id=1, source_target_pairs={{0,16},{2,18},{4,20},{6,22},{8,24},{10,26},{12,28},{14,30},{16,0},... | collective-permute-start | bytes 516104 | tf_op jit(solution)/shard_map/ppermute | solution.py:111
  644.9 13.4 %collective-permute-start.47 = (bf16[3,96,128]{2,1,0:T(8,128)(2,1)S(1)}, bf16[3,96,128]{2,1,0:T(8,128)(2,1)S(1)}, u32[]{:S(2)}, u32[]{:S(2)}) collective-permute-start(bf16[3,96,128]{2,1,0:T(8,128)(2,1)S(1)} %get-tuple-element.193), channel_id=1, source_target_pairs={{0,2},{2,0},{4,6},{6,4},{8,10},{10,8},{12,14},{14,12},{16,18},{18,... | collective-permute-start | bytes 221192 | tf_op jit(solution)/shard_map/ppermute | solution.py:111
  654.5 5.7 collective-permute-start.48
  656.5 8.7 %collective-permute-start.49 = (bf16[3,96,128]{2,1,0:T(8,128)(2,1)S(1)}, bf16[3,96,128]{2,1,0:T(8,128)(2,1)S(1)}, u32[]{:S(2)}, u32[]{:S(2)}) collective-permute-start(bf16[3,96,128]{2,1,0:T(8,128)(2,1)S(1)} %get-tuple-element.191), channel_id=1, source_target_pairs={{0,10},{2,8},{4,14},{6,12},{8,2},{10,0},{12,6},{14,4},{16,26},{18,... | collective-permute-start | bytes 221192 | tf_op jit(solution)/shard_map/ppermute | solution.py:111
  657.8 15.9 %collective-permute-start.38 = (bf16[1,96,1280]{2,1,0:T(8,128)(2,1)S(1)}, bf16[1,96,1280]{2,1,0:T(8,128)(2,1)S(1)}, u32[]{:S(2)}, u32[]{:S(2)}) collective-permute-start(bf16[1,96,1280]{2,1,0:T(8,128)(2,1)S(1)} %slice.483), channel_id=1, source_target_pairs={{0,16},{2,18},{4,20},{6,22},{8,24},{10,26},{12,28},{14,30},{16,0},... | collective-permute-start | bytes 737288 | tf_op jit(solution)/shard_map/ppermute | solution.py:111
  (54 other events, 763.9 us)
Sparse Core Ops, SparseCore 0:
  69.8 189.5 all-gather.2
  439.6 235.2 reduce-scatter.1

commit v4 on v3

--- a/solution.py
+++ b/solution.py
@@ -789,38 +789,39 @@
     forward = experts_forward if in_kernel else experts_forward_plain
     backward = experts_backward if in_kernel else experts_backward_plain
 
+    near, far = (1 << bit for bit in lay.w_bits)
+    qkv = Tree(lay, jnp.concatenate([w_query, key_value_weight[0], key_value_weight[1]], axis=1))
+    router_pad = jnp.zeros((w_router.shape[0], -experts % 128), bf16)
+    out = Tree(lay, jnp.concatenate([w_out, w_router, router_pad], axis=1))
+    steps = len(lay.tree_bits)
+    qkv.step()
+    out.step(qkv.marks[0])
+    qkv.step()
+    input_slices = lay.gather_core(behind(block_input, qkv.marks[0]))
+
     own_routes = lax.dynamic_slice_in_dim(routes, lay.core * own_rows, own_rows, 0)
     expert_ids = jnp.arange(experts, dtype=jnp.int32)
     member = jnp.any(own_routes.T[None, :, :] == expert_ids[:, None, None], axis=1)
     held_ids = lay.place ^ jnp.array(lay.w_masks, jnp.int32)
     held_hot = (held_ids[:, None] == expert_ids).astype(f32)
     shared_parts, group_member = spread_shared(
-        lay, w_shared_in, w_shared_out, member.astype(bf16)
+        lay, *behind((w_shared_in, w_shared_out), qkv.marks[0]), member.astype(bf16)
     )
     held_member = contract("je,get->jgt", held_hot.astype(bf16), group_member)
     before = jnp.triu(jnp.ones((own_rows, own_rows), bf16), 1)
     position = contract("jgu,ut->jgt", held_member.astype(bf16), before)
     position = jnp.where(held_member > 0, position, -1.0)
 
-    near, far = (1 << bit for bit in lay.w_bits)
-    input_slices = lay.gather_core(block_input)
-    qkv = Tree(lay, jnp.concatenate([w_query, key_value_weight[0], key_value_weight[1]], axis=1))
-    router_pad = jnp.zeros((w_router.shape[0], -experts % 128), bf16)
-    out = Tree(lay, jnp.concatenate([w_out, w_router, router_pad], axis=1))
-    steps = len(lay.tree_bits)
-    qkv.step()
-    out.step(qkv.marks[0])
-    qkv.step(shared_parts, input_slices, group_member)
     out.step(qkv.marks[1])
     for k in range(2, steps):
-        qkv.step(out.marks[k - 2])
+        qkv.step(out.marks[k - 2], *([shared_parts, input_slices] if k == 2 else []))
         out.step(qkv.marks[k])
+    shared_far = lay.shift(behind(shared_parts, out.marks[0]), far)
     expert_shares = lax.all_gather(
-        behind(jnp.concatenate([w_expert_in[0], w_expert_out], axis=0), qkv.marks[2]),
+        behind(jnp.concatenate([w_expert_in[0], w_expert_out], axis=0), qkv.marks[2], shared_far),
         ("dp", "tensor"),
         axis_index_groups=lay.w_groups(),
     )
-    shared_far = lay.shift(behind(shared_parts, qkv.marks[-2], out.marks[1]), far)
     shared_near = lay.shift(behind(jnp.stack([shared_parts, shared_far]), out.marks[-2]), near)
 
     spot = jnp.stack([lay.core, length]).astype(jnp.int32)
@@ -870,6 +871,7 @@
     moe_own, scale_moe = normalize_rows(hidden, gain_moe)
 
     arrived = lay.gather_g(moe_own)
+    shared_near = behind(shared_near, arrived[1])
     shared_own = gather_shared(lay, [shared_parts, shared_near[0], shared_far, shared_near[1]])
     shared_full = jnp.concatenate(lay.gather_core(shared_own), axis=2)
     shared_in_full, shared_out_full = shared_full[:2], shared_full[2]

time: 705 us -> 688 us (0.976)
  starting transfers between devices: 70.1 us -> 46.4 us
  waiting for transfers between devices: 383 us -> 403 us
  Pallas kernels: 123 us -> 115 us
    ppermute x42, starting transfers between devices: 68.1 us -> 45 us  [shift(): return lax.ppermute(values, 'dp', [(i, i ^ mask) for i in range(self.dp)])]
    ppermute x42, waiting for transfers between devices: 383 us -> 401 us  [shift(): return lax.ppermute(values, 'dp', [(i, i ^ mask) for i in range(self.dp)])]
    pallas_call x1, Pallas kernels: 53.3 us -> 45.5 us  [experts_backward(): pl.pallas_call(kernel, grid=(held,), in_specs=[scalars, whole, whole, pl....]
  transfers between devices with their start and end apart: 52 -> 52, of which waited for: 35 -> 36; matrix products, arithmetic and copies ran while one was open for 11% -> 10% of each run, Pallas kernels for 7% -> 7%
where the time goes in v4:
time: 688 us; the launch traced here: 679 us
  waiting for transfers between devices  403 us (59%)
  Pallas kernels  115 us (17%)
  starting transfers between devices  46.4 us (7%)
  other arithmetic  37.1 us (5%)
  local copies, waits for them, and re-layouts  31.7 us (5%)
  matrix products  26.9 us (4%)
  between operations  18.5 us (3%)
    ppermute x42, waiting for transfers between devices, shift(): return lax.ppermute(values, 'dp', [(i, i ^ mask) for i in range(self.dp)])  401 us
    pallas_call x1, Pallas kernels, experts_backward(): pl.pallas_call(kernel, grid=(held,), in_specs=[scalars, whole, whole, pl....  45.5 us
    ppermute x42, starting transfers between devices, shift(): return lax.ppermute(values, 'dp', [(i, i ^ mask) for i in range(self.dp)])  45 us
    pallas_call x1, Pallas kernels, experts_forward(): pl.pallas_call(kernel, grid=(held,), in_specs=[scalars, whole, whole, pl....  24 us
    pallas_call x1, Pallas kernels, attend_back(): pl.pallas_call(kernel, in_specs=[scalars, scalars] + [in_vmem] * 4, out_s...  13.8 us
  transfers between devices with their start and end apart: 52, of which 36 were waited for; matrix products, arithmetic and copies ran while one was open for 10% of the time, Pallas kernels for 7%

profile of v4, /device:TPU:0, one launch (start us, length us, event | category | flops | bytes accessed | tf_op | source)
XLA Modules:
  0.0 678.5 jit_solution(15135997624026182494)
XLA Ops:
  9.2 4.1 collective-permute-start
  14.2 10.3 %collective-permute-done = bf16[1,96,1280]{2,1,0:T(8,128)(2,1)S(1)} collective-permute-done((bf16[1,96,1280]{2,1,0:T(8,128)(2,1)S(1)}, bf16[1,96,1280]{2,1,0:T(8,128)(2,1)S(1)}, u32[]{:S(2)}, u32[]{:S(2)}) %collective-permute-start) | collective-permute-done | bytes 245792 | tf_op jit(solution)/shard_map/ppermute | solution.py:111
  29.1 10.6 %collective-permute-done.5 = bf16[320,128]{1,0:T(8,128)(2,1)S(1)} collective-permute-done((bf16[320,128]{1,0:T(8,128)(2,1)S(1)}, bf16[320,128]{1,0:T(8,128)(2,1)S(1)}, u32[]{:S(2)}, u32[]{:S(2)}) %collective-permute-start.5) | collective-permute-done | bytes 81952 | tf_op jit(solution)/shard_map/ppermute | solution.py:111
  39.6 2.8 collective-permute-start.3
  44.2 5.4 collective-permute-done.3
  53.6 13.3 %collective-permute-done.16 = bf16[4,3,96,128]{3,2,1,0:T(8,128)(2,1)S(1)} collective-permute-done((bf16[4,3,96,128]{3,2,1,0:T(8,128)(2,1)S(1)}, bf16[4,3,96,128]{3,2,1,0:T(8,128)(2,1)S(1)}, u32[]{:S(2)}, u32[]{:S(2)}) %collective-permute-start.16) | collective-permute-done | bytes 294944 | tf_op jit(solution)/shard_map/ppermute | solution.py:111
  66.9 6.3 collective-permute-done.7
  75.0 7.0 %collective-permute-done.8 = bf16[2,96,896]{2,1,0:T(8,128)(2,1)S(1)} collective-permute-done((bf16[2,96,896]{2,1,0:T(8,128)(2,1)S(1)}, bf16[2,96,896]{2,1,0:T(8,128)(2,1)S(1)}, u32[]{:S(2)}, u32[]{:S(2)}) %collective-permute-start.8) | collective-permute-done | bytes 344096 | tf_op jit(solution)/shard_map/ppermute | solution.py:111
  85.1 27.9 %collective-permute-done.10 = bf16[4,96,896]{2,1,0:T(8,128)(2,1)S(1)} collective-permute-done((bf16[4,96,896]{2,1,0:T(8,128)(2,1)S(1)}, bf16[4,96,896]{2,1,0:T(8,128)(2,1)S(1)}, u32[]{:S(2)}, u32[]{:S(2)}) %collective-permute-start.10) | collective-permute-done | bytes 688160 | tf_op jit(solution)/shard_map/ppermute | solution.py:111
  113.2 11.6 %collective-permute-done.9.far = bf16[8,96,1280]{2,1,0:T(8,128)(2,1)S(1)} collective-permute-done((bf16[8,96,1280]{2,1,0:T(8,128)(2,1)S(1)}, bf16[8,96,1280]{2,1,0:T(8,128)(2,1)S(1)}, u32[]{:S(2)}, u32[]{:S(2)}) %collective-permute-start.9) | collective-permute-done | bytes 1966112 | tf_op jit(solution)/shard_map/ppermute | solution.py:111
  129.3 10.4 %shard_map.273 = (bf16[512,1536]{1,0:T(8,128)(2,1)}, bf16[512,1280]{1,0:T(8,128)(2,1)}, bf16[512,768]{1,0:T(8,128)(2,1)}, f32[6,512,1]{2,1,0:T(8,128)}) custom-call(s32[16]{0:T(128)} %shift-left_add_fusion.order, s32[2]{0:T(128)} %pad_add_fusion.1.spot, bf16[256,1536]{1,0:T(8,128)(2,1)} %own, bf16[256,1536]{1,0:T(8,128)(2,1)} %copy-done.34, ...), custom_call_target="tpu_custom_call" | custom-call | tf_op jit(solution)/shard_map/pallas_call | solution.py:311
  139.7 14.3 %collective-permute-done.11.far = bf16[8,96,896]{2,1,0:T(8,128)(2,1)} collective-permute-done((bf16[8,96,896]{2,1,0:T(8,128)(2,1)S(1)}, bf16[8,96,896]{2,1,0:T(8,128)(2,1)}, u32[]{:S(2)}, u32[]{:S(2)}) %collective-permute-start.11) | collective-permute-done | bytes 1376288 | tf_op jit(solution)/shard_map/ppermute | solution.py:111
  154.0 6.3 shard_map.274
  172.9 23.2 %collective-permute-done.17 = bf16[2,4,3,96,128]{4,3,2,1,0:T(8,128)(2,1)S(1)} collective-permute-done((bf16[2,4,3,96,128]{4,3,2,1,0:T(8,128)(2,1)}, bf16[2,4,3,96,128]{4,3,2,1,0:T(8,128)(2,1)S(1)}, u32[]{:S(2)}, u32[]{:S(2)}) %collective-permute-start.17) | collective-permute-done | bytes 589856 | tf_op jit(solution)/shard_map/ppermute | solution.py:111
  200.1 6.0 collective-permute-done.14
  206.1 50.1 %collective-permute-done.15 = bf16[256,1536]{1,0:T(8,128)(2,1)} collective-permute-done((bf16[256,1536]{1,0:T(8,128)(2,1)S(1)}, bf16[256,1536]{1,0:T(8,128)(2,1)}, u32[]{:S(2)}, u32[]{:S(2)}) %collective-permute-start.15) | collective-permute-done | bytes 786464 | tf_op jit(solution)/shard_map/ppermute | solution.py:111
  261.2 3.2 fusion.10
  266.3 4.8 fusion.46.init
  271.1 24.0 %shard_map.275 = (bf16[4,256,1536]{2,1,0:T(8,128)(2,1)}, bf16[4,512,1536]{2,1,0:T(8,128)(2,1)}, f32[4,2,2,512,256]{4,3,2,1,0:T(8,128)}) custom-call(s32[4,2]{1,0:T(4,128)} %pad_add_fusion.spots, f32[4,4,256]{2,1,0:T(4,128)} %convolution_select_fusion.1.position, f32[4,4,256]{2,1,0:T(4,128)} %reshape.239.gate, bf16[1024,1536]{1,0:T(8,128)(2,1)} %copy-done.2, ...), custom_call_target="tpu_custom_call" | custom-call | tf_op jit(solution)/shard_map/pallas_call | solution.py:569
  297.7 2.9 collective-permute-start.21
  301.3 15.4 %collective-permute-done.19 = bf16[256,1536]{1,0:T(8,128)(2,1)S(1)} collective-permute-done((bf16[256,1536]{1,0:T(8,128)(2,1)S(1)}, bf16[256,1536]{1,0:T(8,128)(2,1)S(1)}, u32[]{:S(2)}, u32[]{:S(2)}) %collective-permute-start.19) | collective-permute-done | bytes 786464 | tf_op jit(solution)/shard_map/ppermute | solution.py:111
  318.2 15.9 %collective-permute-done.21 = bf16[256,1536]{1,0:T(8,128)(2,1)S(1)} collective-permute-done((bf16[256,1536]{1,0:T(8,128)(2,1)S(1)}, bf16[256,1536]{1,0:T(8,128)(2,1)S(1)}, u32[]{:S(2)}, u32[]{:S(2)}) %collective-permute-start.21) | collective-permute-done | bytes 786464 | tf_op jit(solution)/shard_map/ppermute | solution.py:111
  334.2 2.6 multiply_reduce_fusion
  337.7 2.8 collective-permute-start.24
  340.5 16.1 %collective-permute-done.22 = bf16[256,1536]{1,0:T(8,128)(2,1)S(1)} collective-permute-done((bf16[256,1536]{1,0:T(8,128)(2,1)S(1)}, bf16[256,1536]{1,0:T(8,128)(2,1)S(1)}, u32[]{:S(2)}, u32[]{:S(2)}) %collective-permute-start.22) | collective-permute-done | bytes 786464 | tf_op jit(solution)/shard_map/ppermute | solution.py:111
  357.9 15.0 %collective-permute-done.24 = bf16[256,1536]{1,0:T(8,128)(2,1)S(1)} collective-permute-done((bf16[256,1536]{1,0:T(8,128)(2,1)S(1)}, bf16[256,1536]{1,0:T(8,128)(2,1)S(1)}, u32[]{:S(2)}, u32[]{:S(2)}) %collective-permute-start.24) | collective-permute-done | bytes 786464 | tf_op jit(solution)/shard_map/ppermute | solution.py:111
  373.3 3.0 fusion.55
  376.3 6.2 fusion.24
  382.6 45.5 %shard_map.276 = (bf16[4,272,1536]{2,1,0:T(8,128)(2,1)}, bf16[8,3,1536,256]{3,2,1,0:T(8,128)(2,1)}) custom-call(s32[4,2]{1,0:T(4,128)} %pad_add_fusion.spots, f32[4,4,256]{2,1,0:T(4,128)} %convolution_select_fusion.1.position, f32[4,4,256]{2,1,0:T(4,128)} %reshape.239.gate, bf16[1024,1536]{1,0:T(8,128)(2,1)} %copy-done.8, ...), custom_call_target="tpu_custom_call" | custom-call | tf_op jit(solution)/shard_map/pallas_call | solution.py:681
  436.8 16.7 %collective-permute-done.27 = bf16[272,1536]{1,0:T(8,128)(2,1)S(1)} collective-permute-done((bf16[272,1536]{1,0:T(8,128)(2,1)S(1)}, bf16[272,1536]{1,0:T(8,128)(2,1)S(1)}, u32[]{:S(2)}, u32[]{:S(2)}) %collective-permute-start.27) | collective-permute-done | bytes 835616 | tf_op jit(solution)/shard_map/ppermute | solution.py:111
  453.6 13.0 %collective-permute-done.26 = bf16[272,1536]{1,0:T(8,128)(2,1)S(1)} collective-permute-done((bf16[272,1536]{1,0:T(8,128)(2,1)S(1)}, bf16[272,1536]{1,0:T(8,128)(2,1)S(1)}, u32[]{:S(2)}, u32[]{:S(2)}) %collective-permute-start.26) | collective-permute-done | bytes 835616 | tf_op jit(solution)/shard_map/ppermute | solution.py:111
  468.1 2.3 multiply_reduce_fusion.2
  480.0 7.9 %shard_map.277 = (bf16[512,768]{1,0:T(8,128)(2,1)}, bf16[8,96,896]{2,1,0:T(8,128)(2,1)}, bf16[8,96,896]{2,1,0:T(8,128)(2,1)}) custom-call(s32[16]{0:T(128)} %shift-left_add_fusion.order, bf16[256,1536]{1,0:T(8,128)(2,1)} %get-tuple-element.174.own, bf16[256,1536]{1,0:T(8,128)(2,1)} %collective-permute-done.28.other, ...), custom_call_target="tpu_custom_call" | custom-call | tf_op jit(solution)/shard_map/pallas_call | solution.py:375
  492.0 13.8 %shard_map.278 = (bf16[512,1280]{1,0:T(8,128)(2,1)}, bf16[8,96,1280]{2,1,0:T(8,128)(2,1)}, bf16[8,96,1280]{2,1,0:T(8,128)(2,1)}) custom-call(s32[16]{0:T(128)} %shift-left_add_fusion.order, s32[2]{0:T(128)} %pad_add_fusion.1.spot, bf16[512,768]{1,0:T(8,128)(2,1)} %get-tuple-element.78.grad_mixed, bf16[512,1536]{1,0:T(8,128)(2,1)} %get-tuple-element.79.normed, ...), custom_call_target="tpu_custom_call" | custom-call | tf_op jit(solution)/shard_map/pallas_call | solution.py:419
  505.8 7.3 %shard_map.279 = (f32[256,1536]{1,0:T(8,128)}, bf16[256,1536]{1,0:T(8,128)(2,1)}) custom-call(s32[16]{0:T(128)} %shift-left_add_fusion.order, bf16[512,1280]{1,0:T(8,128)(2,1)} %get-tuple-element.82.grad_made, bf16[8,96,1280]{2,1,0:T(8,128)(2,1)} %copy-done.6, bf16[8,96,1280]{2,1,0:T(8,128)(2,1)} %copy-done.13), custom_call_target="tpu_custom_call" | custom-call | tf_op jit(solution)/shard_map/pallas_call | solution.py:445
  513.7 7.1 %collective-permute-done.31 = bf16[8,96,896]{2,1,0:T(8,128)(2,1)} collective-permute-done((bf16[8,96,896]{2,1,0:T(8,128)(2,1)}, bf16[8,96,896]{2,1,0:T(8,128)(2,1)}, u32[]{:S(2)}, u32[]{:S(2)}) %collective-permute-start.31) | collective-permute-done | bytes 1376288 | tf_op jit(solution)/shard_map/ppermute | solution.py:111
  521.4 2.7 fusion.5
  530.2 3.1 fusion.22
  535.9 29.6 %collective-permute-done.32 = bf16[8,96,1280]{2,1,0:T(8,128)(2,1)} collective-permute-done((bf16[8,96,1280]{2,1,0:T(8,128)(2,1)}, bf16[8,96,1280]{2,1,0:T(8,128)(2,1)}, u32[]{:S(2)}, u32[]{:S(2)}) %collective-permute-start.32) | collective-permute-done | bytes 1966112 | tf_op jit(solution)/shard_map/ppermute | solution.py:111
  568.3 8.6 %collective-permute-done.41 = bf16[4,96,896]{2,1,0:T(8,128)(2,1)S(1)} collective-permute-done((bf16[4,96,896]{2,1,0:T(8,128)(2,1)S(1)}, bf16[4,96,896]{2,1,0:T(8,128)(2,1)S(1)}, u32[]{:S(2)}, u32[]{:S(2)}) %collective-permute-start.41) | collective-permute-done | bytes 688160 | tf_op jit(solution)/shard_map/ppermute | solution.py:111
  581.1 31.3 %collective-permute-done.34 = bf16[4,96,1280]{2,1,0:T(8,128)(2,1)S(1)} collective-permute-done((bf16[4,96,1280]{2,1,0:T(8,128)(2,1)S(1)}, bf16[4,96,1280]{2,1,0:T(8,128)(2,1)S(1)}, u32[]{:S(2)}, u32[]{:S(2)}) %collective-permute-start.34) | collective-permute-done | bytes 983072 | tf_op jit(solution)/shard_map/ppermute | solution.py:111
  612.7 3.3 collective-permute-done.46
  616.4 3.6 collective-permute-done.35
  620.1 6.1 collective-permute-done.36
  628.1 7.6 %collective-permute-done.43 = bf16[1,96,896]{2,1,0:T(8,128)(2,1)S(1)} collective-permute-done((bf16[1,96,896]{2,1,0:T(8,128)(2,1)S(1)}, bf16[1,96,896]{2,1,0:T(8,128)(2,1)S(1)}, u32[]{:S(2)}, u32[]{:S(2)}) %collective-permute-start.43) | collective-permute-done | bytes 172064 | tf_op jit(solution)/shard_map/ppermute | solution.py:111
  642.1 5.1 collective-permute-done.49
  648.7 7.3 %collective-permute-done.38 = bf16[1,96,1280]{2,1,0:T(8,128)(2,1)S(1)} collective-permute-done((bf16[1,96,1280]{2,1,0:T(8,128)(2,1)S(1)}, bf16[1,96,1280]{2,1,0:T(8,128)(2,1)S(1)}, u32[]{:S(2)}, u32[]{:S(2)}) %collective-permute-start.38) | collective-permute-done | bytes 245792 | tf_op jit(solution)/shard_map/ppermute | solution.py:111
  656.1 4.7 collective-permute-done.39
  (322 shorter events, 111.7 us)
Async XLA Ops:
  7.2 263.9 %all-gather.3.cloned.1.call-start = ((), (), s32[]{:S(2)}) async-start(), calls=%async_computation.2 | async-start | bytes 21233664 | tf_op jit(solution)/shard_map/all_gather | solution.py:820
  9.2 15.3 %collective-permute-start = (bf16[1,96,1280]{2,1,0:T(8,128)(2,1)S(1)}, bf16[1,96,1280]{2,1,0:T(8,128)(2,1)S(1)}, u32[]{:S(2)}, u32[]{:S(2)}) collective-permute-start(bf16[1,96,1280]{2,1,0:T(8,128)(2,1)S(1)} %maximum_bitcast_fusion), channel_id=1, source_target_pairs={{0,16},{2,18},{4,20},{6,22},{8,24},{10,26},{12,28},{14,30},{16,0},... | collective-permute-start | bytes 737288 | tf_op jit(solution)/shard_map/ppermute | solution.py:111
  24.5 19.5 %collective-permute-start.2 = (bf16[2,96,1280]{2,1,0:T(8,128)(2,1)S(1)}, bf16[2,96,1280]{2,1,0:T(8,128)(2,1)S(1)}, u32[]{:S(2)}, u32[]{:S(2)}) collective-permute-start(bf16[2,96,1280]{2,1,0:T(8,128)(2,1)S(1)} %pad_maximum_fusion.15), channel_id=1, source_target_pairs={{0,8},{2,10},{4,12},{6,14},{8,0},{10,2},{12,4},{14,6},{16,24},{18,... | collective-permute-start | bytes 1474568 | tf_op jit(solution)/shard_map/ppermute | solution.py:111
  25.3 24.3 %collective-permute-start.1 = (bf16[256,1536]{1,0:T(8,128)(2,1)S(1)}, bf16[256,1536]{1,0:T(8,128)(2,1)S(1)}, u32[]{:S(2)}, u32[]{:S(2)}) collective-permute-start(bf16[256,1536]{1,0:T(8,128)(2,1)S(1)} %copy-done.10), channel_id=1, source_target_pairs={{0,1},{1,0},{2,3},{3,2},{4,5},{5,4},{6,7},{7,6},{8,9},{9,8},{10,11... | collective-permute-start | bytes 2359304 | tf_op jit(solution)/shard_map/ppermute | solution.py:130
  25.5 14.2 %collective-permute-start.5 = (bf16[320,128]{1,0:T(8,128)(2,1)S(1)}, bf16[320,128]{1,0:T(8,128)(2,1)S(1)}, u32[]{:S(2)}, u32[]{:S(2)}) collective-permute-start(bf16[320,128]{1,0:T(8,128)(2,1)S(1)} %get-tuple-element.208), channel_id=1, source_target_pairs={{0,8},{2,10},{4,12},{6,14},{8,0},{10,2},{12,4},{14,6},{16,24},{18,... | collective-permute-start | bytes 245768 | tf_op jit(solution)/shard_map/ppermute | solution.py:111
  26.9 15.6 %collective-permute-start.6 = (bf16[320,128]{1,0:T(8,128)(2,1)S(1)}, bf16[320,128]{1,0:T(8,128)(2,1)S(1)}, u32[]{:S(2)}, u32[]{:S(2)}) collective-permute-start(bf16[320,128]{1,0:T(8,128)(2,1)S(1)} %get-tuple-element.209), channel_id=1, source_target_pairs={{0,10},{2,8},{4,14},{6,12},{8,2},{10,0},{12,6},{14,4},{16,26},{18,... | collective-permute-start | bytes 245768 | tf_op jit(solution)/shard_map/ppermute | solution.py:111
  28.5 14.6 %collective-permute-start.4 = (bf16[320,128]{1,0:T(8,128)(2,1)S(1)}, bf16[320,128]{1,0:T(8,128)(2,1)S(1)}, u32[]{:S(2)}, u32[]{:S(2)}) collective-permute-start(bf16[320,128]{1,0:T(8,128)(2,1)S(1)} %get-tuple-element.207), channel_id=1, source_target_pairs={{0,2},{2,0},{4,6},{6,4},{8,10},{10,8},{12,14},{14,12},{16,18},{18,... | collective-permute-start | bytes 245768 | tf_op jit(solution)/shard_map/ppermute | solution.py:111
  39.6 9.9 %collective-permute-start.3 = (bf16[1,96,896]{2,1,0:T(8,128)(2,1)S(1)}, bf16[1,96,896]{2,1,0:T(8,128)(2,1)S(1)}, u32[]{:S(2)}, u32[]{:S(2)}) collective-permute-start(bf16[1,96,896]{2,1,0:T(8,128)(2,1)S(1)} %maximum_bitcast_fusion.1), channel_id=1, source_target_pairs={{0,16},{2,18},{4,20},{6,22},{8,24},{10,26},{12,28},{14,30},{16,0},... | collective-permute-start | bytes 516104 | tf_op jit(solution)/shard_map/ppermute | solution.py:111
  50.5 22.7 %collective-permute-start.7 = (bf16[4,96,1280]{2,1,0:T(8,128)(2,1)S(1)}, bf16[4,96,1280]{2,1,0:T(8,128)(2,1)S(1)}, u32[]{:S(2)}, u32[]{:S(2)}) collective-permute-start(bf16[4,96,1280]{2,1,0:T(8,128)(2,1)S(1)} %pad_maximum_fusion.8), channel_id=1, source_target_pairs={{0,4},{2,6},{4,0},{6,2},{8,12},{10,14},{12,8},{14,10},{16,20},{18,... | collective-permute-start | bytes 2949128 | tf_op jit(solution)/shard_map/ppermute | solution.py:111
  52.0 14.9 %collective-permute-start.16 = (bf16[4,3,96,128]{3,2,1,0:T(8,128)(2,1)S(1)}, bf16[4,3,96,128]{3,2,1,0:T(8,128)(2,1)S(1)}, u32[]{:S(2)}, u32[]{:S(2)}) collective-permute-start(bf16[4,3,96,128]{3,2,1,0:T(8,128)(2,1)S(1)} %get-tuple-element.70), channel_id=1, source_target_pairs={{0,16},{2,18},{4,20},{6,22},{8,24},{10,26},{12,28},{14,30},{16,0},... | collective-permute-start | bytes 884744 | tf_op jit(solution)/shard_map/ppermute | solution.py:111
  73.2 590.9 %reduce-scatter.2.cloned.1.call-start = ((), (), s32[]{:S(2)}) async-start(), calls=%async_computation.1 | async-start | bytes 21233664 | tf_op jit(solution)/shard_map/reduce_scatter | solution.py:914
  73.3 8.6 %collective-permute-start.8 = (bf16[2,96,896]{2,1,0:T(8,128)(2,1)S(1)}, bf16[2,96,896]{2,1,0:T(8,128)(2,1)S(1)}, u32[]{:S(2)}, u32[]{:S(2)}) collective-permute-start(bf16[2,96,896]{2,1,0:T(8,128)(2,1)S(1)} %pad_maximum_fusion.16), channel_id=1, source_target_pairs={{0,8},{2,10},{4,12},{6,14},{8,0},{10,2},{12,4},{14,6},{16,24},{18,... | collective-permute-start | bytes 1032200 | tf_op jit(solution)/shard_map/ppermute | solution.py:111
  82.0 42.9 %collective-permute-start.9 = (bf16[8,96,1280]{2,1,0:T(8,128)(2,1)S(1)}, bf16[8,96,1280]{2,1,0:T(8,128)(2,1)S(1)}, u32[]{:S(2)}, u32[]{:S(2)}) collective-permute-start(bf16[8,96,1280]{2,1,0:T(8,128)(2,1)S(1)} %pad_maximum_fusion.4.near), channel_id=1, source_target_pairs={{0,2},{2,0},{4,6},{6,4},{8,10},{10,8},{12,14},{14,12},{16,18},{18,... | collective-permute-start | bytes 5898248 | tf_op jit(solution)/shard_map/ppermute | solution.py:111
  83.6 29.5 %collective-permute-start.10 = (bf16[4,96,896]{2,1,0:T(8,128)(2,1)S(1)}, bf16[4,96,896]{2,1,0:T(8,128)(2,1)S(1)}, u32[]{:S(2)}, u32[]{:S(2)}) collective-permute-start(bf16[4,96,896]{2,1,0:T(8,128)(2,1)S(1)} %pad_maximum_fusion.10), channel_id=1, source_target_pairs={{0,4},{2,6},{4,0},{6,2},{8,12},{10,14},{12,8},{14,10},{16,20},{18,... | collective-permute-start | bytes 2064392 | tf_op jit(solution)/shard_map/ppermute | solution.py:111
  124.8 29.1 %collective-permute-start.11 = (bf16[8,96,896]{2,1,0:T(8,128)(2,1)S(1)}, bf16[8,96,896]{2,1,0:T(8,128)(2,1)}, u32[]{:S(2)}, u32[]{:S(2)}) collective-permute-start(bf16[8,96,896]{2,1,0:T(8,128)(2,1)S(1)} %pad_maximum_fusion.5.near), channel_id=1, source_target_pairs={{0,2},{2,0},{4,6},{6,4},{8,10},{10,8},{12,14},{14,12},{16,18},{18,... | collective-permute-start | bytes 4128776 | tf_op jit(solution)/shard_map/ppermute | solution.py:111
  165.1 31.1 %collective-permute-start.13 = (bf16[256,1536]{1,0:T(8,128)(2,1)S(1)}, bf16[256,1536]{1,0:T(8,128)(2,1)S(1)}, u32[]{:S(2)}, u32[]{:S(2)}) collective-permute-start(bf16[256,1536]{1,0:T(8,128)(2,1)S(1)} %multiply_convert_fusion), channel_id=1, source_target_pairs={{0,2},{2,0},{4,6},{6,4},{8,10},{10,8},{12,14},{14,12},{16,18},{18,... | collective-permute-start | bytes 2359304 | tf_op jit(solution)/shard_map/ppermute | solution.py:111
  167.5 28.6 %collective-permute-start.17 = (bf16[2,4,3,96,128]{4,3,2,1,0:T(8,128)(2,1)}, bf16[2,4,3,96,128]{4,3,2,1,0:T(8,128)(2,1)S(1)}, u32[]{:S(2)}, u32[]{:S(2)}) collective-permute-start(bf16[2,4,3,96,128]{4,3,2,1,0:T(8,128)(2,1)} %pad_maximum_fusion.13), channel_id=1, source_target_pairs={{0,4},{2,6},{4,0},{6,2},{8,12},{10,14},{12,8},{14,10},{16,20},{18,... | collective-permute-start | bytes 1769480 | tf_op jit(solution)/shard_map/ppermute | solution.py:111
  169.1 37.0 %collective-permute-start.14 = (bf16[256,1536]{1,0:T(8,128)(2,1)S(1)}, bf16[256,1536]{1,0:T(8,128)(2,1)}, u32[]{:S(2)}, u32[]{:S(2)}) collective-permute-start(bf16[256,1536]{1,0:T(8,128)(2,1)S(1)} %multiply_convert_fusion), channel_id=1, source_target_pairs={{0,8},{2,10},{4,12},{6,14},{8,0},{10,2},{12,4},{14,6},{16,24},{18,... | collective-permute-start | bytes 2359304 | tf_op jit(solution)/shard_map/ppermute | solution.py:111
  171.3 84.8 %collective-permute-start.15 = (bf16[256,1536]{1,0:T(8,128)(2,1)S(1)}, bf16[256,1536]{1,0:T(8,128)(2,1)}, u32[]{:S(2)}, u32[]{:S(2)}) collective-permute-start(bf16[256,1536]{1,0:T(8,128)(2,1)S(1)} %multiply_convert_fusion), channel_id=1, source_target_pairs={{0,10},{2,8},{4,14},{6,12},{8,2},{10,0},{12,6},{14,4},{16,26},{18,... | collective-permute-start | bytes 2359304 | tf_op jit(solution)/shard_map/ppermute | solution.py:111
  200.0 61.2 %collective-permute-start.18 = (bf16[3,1536,128]{1,2,0:T(8,128)(2,1)}, bf16[3,1536,128]{1,2,0:T(8,128)(2,1)}, u32[]{:S(2)}, u32[]{:S(2)}) collective-permute-start(bf16[3,1536,128]{1,2,0:T(8,128)(2,1)} %copy.128), channel_id=1, source_target_pairs={{0,1},{1,0},{2,3},{3,2},{4,5},{5,4},{6,7},{7,6},{8,9},{9,8},{10,11... | collective-permute-start | bytes 3538952 | tf_op jit(solution)/shard_map/ppermute | solution.py:130
  297.0 19.6 %collective-permute-start.19 = (bf16[256,1536]{1,0:T(8,128)(2,1)S(1)}, bf16[256,1536]{1,0:T(8,128)(2,1)S(1)}, u32[]{:S(2)}, u32[]{:S(2)}) collective-permute-start(bf16[256,1536]{1,0:T(8,128)(2,1)S(1)} %get-tuple-element.184), channel_id=1, source_target_pairs={{0,2},{2,0},{4,6},{6,4},{8,10},{10,8},{12,14},{14,12},{16,18},{18,... | collective-permute-start | bytes 2359304 | tf_op jit(solution)/shard_map/ppermute | solution.py:111
  297.7 20.5 %collective-permute-start.20 = (bf16[256,1536]{1,0:T(8,128)(2,1)S(1)}, bf16[256,1536]{1,0:T(8,128)(2,1)S(1)}, u32[]{:S(2)}, u32[]{:S(2)}) collective-permute-start(bf16[256,1536]{1,0:T(8,128)(2,1)S(1)} %get-tuple-element.186), channel_id=1, source_target_pairs={{0,8},{2,10},{4,12},{6,14},{8,0},{10,2},{12,4},{14,6},{16,24},{18,... | collective-permute-start | bytes 2359304 | tf_op jit(solution)/shard_map/ppermute | solution.py:111
  297.7 36.4 %collective-permute-start.21 = (bf16[256,1536]{1,0:T(8,128)(2,1)S(1)}, bf16[256,1536]{1,0:T(8,128)(2,1)S(1)}, u32[]{:S(2)}, u32[]{:S(2)}) collective-permute-start(bf16[256,1536]{1,0:T(8,128)(2,1)S(1)} %get-tuple-element.185), channel_id=1, source_target_pairs={{0,10},{2,8},{4,14},{6,12},{8,2},{10,0},{12,6},{14,4},{16,26},{18,... | collective-permute-start | bytes 2359304 | tf_op jit(solution)/shard_map/ppermute | solution.py:111
  337.0 19.6 %collective-permute-start.22 = (bf16[256,1536]{1,0:T(8,128)(2,1)S(1)}, bf16[256,1536]{1,0:T(8,128)(2,1)S(1)}, u32[]{:S(2)}, u32[]{:S(2)}) collective-permute-start(bf16[256,1536]{1,0:T(8,128)(2,1)S(1)} %fusion.86), channel_id=1, source_target_pairs={{0,2},{2,0},{4,6},{6,4},{8,10},{10,8},{12,14},{14,12},{16,18},{18,... | collective-permute-start | bytes 2359304 | tf_op jit(solution)/shard_map/ppermute | solution.py:111
  337.4 20.5 %collective-permute-start.23 = (bf16[256,1536]{1,0:T(8,128)(2,1)S(1)}, bf16[256,1536]{1,0:T(8,128)(2,1)S(1)}, u32[]{:S(2)}, u32[]{:S(2)}) collective-permute-start(bf16[256,1536]{1,0:T(8,128)(2,1)S(1)} %fusion.86), channel_id=1, source_target_pairs={{0,8},{2,10},{4,12},{6,14},{8,0},{10,2},{12,4},{14,6},{16,24},{18,... | collective-permute-start | bytes 2359304 | tf_op jit(solution)/shard_map/ppermute | solution.py:111
  337.7 35.2 %collective-permute-start.24 = (bf16[256,1536]{1,0:T(8,128)(2,1)S(1)}, bf16[256,1536]{1,0:T(8,128)(2,1)S(1)}, u32[]{:S(2)}, u32[]{:S(2)}) collective-permute-start(bf16[256,1536]{1,0:T(8,128)(2,1)S(1)} %fusion.86), channel_id=1, source_target_pairs={{0,10},{2,8},{4,14},{6,12},{8,2},{10,0},{12,6},{14,4},{16,26},{18,... | collective-permute-start | bytes 2359304 | tf_op jit(solution)/shard_map/ppermute | solution.py:111
  431.1 22.5 %collective-permute-start.27 = (bf16[272,1536]{1,0:T(8,128)(2,1)S(1)}, bf16[272,1536]{1,0:T(8,128)(2,1)S(1)}, u32[]{:S(2)}, u32[]{:S(2)}) collective-permute-start(bf16[272,1536]{1,0:T(8,128)(2,1)S(1)} %get-tuple-element.179), channel_id=1, source_target_pairs={{0,10},{2,8},{4,14},{6,12},{8,2},{10,0},{12,6},{14,4},{16,26},{18,... | collective-permute-start | bytes 2506760 | tf_op jit(solution)/shard_map/ppermute | solution.py:111
  431.5 35.0 %collective-permute-start.26 = (bf16[272,1536]{1,0:T(8,128)(2,1)S(1)}, bf16[272,1536]{1,0:T(8,128)(2,1)S(1)}, u32[]{:S(2)}, u32[]{:S(2)}) collective-permute-start(bf16[272,1536]{1,0:T(8,128)(2,1)S(1)} %get-tuple-element.180), channel_id=1, source_target_pairs={{0,8},{2,10},{4,12},{6,14},{8,0},{10,2},{12,4},{14,6},{16,24},{18,... | collective-permute-start | bytes 2506760 | tf_op jit(solution)/shard_map/ppermute | solution.py:111
  432.9 34.6 %collective-permute-start.25 = (bf16[272,1536]{1,0:T(8,128)(2,1)S(1)}, bf16[272,1536]{1,0:T(8,128)(2,1)S(1)}, u32[]{:S(2)}, u32[]{:S(2)}) collective-permute-start(bf16[272,1536]{1,0:T(8,128)(2,1)S(1)} %get-tuple-element.181), channel_id=1, source_target_pairs={{0,2},{2,0},{4,6},{6,4},{8,10},{10,8},{12,14},{14,12},{16,18},{18,... | collective-permute-start | bytes 2506760 | tf_op jit(solution)/shard_map/ppermute | solution.py:111
  468.0 8.6 %collective-permute-start.29 = (bf16[1536,16]{0,1:T(8,128)(2,1)S(1)}, bf16[1536,16]{0,1:T(8,128)(2,1)S(1)}, u32[]{:S(2)}, u32[]{:S(2)}) collective-permute-start(bf16[1536,16]{0,1:T(8,128)(2,1)S(1)} %get-tuple-element.219), channel_id=1, source_target_pairs={{0,1},{1,0},{2,3},{3,2},{4,5},{5,4},{6,7},{7,6},{8,9},{9,8},{10,11... | collective-permute-start | bytes 147464 | tf_op jit(solution)/shard_map/ppermute | solution.py:130
  472.7 7.3 %collective-permute-start.28 = (bf16[256,1536]{1,0:T(8,128)(2,1)}, bf16[256,1536]{1,0:T(8,128)(2,1)}, u32[]{:S(2)}, u32[]{:S(2)}) collective-permute-start(bf16[256,1536]{1,0:T(8,128)(2,1)} %get-tuple-element.174.own), channel_id=1, source_target_pairs={{0,1},{1,0},{2,3},{3,2},{4,5},{5,4},{6,7},{7,6},{8,9},{9,8},{10,11... | collective-permute-start | bytes 2359304 | tf_op jit(solution)/shard_map/ppermute | solution.py:130
  487.9 32.9 %collective-permute-start.31 = (bf16[8,96,896]{2,1,0:T(8,128)(2,1)}, bf16[8,96,896]{2,1,0:T(8,128)(2,1)}, u32[]{:S(2)}, u32[]{:S(2)}) collective-permute-start(bf16[8,96,896]{2,1,0:T(8,128)(2,1)} %get-tuple-element.86), channel_id=1, source_target_pairs={{0,2},{2,0},{4,6},{6,4},{8,10},{10,8},{12,14},{14,12},{16,18},{18,... | collective-permute-start | bytes 4128776 | tf_op jit(solution)/shard_map/ppermute | solution.py:111
  489.8 31.7 %collective-permute-start.44 = (bf16[3,1536,128]{1,2,0:T(8,128)(2,1)}, bf16[3,1536,128]{1,2,0:T(8,128)(2,1)}, u32[]{:S(2)}, u32[]{:S(2)}) collective-permute-start(bf16[3,1536,128]{1,2,0:T(8,128)(2,1)} %fusion.6), channel_id=1, source_target_pairs={{0,1},{1,0},{2,3},{3,2},{4,5},{5,4},{6,7},{7,6},{8,9},{9,8},{10,11... | collective-permute-start | bytes 3538952 | tf_op jit(solution)/shard_map/ppermute | solution.py:130
  513.1 14.6 %collective-permute-start.30 = (bf16[256,1536]{1,0:T(8,128)(2,1)}, bf16[256,1536]{1,0:T(8,128)(2,1)}, u32[]{:S(2)}, u32[]{:S(2)}) collective-permute-start(bf16[256,1536]{1,0:T(8,128)(2,1)} %get-tuple-element.84), channel_id=1, source_target_pairs={{0,1},{1,0},{2,3},{3,2},{4,5},{5,4},{6,7},{7,6},{8,9},{9,8},{10,11... | collective-permute-start | bytes 2359304 | tf_op jit(solution)/shard_map/ppermute | solution.py:130
  520.8 44.7 %collective-permute-start.32 = (bf16[8,96,1280]{2,1,0:T(8,128)(2,1)}, bf16[8,96,1280]{2,1,0:T(8,128)(2,1)}, u32[]{:S(2)}, u32[]{:S(2)}) collective-permute-start(bf16[8,96,1280]{2,1,0:T(8,128)(2,1)} %get-tuple-element.88), channel_id=1, source_target_pairs={{0,2},{2,0},{4,6},{6,4},{8,10},{10,8},{12,14},{14,12},{16,18},{18,... | collective-permute-start | bytes 5898248 | tf_op jit(solution)/shard_map/ppermute | solution.py:111
  526.9 50.3 %collective-permute-start.45 = (bf16[2,4,3,96,128]{4,3,2,1,0:T(8,128)(2,1)S(1)}, bf16[2,4,3,96,128]{4,3,2,1,0:T(8,128)(2,1)S(1)}, u32[]{:S(2)}, u32[]{:S(2)}) collective-permute-start(bf16[2,4,3,96,128]{4,3,2,1,0:T(8,128)(2,1)S(1)} %pad_maximum_fusion.14), channel_id=1, source_target_pairs={{0,4},{2,6},{4,0},{6,2},{8,12},{10,14},{12,8},{14,10},{16,20},{18,... | collective-permute-start | bytes 1769480 | tf_op jit(solution)/shard_map/ppermute | solution.py:111
  535.2 41.8 %collective-permute-start.41 = (bf16[4,96,896]{2,1,0:T(8,128)(2,1)S(1)}, bf16[4,96,896]{2,1,0:T(8,128)(2,1)S(1)}, u32[]{:S(2)}, u32[]{:S(2)}) collective-permute-start(bf16[4,96,896]{2,1,0:T(8,128)(2,1)S(1)} %slice.478), channel_id=1, source_target_pairs={{0,4},{2,6},{4,0},{6,2},{8,12},{10,14},{12,8},{14,10},{16,20},{18,... | collective-permute-start | bytes 2064392 | tf_op jit(solution)/shard_map/ppermute | solution.py:111
  567.6 44.8 %collective-permute-start.34 = (bf16[4,96,1280]{2,1,0:T(8,128)(2,1)S(1)}, bf16[4,96,1280]{2,1,0:T(8,128)(2,1)S(1)}, u32[]{:S(2)}, u32[]{:S(2)}) collective-permute-start(bf16[4,96,1280]{2,1,0:T(8,128)(2,1)S(1)} %slice.477), channel_id=1, source_target_pairs={{0,4},{2,6},{4,0},{6,2},{8,12},{10,14},{12,8},{14,10},{16,20},{18,... | collective-permute-start | bytes 2949128 | tf_op jit(solution)/shard_map/ppermute | solution.py:111
  577.1 39.1 %collective-permute-start.42 = (bf16[2,96,896]{2,1,0:T(8,128)(2,1)S(1)}, bf16[2,96,896]{2,1,0:T(8,128)(2,1)S(1)}, u32[]{:S(2)}, u32[]{:S(2)}) collective-permute-start(bf16[2,96,896]{2,1,0:T(8,128)(2,1)S(1)} %slice.480), channel_id=1, source_target_pairs={{0,8},{2,10},{4,12},{6,14},{8,0},{10,2},{12,4},{14,6},{16,24},{18,... | collective-permute-start | bytes 1032200 | tf_op jit(solution)/shard_map/ppermute | solution.py:111
  578.7 37.4 %collective-permute-start.46 = (bf16[4,3,96,128]{3,2,1,0:T(8,128)(2,1)S(1)}, bf16[4,3,96,128]{3,2,1,0:T(8,128)(2,1)S(1)}, u32[]{:S(2)}, u32[]{:S(2)}) collective-permute-start(bf16[4,3,96,128]{3,2,1,0:T(8,128)(2,1)S(1)} %fusion.50), channel_id=1, source_target_pairs={{0,16},{2,18},{4,20},{6,22},{8,24},{10,26},{12,28},{14,30},{16,0},... | collective-permute-start | bytes 884744 | tf_op jit(solution)/shard_map/ppermute | solution.py:111
  612.7 13.5 %collective-permute-start.36 = (bf16[2,96,1280]{2,1,0:T(8,128)(2,1)S(1)}, bf16[2,96,1280]{2,1,0:T(8,128)(2,1)S(1)}, u32[]{:S(2)}, u32[]{:S(2)}) collective-permute-start(bf16[2,96,1280]{2,1,0:T(8,128)(2,1)S(1)} %slice.479), channel_id=1, source_target_pairs={{0,8},{2,10},{4,12},{6,14},{8,0},{10,2},{12,4},{14,6},{16,24},{18,... | collective-permute-start | bytes 1474568 | tf_op jit(solution)/shard_map/ppermute | solution.py:111
  616.4 19.4 %collective-permute-start.43 = (bf16[1,96,896]{2,1,0:T(8,128)(2,1)S(1)}, bf16[1,96,896]{2,1,0:T(8,128)(2,1)S(1)}, u32[]{:S(2)}, u32[]{:S(2)}) collective-permute-start(bf16[1,96,896]{2,1,0:T(8,128)(2,1)S(1)} %slice.482), channel_id=1, source_target_pairs={{0,16},{2,18},{4,20},{6,22},{8,24},{10,26},{12,28},{14,30},{16,0},... | collective-permute-start | bytes 516104 | tf_op jit(solution)/shard_map/ppermute | solution.py:111
  626.3 13.6 %collective-permute-start.47 = (bf16[3,96,128]{2,1,0:T(8,128)(2,1)S(1)}, bf16[3,96,128]{2,1,0:T(8,128)(2,1)S(1)}, u32[]{:S(2)}, u32[]{:S(2)}) collective-permute-start(bf16[3,96,128]{2,1,0:T(8,128)(2,1)S(1)} %get-tuple-element.197), channel_id=1, source_target_pairs={{0,2},{2,0},{4,6},{6,4},{8,10},{10,8},{12,14},{14,12},{16,18},{18,... | collective-permute-start | bytes 221192 | tf_op jit(solution)/shard_map/ppermute | solution.py:111
  635.8 4.1 collective-permute-start.37
  636.8 5.3 collective-permute-start.48
  638.8 8.4 %collective-permute-start.49 = (bf16[3,96,128]{2,1,0:T(8,128)(2,1)S(1)}, bf16[3,96,128]{2,1,0:T(8,128)(2,1)S(1)}, u32[]{:S(2)}, u32[]{:S(2)}) collective-permute-start(bf16[3,96,128]{2,1,0:T(8,128)(2,1)S(1)} %get-tuple-element.195), channel_id=1, source_target_pairs={{0,10},{2,8},{4,14},{6,12},{8,2},{10,0},{12,6},{14,4},{16,26},{18,... | collective-permute-start | bytes 221192 | tf_op jit(solution)/shard_map/ppermute | solution.py:111
  639.6 16.4 %collective-permute-start.38 = (bf16[1,96,1280]{2,1,0:T(8,128)(2,1)S(1)}, bf16[1,96,1280]{2,1,0:T(8,128)(2,1)S(1)}, u32[]{:S(2)}, u32[]{:S(2)}) collective-permute-start(bf16[1,96,1280]{2,1,0:T(8,128)(2,1)S(1)} %slice.481), channel_id=1, source_target_pairs={{0,16},{2,18},{4,20},{6,22},{8,24},{10,26},{12,28},{14,30},{16,0},... | collective-permute-start | bytes 737288 | tf_op jit(solution)/shard_map/ppermute | solution.py:111
  656.0 4.8 collective-permute-start.39
  (56 other events, 648.5 us)
Sparse Core Ops, SparseCore 0:
  73.4 177.2 all-gather.2
  428.2 233.7 reduce-scatter.1
